TPU v7x, 512 devices: a whole 4x8x8 slice. The times are simulated.
512 devices in a mesh: mode: 16 (over x, z_lo), space: 32 (over y, z_hi, core).
Axes of the slice: x: 4, y: 8, z: 8 (z_hi: 2, z_lo: 4; z = z_hi * 4 + z_lo), core: 2. Of those that a mesh axis runs over, the one named last changes fastest.
Arguments:
- modes: bfloat16 [64, 64, 64, 128], P('mode', 'space'), may hold values from -1.25 to 1.25
- regions: int32 [64, 64, 128], P('space'), may hold values from 0 to 7
- stiffness: float32 [8], replicated, may hold values from 0.05 to 4
- nonlinear: float32 [8], replicated, may hold values from 0.5 to 2
- plan: int32 [64, 3], P('mode'), may hold values from 0 to 3
Outputs:
- derivatives: float32 [64, 3, 64, 64, 128], P('mode', None, 'space')
All inputs are finite; a program needn't handle non-finite values.
Results may differ from a plain program's by a relative error of at most 0.0003.
Values may be sent and summed in bfloat16 or wider, within the bound.
No kernel may reach another device: no remote copies, remote signals or barrier semaphores. Data moves between devices by JAX's collectives and lax.ppermute only.
A program may use at most 64 MiB of HBM per device.

v0:
```python
import jax
import jax.numpy as jnp
from jax import lax
from jax.experimental import pallas as pl
from jax.experimental.pallas import tpu as pltpu
from jax.sharding import PartitionSpec as P

PARTNERS = 3
MASS = 0.5
WINDOW = 11
MOMENTS = 6
GROUP = 2
PAD = 8


f32 = jnp.float32


def clear_rims(ref, lead):
    ny = ref.shape[-2] - 2 * PAD
    zero = jnp.zeros((PAD, ref.shape[-1]), f32)
    for i in range(ref.shape[-3]):
        ref[lead + (i, pl.ds(0, PAD))] = zero
        ref[lead + (i, pl.ds(PAD + ny, PAD))] = zero


def fill_window(wide, mine, other, edge, edge_at):
    stacks, ny = mine.shape[0], mine.shape[2]
    space = lax.axis_index("space")
    core = space % 2
    high = (space // 2) % 2
    origin = 4 * high + 2 * core

    def clear(m, carry):
        clear_rims(wide, (m,))
        return carry

    lax.fori_loop(0, stacks, clear, 0)

    def place(ref, slot, at, first):
        spot = at - origin

        @pl.when(jnp.logical_and(spot >= 0, spot < WINDOW))
        def _():
            for m in range(stacks):
                wide[m, spot, pl.ds(PAD, ny)] = ref[first + m, slot].astype(f32)

    for ref, q in ((mine, core), (other, 1 - core)):
        for i in range(2):
            place(ref, i, 5 + 4 * high + 2 * q + i, 0)
            place(ref, 2 + i, 5 + 4 * (1 - high) + 2 * q + i, 0)
            place(ref, 4 + i, 1 + 12 * high + 2 * q + i, 0)
    place(edge, 0, 4 * high, edge_at)


def laplace_at(ref, lead, i, r, lane):
    nz = ref.shape[-1]
    at = PAD + r
    x = ref[lead + (i, pl.ds(at, 8))]
    left = jnp.where(lane == 0, 0.0, pltpu.roll(x, 1, 1))
    right = jnp.where(lane == nz - 1, 0.0, pltpu.roll(x, nz - 1, 1))
    rows = ref[lead + (i, pl.ds(at - 1, 8))] + ref[lead + (i, pl.ds(at + 1, 8))]
    slabs = ref[lead + (i - 1, pl.ds(at, 8))] + ref[lead + (i + 1, pl.ds(at, 8))]
    return 6.0 * x - ((rows + slabs) + (left + right))


def material(wide, label_at, stiff, cubic, gain, dinv, diag, faces):
    ny, nz = gain.shape[-2:]
    row = lax.broadcasted_iota(jnp.int32, (ny, nz), 0)
    lane = lax.broadcasted_iota(jnp.int32, (ny, nz), 1)
    body = pl.ds(PAD, ny)
    for i in range(1, 10):
        label = wide[label_at, i, body]
        c = jnp.zeros((ny, nz), f32)
        g = jnp.zeros((ny, nz), f32)
        for r in range(stiff.shape[0]):
            hit = label == float(r + 1)
            c = jnp.where(hit, stiff[r], c)
            g = jnp.where(hit, cubic[r], g)
        wide[label_at, i, body] = c
        gain[i - 1] = g
    for i in range(2, 9):
        c = wide[label_at, i, body]
        beside = (
            wide[label_at, i - 1, body],
            wide[label_at, i + 1, body],
            wide[label_at, i, pl.ds(PAD - 1, ny)],
            wide[label_at, i, pl.ds(PAD + 1, ny)],
            jnp.where(lane == 0, 0.0, pltpu.roll(c, 1, 1)),
            jnp.where(lane == nz - 1, 0.0, pltpu.roll(c, nz - 1, 1)),
        )
        ws = [0.5 * (c + n) for n in beside]
        d = MASS + ws[0] + ws[1] + ws[2] + ws[3] + ws[4] + ws[5]
        inv = jnp.where(gain[i - 1] > 0.0, 1.0 / d, 0.0)
        dinv[i - 2] = inv
        if 5 <= i <= 6:
            diag[i - 5] = d
        if 3 <= i <= 7:
            for k in range(4):
                faces[k, i - 3] = ws[k] * inv
            faces[4, i - 3] = jnp.where(lane > 0, ws[4] * inv, 0.0)
            faces[5, i - 3] = jnp.where(lane < nz - 1, ws[5] * inv, 0.0)


def krylov(group, lap_own, lap_of, j_of, shared, outs, scratch, total):
    dinv, diag, faces = shared
    first, second, third = outs
    prod, v0, v1, v2 = scratch
    ny, nz = diag.shape[-2:]
    lane = lax.broadcasted_iota(jnp.int32, (8, nz), 1)
    mrow = lax.broadcasted_iota(jnp.int32, (8, nz), 0)
    rows = range(0, ny, 8)

    for t, (a, _, _) in enumerate(group):
        for i in range(1, 10):
            for r in rows:
                at = pl.ds(r, 8)
                prod[t, i, pl.ds(PAD + r, 8)] = lap_own[a, i - 1, at] * lap_of[j_of[t], i - 1, at]
    for i in range(2, 9):
        for r in rows:
            scale = -dinv[i - 2, pl.ds(r, 8)]
            for t in range(len(group)):
                v0[t, i, pl.ds(PAD + r, 8)] = laplace_at(prod, (t,), i, r, lane) * scale

    def image(ref, t, i, r, w, twice):
        at = PAD + r
        x = ref[t, i, pl.ds(at, 8)]
        out = w[2] * ref[t, i, pl.ds(at - 1, 8)] + w[3] * ref[t, i, pl.ds(at + 1, 8)]
        out = out + (w[4] * pltpu.roll(x, 1, 1) + w[5] * pltpu.roll(x, nz - 1, 1))
        lower = w[0] * ref[t, i - 1, pl.ds(at, 8)]
        if twice:
            return out + 2.0 * lower, x
        return out + (lower + w[1] * ref[t, i + 1, pl.ds(at, 8)]), x

    for src, dst, low, top in ((v0, v1, 3, 8), (v1, v2, 4, 7)):
        for i in range(low, top):
            for r in rows:
                w = [faces[k, i - 3, pl.ds(r, 8)] for k in range(6)]
                for t in range(len(group)):
                    dst[t, i, pl.ds(PAD + r, 8)] = image(src, t, i, r, w, False)[0]

    parts = [[jnp.zeros((8, nz), f32)] * MOMENTS for _ in group]
    for i in (5, 6):
        for r in rows:
            w = [faces[k, i - 3, pl.ds(r, 8)] for k in range(6)]
            d = diag[i - 5, pl.ds(r, 8)]
            for t, (_, f, _) in enumerate(group):
                ring, x2 = image(v2, t, i, r, w, True)
                x0, x1 = v0[t, i, pl.ds(PAD + r, 8)], v1[t, i, pl.ds(PAD + r, 8)]
                first[f, i - 5, pl.ds(r, 8)] = x0
                second[f, i - 5, pl.ds(r, 8)] = x1
                third[f, i - 5, pl.ds(r, 8)] = x2
                d0, d1, d2 = d * x0, d * x1, d * x2
                pairs = (d0 * x0, d1 * x0, d1 * x1, d2 * x1, d2 * x2, d2 * ring)
                parts[t] = [p + q for p, q in zip(parts[t], pairs)]
    for t, (_, _, column) in enumerate(group):
        col = jnp.zeros((8, nz), f32)
        for k in range(MOMENTS):
            col = jnp.where(mrow == k, jnp.sum(parts[t][k], axis=0, keepdims=True), col)
        total = jnp.where(lane == column, jnp.sum(col, axis=1, keepdims=True), total)
    return total


def laps(wide, lap, count):
    ny, nz = lap.shape[-2:]
    lane = lax.broadcasted_iota(jnp.int32, (8, nz), 1)

    def one(m, carry):
        for i in range(1, 10):
            for r in range(0, ny, 8):
                lap[m, i - 1, pl.ds(r, 8)] = laplace_at(wide, (m,), i, r, lane)
        return carry

    lax.fori_loop(0, count, one, 0)


def clear_fields(scratch):
    for ref in scratch:
        for t in range(ref.shape[0]):
            clear_rims(ref, (t,))


def own_kernel(plan, stiff, cubic, mine, other, edge,
               first, second, third, lap_own, dinv, diag, faces, moments,
               wide, gain, lap, prod, v0, v1, v2):
    blocks, nz = lap.shape[0], lap.shape[-1]
    scratch = (prod, v0, v1, v2)
    clear_fields(scratch)
    fill_window(wide, mine, other, edge, 0)
    material(wide, blocks, stiff, cubic, gain, dinv, diag, faces)
    laps(wide, lap, blocks)

    def scaled(m, carry):
        for i in range(9):
            lap_own[m, i] = gain[i] * lap[m, i]
        return carry

    lax.fori_loop(0, blocks, scaled, 0)

    def step(h, total):
        group = [(h * GROUP + t, h * GROUP + t, (h * GROUP + t) * PARTNERS) for t in range(GROUP)]
        j_of = [plan[g[0], 0] for g in group]
        return krylov(group, lap_own, lap, j_of, (dinv, diag, faces), (first, second, third), scratch, total)

    moments[...] = lax.fori_loop(0, blocks // GROUP, step, jnp.zeros((8, nz), f32))


def partner_kernel(plan, mine, other, edge, lap_own, dinv, diag, faces, moments,
                   first, second, third, sums,
                   wide, lap, prod, v0, v1, v2):
    blocks = lap_own.shape[0]
    scratch = (prod, v0, v1, v2)
    clear_fields(scratch)
    fill_window(wide, mine, other, edge, blocks + 1)
    laps(wide, lap, lap.shape[0])
    per = blocks // GROUP

    def step(h, total):
        s = 1 + h // per
        b = (h - (s - 1) * per) * GROUP
        group = [(b + t, (s - 1) * blocks + b + t, (b + t) * PARTNERS + s) for t in range(GROUP)]
        j_of = [(s - 1) * blocks + plan[g[0], s] for g in group]
        return krylov(group, lap_own, lap, j_of, (dinv, diag, faces), (first, second, third), scratch, total)

    total = lax.fori_loop(0, (PARTNERS - 1) * per, step, moments[...])
    for d in range(sums.shape[0]):
        sums[d] = total


def combine_kernel(sums, a0, a1, a2, b0, b1, b2, out):
    m = jnp.sum(sums[...], axis=0)
    mu = [m[k : k + 1] for k in range(MOMENTS)]
    ka = [mu[k] - mu[k + 1] for k in range(MOMENTS - 1)]

    def square(c, form):
        total = None
        for i in range(len(c)):
            for j in range(i, len(c)):
                term = c[i] * c[j] * form[i + j]
                if i != j:
                    term = 2.0 * term
                total = term if total is None else total + term
        return total

    alpha = mu[0] / ka[0]
    x = [alpha, None, None]
    z = [1.0 - alpha, alpha]
    rz = square(z, mu)
    beta = rz / mu[0]
    p = [z[0] + beta, z[1]]
    alpha = rz / square(p, ka)
    x = [x[0] + alpha * p[0], alpha * p[1]]
    z = [z[0] - alpha * p[0], z[1] - alpha * (p[1] - p[0]), alpha * p[1]]
    new = square(z, mu)
    beta = new / rz
    p = [z[0] + beta * p[0], z[1] + beta * p[1], z[2]]
    alpha = new / square(p, ka)
    x = [x[0] + alpha * p[0], x[1] + alpha * p[1], alpha * p[2]]

    lane = lax.broadcasted_iota(jnp.int32, x[0].shape, 1)

    def pick(c, f):
        return jnp.sum(jnp.where(lane == f, c, 0.0), axis=1, keepdims=True)

    blocks = a0.shape[0]
    for f in range(out.shape[0]):
        a, s = f // PARTNERS, f % PARTNERS
        basis, at = ((a0, a1, a2), a) if s == 0 else ((b0, b1, b2), (s - 1) * blocks + a)
        c0, c1, c2 = (pick(c, f) for c in x)
        for i in range(out.shape[1]):
            out[f, i] = c0 * basis[0][at, i] + c1 * basis[1][at, i] + c2 * basis[2][at, i]


def shards(modes, regions, stiffness, nonlinear, plan):
    per_block, slabs, ny, nz = modes.shape
    fields = per_block * PARTNERS
    n_mode, n_space = lax.axis_size("mode"), lax.axis_size("space")

    def send(x, to):
        pairs = []
        for m in range(n_mode):
            for s in range(n_space):
                t = to(m, s // 4, (s // 2) % 2, s % 2)
                if t is not None and 0 <= t[1] < n_space // 4:
                    tm, ty, th, tc = t
                    pairs.append((m * n_space + s, (tm % n_mode) * n_space + (ty * 2 + th) * 2 + tc))
        return lax.ppermute(x, ("mode", "space"), pairs)

    def along(m, y, h, c):
        return m, y + 1 if h == 0 else y - 1, h, c

    def partner_core(m, y, h, c):
        return m, y, h, 1 - c

    labels = (regions + 1).astype(jnp.bfloat16)[None]
    raw = jnp.concatenate([modes, labels], 0)
    far0 = send(raw, lambda m, y, h, c: (m, y, 1 - h, c))
    far1 = send(modes, lambda m, y, h, c: (m + 1, y, 1 - h, c))
    far2 = send(modes, lambda m, y, h, c: (m + 2, y, 1 - h, c))
    near1 = send(modes, lambda m, y, h, c: (m + 1, y, h, c))
    near2 = send(modes, lambda m, y, h, c: (m + 2, y, h, c))
    far12 = jnp.concatenate([far1, far2], 0)
    near12 = jnp.concatenate([near1, near2], 0)
    along0 = send(far0, along)
    near = jnp.concatenate([raw, near12], 0)[:, 1:]
    edge = send(near, lambda m, y, h, c: (m, y + 1, h, 0) if c == 1 else None)
    along12 = send(far12, along)
    mine0 = jnp.concatenate([raw, far0, along0], 1)
    mine12 = jnp.concatenate([near12, far12, along12], 1)
    other0 = send(mine0, partner_core)
    other12 = send(mine12, partner_core)

    vm = pl.BlockSpec(memory_space=pltpu.VMEM)
    sm = pl.BlockSpec(memory_space=pltpu.SMEM)
    slab, padded = (ny, nz), (ny + 2 * PAD, nz)

    def array(*shape):
        return jax.ShapeDtypeStruct(shape, f32)

    field_scratch = [pltpu.VMEM((GROUP, WINDOW) + padded, f32) for _ in range(4)]
    vectors = [array(per_block, *(slabs,), *slab)] * 3
    a0, a1, a2, lap_own, dinv, diag, faces, moments = pl.pallas_call(
        own_kernel,
        out_shape=(
            *vectors,
            array(per_block, 9, *slab),
            array(7, *slab),
            array(slabs, *slab),
            array(6, 5, *slab),
            array(8, nz),
        ),
        in_specs=[sm, sm, sm, vm, vm, vm],
        out_specs=(vm,) * 8,
        scratch_shapes=[
            pltpu.VMEM((per_block + 1, WINDOW) + padded, f32),
            pltpu.VMEM((9,) + slab, f32),
            pltpu.VMEM((per_block, 9) + slab, f32),
            *field_scratch,
        ],
        compiler_params=pltpu.CompilerParams(vmem_limit_bytes=24 << 20),
        cost_estimate=pl.CostEstimate(flops=20_000_000, bytes_accessed=8 << 20, transcendentals=0),
        name="own",
    )(plan, stiffness, nonlinear, mine0, other0, edge)

    rest = per_block * (PARTNERS - 1)
    b0, b1, b2, sums = pl.pallas_call(
        partner_kernel,
        out_shape=(*([array(rest, slabs, *slab)] * 3), array(n_space, 8, nz)),
        in_specs=[sm] + [vm] * 8,
        out_specs=(vm,) * 4,
        scratch_shapes=[
            pltpu.VMEM((rest, WINDOW) + padded, f32),
            pltpu.VMEM((rest, 9) + slab, f32),
            *field_scratch,
        ],
        compiler_params=pltpu.CompilerParams(vmem_limit_bytes=24 << 20),
        cost_estimate=pl.CostEstimate(flops=40_000_000, bytes_accessed=16 << 20, transcendentals=0),
        name="partner",
    )(plan, mine12, other12, edge, lap_own, dinv, diag, faces, moments)

    gathered = lax.all_to_all(sums, "space", 0, 0)

    out = pl.pallas_call(
        combine_kernel,
        out_shape=array(fields, slabs, *slab),
        in_specs=[vm] * 7,
        out_specs=vm,
        compiler_params=pltpu.CompilerParams(vmem_limit_bytes=16 << 20),
        name="combine",
    )(gathered, a0, a1, a2, b0, b1, b2)
    return out.reshape((per_block, PARTNERS, slabs, ny, nz))


def solution(mesh):
    return jax.shard_map(
        shards,
        mesh=mesh,
        in_specs=(
            P("mode", "space", None, None),
            P("space", None, None),
            P(),
            P(),
            P("mode", None),
        ),
        out_specs=P("mode", None, "space", None, None),
        check_vma=False,
    )
```

profile of v0, /device:TPU:1, one launch (start us, length us, event | category | flops | bytes accessed | tf_op | source)
XLA Modules:
  0.0 96.0 jit_solution(18016994887652743395)
XLA Ops:
  0.0 11.5 %collective-permute-start.2 = (bf16[4,2,64,128]{3,2,1,0:T(8,128)(2,1)}, bf16[4,2,64,128]{3,2,1,0:T(8,128)(2,1)S(1)}, u32[]{:S(2)}, u32[]{:S(2)}) collective-permute-start(bf16[4,2,64,128]{3,2,1,0:T(8,128)(2,1)} %param.5), channel_id=1, source_target_pairs={{0,34},{1,35},{2,32},{3,33},{4,38},{5,39},{6,36},{7,37},{8,42},{9,... | collective-permute-start | bytes 393224 | tf_op jit(solution)/shard_map/ppermute | solution.py:287
  11.5 1.9 %collective-permute-start.3 = (bf16[4,2,64,128]{3,2,1,0:T(8,128)(2,1)}, bf16[4,2,64,128]{3,2,1,0:T(8,128)(2,1)S(1)}, u32[]{:S(2)}, u32[]{:S(2)}) collective-permute-start(bf16[4,2,64,128]{3,2,1,0:T(8,128)(2,1)} %param.5), channel_id=1, source_target_pairs={{0,66},{1,67},{2,64},{3,65},{4,70},{5,71},{6,68},{7,69},{8,74},{9,... | collective-permute-start | bytes 393224 | tf_op jit(solution)/shard_map/ppermute | solution.py:287
  13.4 4.0 %collective-permute-start.1 = (bf16[4,2,64,128]{3,2,1,0:T(8,128)(2,1)}, bf16[4,2,64,128]{3,2,1,0:T(8,128)(2,1)S(1)}, u32[]{:S(2)}, u32[]{:S(2)}) collective-permute-start(bf16[4,2,64,128]{3,2,1,0:T(8,128)(2,1)} %param.5), channel_id=1, source_target_pairs={{0,64},{1,65},{2,66},{3,67},{4,68},{5,69},{6,70},{7,71},{8,72},{9,... | collective-permute-start | bytes 393224 | tf_op jit(solution)/shard_map/ppermute | solution.py:287
  17.4 2.2 %collective-permute-start = (bf16[4,2,64,128]{3,2,1,0:T(8,128)(2,1)}, bf16[4,2,64,128]{3,2,1,0:T(8,128)(2,1)S(1)}, u32[]{:S(2)}, u32[]{:S(2)}) collective-permute-start(bf16[4,2,64,128]{3,2,1,0:T(8,128)(2,1)} %param.5), channel_id=1, source_target_pairs={{0,32},{1,33},{2,34},{3,35},{4,36},{5,37},{6,38},{7,39},{8,40},{9,... | collective-permute-start | bytes 393224 | tf_op jit(solution)/shard_map/ppermute | solution.py:287
  19.6 0.3 collective-permute-done.2
  20.0 5.4 %collective-permute-done.3 = bf16[4,2,64,128]{3,2,1,0:T(8,128)(2,1)S(1)} collective-permute-done((bf16[4,2,64,128]{3,2,1,0:T(8,128)(2,1)}, bf16[4,2,64,128]{3,2,1,0:T(8,128)(2,1)S(1)}, u32[]{:S(2)}, u32[]{:S(2)}) %collective-permute-start.3) | collective-permute-done | bytes 131104 | tf_op jit(solution)/shard_map/ppermute | solution.py:287
  25.4 3.2 %collective-permute-start.4 = (bf16[8,2,64,128]{3,2,1,0:T(8,128)(2,1)S(1)}, bf16[8,2,64,128]{3,2,1,0:T(8,128)(2,1)S(1)}, u32[]{:S(2)}, u32[]{:S(2)}) collective-permute-start(bf16[8,2,64,128]{3,2,1,0:T(8,128)(2,1)S(1)} %constant_dynamic-update-slice_fusion), channel_id=1, source_target_pairs={{0,4},{1,5},{4,8},{5,9},{6,2},{7,3},{8,12},{9,13},{10,6},{11,7},{1... | collective-permute-start | bytes 786440 | tf_op jit(solution)/shard_map/ppermute | solution.py:287
  28.6 0.9 fusion
  29.4 0.9 pad_maximum_fusion.5
  30.4 1.9 %collective-permute-start.7 = (bf16[5,2,64,128]{3,2,1,0:T(8,128)(2,1)S(1)}, bf16[5,2,64,128]{3,2,1,0:T(8,128)(2,1)S(1)}, u32[]{:S(2)}, u32[]{:S(2)}) collective-permute-start(bf16[5,2,64,128]{3,2,1,0:T(8,128)(2,1)S(1)} %pad_maximum_fusion.5), channel_id=1, source_target_pairs={{0,2},{1,3},{2,0},{3,1},{4,6},{5,7},{6,4},{7,5},{8,10},{9,11},{10,... | collective-permute-start | bytes 491528 | tf_op jit(solution)/shard_map/ppermute | solution.py:287
  32.3 0.5 collective-permute-done.4
  32.8 0.1 pad_maximum_fusion.mine
  32.9 4.3 %collective-permute-start.5 = (bf16[8,6,64,128]{3,2,1,0:T(8,128)(2,1)S(1)}, bf16[8,6,64,128]{3,2,1,0:T(8,128)(2,1)S(1)}, u32[]{:S(2)}, u32[]{:S(2)}) collective-permute-start(bf16[8,6,64,128]{3,2,1,0:T(8,128)(2,1)S(1)} %pad_maximum_fusion.mine), channel_id=1, source_target_pairs={{0,1},{1,0},{2,3},{3,2},{4,5},{5,4},{6,7},{7,6},{8,9},{9,8},{10,11... | collective-permute-start | bytes 2359304 | tf_op jit(solution)/shard_map/ppermute | solution.py:287
  37.2 3.2 %collective-permute-done.7 = bf16[5,2,64,128]{3,2,1,0:T(8,128)(2,1)S(1)} collective-permute-done((bf16[5,2,64,128]{3,2,1,0:T(8,128)(2,1)S(1)}, bf16[5,2,64,128]{3,2,1,0:T(8,128)(2,1)S(1)}, u32[]{:S(2)}, u32[]{:S(2)}) %collective-permute-start.7) | collective-permute-done | bytes 163872 | tf_op jit(solution)/shard_map/ppermute | solution.py:287
  40.4 3.2 %collective-permute-start.8 = (bf16[5,2,64,128]{3,2,1,0:T(8,128)(2,1)S(1)}, bf16[5,2,64,128]{3,2,1,0:T(8,128)(2,1)S(1)}, u32[]{:S(2)}, u32[]{:S(2)}) collective-permute-start(bf16[5,2,64,128]{3,2,1,0:T(8,128)(2,1)S(1)} %collective-permute-done.7), channel_id=1, source_target_pairs={{0,4},{1,5},{4,8},{5,9},{6,2},{7,3},{8,12},{9,13},{10,6},{11,7},{1... | collective-permute-start | bytes 491528 | tf_op jit(solution)/shard_map/ppermute | solution.py:287
  43.6 2.2 %collective-permute-done.8 = bf16[5,2,64,128]{3,2,1,0:T(8,128)(2,1)S(1)} collective-permute-done((bf16[5,2,64,128]{3,2,1,0:T(8,128)(2,1)S(1)}, bf16[5,2,64,128]{3,2,1,0:T(8,128)(2,1)S(1)}, u32[]{:S(2)}, u32[]{:S(2)}) %collective-permute-start.8) | collective-permute-done | bytes 163872 | tf_op jit(solution)/shard_map/ppermute | solution.py:287
  45.9 0.1 pad_maximum_fusion.1.mine
  45.9 9.0 %collective-permute-start.9 = (bf16[5,6,64,128]{3,2,1,0:T(8,128)(2,1)S(1)}, bf16[5,6,64,128]{3,2,1,0:T(8,128)(2,1)S(1)}, u32[]{:S(2)}, u32[]{:S(2)}) collective-permute-start(bf16[5,6,64,128]{3,2,1,0:T(8,128)(2,1)S(1)} %pad_maximum_fusion.1.mine), channel_id=1, source_target_pairs={{0,1},{1,0},{2,3},{3,2},{4,5},{5,4},{6,7},{7,6},{8,9},{9,8},{10,11... | collective-permute-start | bytes 1474568 | tf_op jit(solution)/shard_map/ppermute | solution.py:287
  55.0 4.0 %collective-permute-start.6 = (bf16[13,1,64,128]{3,2,1,0:T(8,128)(2,1)S(1)}, bf16[13,1,64,128]{3,2,1,0:T(8,128)(2,1)S(1)}, u32[]{:S(2)}, u32[]{:S(2)}) collective-permute-start(bf16[13,1,64,128]{3,2,1,0:T(8,128)(2,1)S(1)} %pad_maximum_fusion.2), channel_id=1, source_target_pairs={{1,4},{3,6},{5,8},{7,10},{9,12},{11,14},{13,16},{15,18},{17,20},{1... | collective-permute-start | bytes 638984 | tf_op jit(solution)/shard_map/ppermute | solution.py:287
  59.0 2.8 %collective-permute-done.6.edge = bf16[13,1,64,128]{3,2,1,0:T(8,128)(2,1)S(1)} collective-permute-done((bf16[13,1,64,128]{3,2,1,0:T(8,128)(2,1)S(1)}, bf16[13,1,64,128]{3,2,1,0:T(8,128)(2,1)S(1)}, u32[]{:S(2)}, u32[]{:S(2)}) %collective-permute-start.6) | collective-permute-done | bytes 213024 | tf_op jit(solution)/shard_map/ppermute | solution.py:287
  61.8 4.3 %own.1 = (f32[4,2,64,128]{3,2,1,0:T(8,128)S(1)}, f32[4,2,64,128]{3,2,1,0:T(8,128)S(1)}, f32[4,2,64,128]{3,2,1,0:T(8,128)S(1)}, f32[4,9,64,128]{3,2,1,0:T(8,128)S...) custom-call(s32[4,3]{1,0:T(4,128)S(1)} %copy-done, ...), custom_call_target="tpu_custom_call" | custom-call | flops 20000000 | bytes 8388608 | tf_op jit(solution)/shard_map/own/pallas_call | solution.py:322
  66.1 6.4 %partner.1 = (f32[8,2,64,128]{3,2,1,0:T(8,128)S(1)}, f32[8,2,64,128]{3,2,1,0:T(8,128)S(1)}, f32[8,2,64,128]{3,2,1,0:T(8,128)S(1)}, f32[32,8,128]{2,1,0:T(8,128)S(1)}) custom-call(s32[4,3]{1,0:T(4,128)S(1)} %copy-done, bf16[8,6,64,128]{3,2,1,0:T(8,128)(2,1)S(1)} %pad_maximum_fusion.mine, bf16[8,6,64,128]{3,2,1,0:T(8,128)(2,1)S(1)} %collective-permute-done.5.other, ...), custom_call_target="tpu_custom_call" | custom-call | flops 40000000 | bytes 16777216 | tf_op jit(solution)/shard_map/partner/pallas_call | solution.py:346
  72.5 22.3 %all_to_all.5.sums = f32[32,8,128]{2,1,0:T(8,128)S(1)} all-to-all(f32[32,8,128]{2,1,0:T(8,128)S(1)} %get-tuple-element.22), channel_id=1, replica_groups=mesh['mode'=16,'space'=32] {'space'}, dimensions={0} | all-to-all | bytes 262144 | tf_op jit(solution)/shard_map/all_to_all | solution.py:361
  94.8 1.2 %combine.1 = f32[12,2,64,128]{3,2,1,0:T(8,128)} custom-call(f32[32,8,128]{2,1,0:T(8,128)S(1)} %all_to_all.5.sums, f32[4,2,64,128]{3,2,1,0:T(8,128)S(1)} %get-tuple-element.23.a0, f32[4,2,64,128]{3,2,1,0:T(8,128)S(1)} %get-tuple-element.24.a1, f32[4,2,64,128]{3,2,1,0:T(8,128)S(1)} %get-tuple-element.25.a2, f32[8,2,64,128]{3,2,1,0:T(8,128)S(1)} %get-tuple-element.26.b0, ...), custom_call_target="tpu_custom_call" | custom-call | tf_op jit(solution)/shard_map/combine/pallas_call | solution.py:363
  (15 shorter events, 0.1 us)
Async XLA Ops:
  0.0 19.9 %collective-permute-start.2 = (bf16[4,2,64,128]{3,2,1,0:T(8,128)(2,1)}, bf16[4,2,64,128]{3,2,1,0:T(8,128)(2,1)S(1)}, u32[]{:S(2)}, u32[]{:S(2)}) collective-permute-start(bf16[4,2,64,128]{3,2,1,0:T(8,128)(2,1)} %param.5), channel_id=1, source_target_pairs={{0,34},{1,35},{2,32},{3,33},{4,38},{5,39},{6,36},{7,37},{8,42},{9,... | collective-permute-start | bytes 393224 | tf_op jit(solution)/shard_map/ppermute | solution.py:287
  11.5 13.9 %collective-permute-start.3 = (bf16[4,2,64,128]{3,2,1,0:T(8,128)(2,1)}, bf16[4,2,64,128]{3,2,1,0:T(8,128)(2,1)S(1)}, u32[]{:S(2)}, u32[]{:S(2)}) collective-permute-start(bf16[4,2,64,128]{3,2,1,0:T(8,128)(2,1)} %param.5), channel_id=1, source_target_pairs={{0,66},{1,67},{2,64},{3,65},{4,70},{5,71},{6,68},{7,69},{8,74},{9,... | collective-permute-start | bytes 393224 | tf_op jit(solution)/shard_map/ppermute | solution.py:287
  13.4 18.9 %collective-permute-start.1 = (bf16[4,2,64,128]{3,2,1,0:T(8,128)(2,1)}, bf16[4,2,64,128]{3,2,1,0:T(8,128)(2,1)S(1)}, u32[]{:S(2)}, u32[]{:S(2)}) collective-permute-start(bf16[4,2,64,128]{3,2,1,0:T(8,128)(2,1)} %param.5), channel_id=1, source_target_pairs={{0,64},{1,65},{2,66},{3,67},{4,68},{5,69},{6,70},{7,71},{8,72},{9,... | collective-permute-start | bytes 393224 | tf_op jit(solution)/shard_map/ppermute | solution.py:287
  17.4 14.9 %collective-permute-start = (bf16[4,2,64,128]{3,2,1,0:T(8,128)(2,1)}, bf16[4,2,64,128]{3,2,1,0:T(8,128)(2,1)S(1)}, u32[]{:S(2)}, u32[]{:S(2)}) collective-permute-start(bf16[4,2,64,128]{3,2,1,0:T(8,128)(2,1)} %param.5), channel_id=1, source_target_pairs={{0,32},{1,33},{2,34},{3,35},{4,36},{5,37},{6,38},{7,39},{8,40},{9,... | collective-permute-start | bytes 393224 | tf_op jit(solution)/shard_map/ppermute | solution.py:287
  20.0 25.9 %copy-start.3 = (bf16[4,2,64,128]{3,2,1,0:T(8,128)(2,1)S(1)}, bf16[4,2,64,128]{3,2,1,0:T(8,128)(2,1)}, u32[]{:S(2)}) copy-start(bf16[4,2,64,128]{3,2,1,0:T(8,128)(2,1)} %param.5) | copy-start | bytes 393220
  25.4 7.5 %collective-permute-start.4 = (bf16[8,2,64,128]{3,2,1,0:T(8,128)(2,1)S(1)}, bf16[8,2,64,128]{3,2,1,0:T(8,128)(2,1)S(1)}, u32[]{:S(2)}, u32[]{:S(2)}) collective-permute-start(bf16[8,2,64,128]{3,2,1,0:T(8,128)(2,1)S(1)} %constant_dynamic-update-slice_fusion), channel_id=1, source_target_pairs={{0,4},{1,5},{4,8},{5,9},{6,2},{7,3},{8,12},{9,13},{10,6},{11,7},{1... | collective-permute-start | bytes 786440 | tf_op jit(solution)/shard_map/ppermute | solution.py:287
  30.4 10.1 %collective-permute-start.7 = (bf16[5,2,64,128]{3,2,1,0:T(8,128)(2,1)S(1)}, bf16[5,2,64,128]{3,2,1,0:T(8,128)(2,1)S(1)}, u32[]{:S(2)}, u32[]{:S(2)}) collective-permute-start(bf16[5,2,64,128]{3,2,1,0:T(8,128)(2,1)S(1)} %pad_maximum_fusion.5), channel_id=1, source_target_pairs={{0,2},{1,3},{2,0},{3,1},{4,6},{5,7},{6,4},{7,5},{8,10},{9,11},{10,... | collective-permute-start | bytes 491528 | tf_op jit(solution)/shard_map/ppermute | solution.py:287
  32.9 28.9 %copy-start = (s32[4,3]{1,0:T(4,128)S(1)}, s32[4,3]{1,0:T(4,128)}, u32[]{:S(2)}) copy-start(s32[4,3]{1,0:T(4,128)} %plan.3) | copy-start | bytes 148
  32.9 28.9 %copy-start.1 = (f32[8]{0:T(128)S(1)}, f32[8]{0:T(128)}, u32[]{:S(2)}) copy-start(f32[8]{0:T(128)} %stiff.1) | copy-start | bytes 100
  32.9 28.8 %copy-start.2 = (f32[8]{0:T(128)S(1)}, f32[8]{0:T(128)}, u32[]{:S(2)}) copy-start(f32[8]{0:T(128)} %cubic.1) | copy-start | bytes 100
  32.9 33.2 %collective-permute-start.5 = (bf16[8,6,64,128]{3,2,1,0:T(8,128)(2,1)S(1)}, bf16[8,6,64,128]{3,2,1,0:T(8,128)(2,1)S(1)}, u32[]{:S(2)}, u32[]{:S(2)}) collective-permute-start(bf16[8,6,64,128]{3,2,1,0:T(8,128)(2,1)S(1)} %pad_maximum_fusion.mine), channel_id=1, source_target_pairs={{0,1},{1,0},{2,3},{3,2},{4,5},{5,4},{6,7},{7,6},{8,9},{9,8},{10,11... | collective-permute-start | bytes 2359304 | tf_op jit(solution)/shard_map/ppermute | solution.py:287
  40.4 5.4 %collective-permute-start.8 = (bf16[5,2,64,128]{3,2,1,0:T(8,128)(2,1)S(1)}, bf16[5,2,64,128]{3,2,1,0:T(8,128)(2,1)S(1)}, u32[]{:S(2)}, u32[]{:S(2)}) collective-permute-start(bf16[5,2,64,128]{3,2,1,0:T(8,128)(2,1)S(1)} %collective-permute-done.7), channel_id=1, source_target_pairs={{0,4},{1,5},{4,8},{5,9},{6,2},{7,3},{8,12},{9,13},{10,6},{11,7},{1... | collective-permute-start | bytes 491528 | tf_op jit(solution)/shard_map/ppermute | solution.py:287
  45.9 15.8 %collective-permute-start.9 = (bf16[5,6,64,128]{3,2,1,0:T(8,128)(2,1)S(1)}, bf16[5,6,64,128]{3,2,1,0:T(8,128)(2,1)S(1)}, u32[]{:S(2)}, u32[]{:S(2)}) collective-permute-start(bf16[5,6,64,128]{3,2,1,0:T(8,128)(2,1)S(1)} %pad_maximum_fusion.1.mine), channel_id=1, source_target_pairs={{0,1},{1,0},{2,3},{3,2},{4,5},{5,4},{6,7},{7,6},{8,9},{9,8},{10,11... | collective-permute-start | bytes 1474568 | tf_op jit(solution)/shard_map/ppermute | solution.py:287
  55.0 6.8 %collective-permute-start.6 = (bf16[13,1,64,128]{3,2,1,0:T(8,128)(2,1)S(1)}, bf16[13,1,64,128]{3,2,1,0:T(8,128)(2,1)S(1)}, u32[]{:S(2)}, u32[]{:S(2)}) collective-permute-start(bf16[13,1,64,128]{3,2,1,0:T(8,128)(2,1)S(1)} %pad_maximum_fusion.2), channel_id=1, source_target_pairs={{1,4},{3,6},{5,8},{7,10},{9,12},{11,14},{13,16},{15,18},{17,20},{1... | collective-permute-start | bytes 638984 | tf_op jit(solution)/shard_map/ppermute | solution.py:287
where the time goes:
time: 96.4 us; the launch traced here: 96 us
  starting transfers between devices  45.2 us (47%)
  blocking collectives  22.3 us (23%)
  waiting for transfers between devices  14.4 us (15%)
  Pallas kernels  11.9 us (12%)
  other arithmetic  1.95 us (2%)
    ppermute x10, starting transfers between devices, send(): return lax.ppermute(x, ('mode', 'space'), pairs)  45.2 us
    all_to_all x1, blocking collectives, shards(): gathered = lax.all_to_all(sums, 'space', 0, 0)  22.3 us
    ppermute x10, waiting for transfers between devices, send(): return lax.ppermute(x, ('mode', 'space'), pairs)  14.4 us
    pallas_call x1, Pallas kernels, shards(): pl.pallas_call(partner_kernel, out_shape=(*[array(rest, slabs, *slab)] *...  6.37 us
    pallas_call x1, Pallas kernels, shards(): pl.pallas_call(own_kernel, out_shape=(*vectors, array(per_block, 9, *slab...  4.31 us
  transfers between devices with their start and end apart: 10, of which 6 were waited for; matrix products, arithmetic and copies ran while one was open for 2% of the time, Pallas kernels for 4%

commit v1 on v0

--- a/solution.py
+++ b/solution.py
@@ -24,33 +24,29 @@
         ref[lead + (i, pl.ds(PAD + ny, PAD))] = zero
 
 
-def fill_window(wide, mine, other, edge, edge_at):
-    stacks, ny = mine.shape[0], mine.shape[2]
+def position():
     space = lax.axis_index("space")
     core = space % 2
     high = (space // 2) % 2
-    origin = 4 * high + 2 * core
-
+    return core, high, 4 * high + 2 * core
+
+
+def clear_window(wide):
     def clear(m, carry):
         clear_rims(wide, (m,))
         return carry
 
-    lax.fori_loop(0, stacks, clear, 0)
-
-    def place(ref, slot, at, first):
-        spot = at - origin
-
-        @pl.when(jnp.logical_and(spot >= 0, spot < WINDOW))
-        def _():
-            for m in range(stacks):
-                wide[m, spot, pl.ds(PAD, ny)] = ref[first + m, slot].astype(f32)
-
-    for ref, q in ((mine, core), (other, 1 - core)):
-        for i in range(2):
-            place(ref, i, 5 + 4 * high + 2 * q + i, 0)
-            place(ref, 2 + i, 5 + 4 * (1 - high) + 2 * q + i, 0)
-            place(ref, 4 + i, 1 + 12 * high + 2 * q + i, 0)
-    place(edge, 0, 4 * high, edge_at)
+    lax.fori_loop(0, wide.shape[0], clear, 0)
+
+
+def place(wide, origin, to, ref, slot, at, first, count):
+    ny = ref.shape[2]
+    spot = at - origin
+
+    @pl.when(jnp.logical_and(spot >= 0, spot < WINDOW))
+    def _():
+        for m in range(count):
+            wide[to + m, spot, pl.ds(PAD, ny)] = ref[first + m, slot].astype(f32)
 
 
 def laplace_at(ref, lead, i, r, lane):
@@ -180,13 +176,36 @@
             clear_rims(ref, (t,))
 
 
-def own_kernel(plan, stiff, cubic, mine, other, edge,
-               first, second, third, lap_own, dinv, diag, faces, moments,
-               wide, gain, lap, prod, v0, v1, v2):
-    blocks, nz = lap.shape[0], lap.shape[-1]
+def partner_kernel(mine, other, lap, wide):
+    count = mine.shape[0]
+    core, high, origin = position()
+    clear_window(wide)
+    for ref, q in ((mine, core), (other, 1 - core)):
+        to = q * count
+        for k in range(4):
+            slab = 2 * q + k if k < 2 else 2 * (1 - q) + k - 2
+            place(wide, origin, to, ref, k, 5 + 4 * high + slab, 0, count)
+            place(wide, origin, to, ref, 4 + k, 5 + 4 * (1 - high) + slab, 0, count)
+            place(wide, origin, to, ref, 8 + k, 1 + 12 * high + slab, 0, count)
+        place(wide, origin, to, ref, 12, 4 * high, 0, count)
+    laps(wide, lap, lap.shape[0])
+
+
+def field_kernel(plan, stiff, cubic, mine, other, far, far_other, edge, lap_rest,
+                 first, second, third, sums,
+                 wide, gain, dinv, diag, faces, lap, lap_own, prod, v0, v1, v2):
+    blocks, nz = lap_own.shape[0], lap.shape[-1]
+    core, high, origin = position()
     scratch = (prod, v0, v1, v2)
     clear_fields(scratch)
-    fill_window(wide, mine, other, edge, 0)
+    clear_window(wide)
+    stacks = blocks + 1
+    for ref, more, q in ((mine, far, core), (other, far_other, 1 - core)):
+        for i in range(2):
+            place(wide, origin, 0, ref, i, 5 + 4 * high + 2 * q + i, 0, stacks)
+            place(wide, origin, 0, more, i, 5 + 4 * (1 - high) + 2 * q + i, 0, stacks)
+            place(wide, origin, 0, more, 2 + i, 1 + 12 * high + 2 * q + i, 0, stacks)
+    place(wide, origin, 0, edge, 0, 4 * high, 0, stacks)
     material(wide, blocks, stiff, cubic, gain, dinv, diag, faces)
     laps(wide, lap, blocks)
 
@@ -197,37 +216,26 @@
 
     lax.fori_loop(0, blocks, scaled, 0)
 
-    def step(h, total):
-        group = [(h * GROUP + t, h * GROUP + t, (h * GROUP + t) * PARTNERS) for t in range(GROUP)]
-        j_of = [plan[g[0], 0] for g in group]
-        return krylov(group, lap_own, lap, j_of, (dinv, diag, faces), (first, second, third), scratch, total)
-
-    moments[...] = lax.fori_loop(0, blocks // GROUP, step, jnp.zeros((8, nz), f32))
-
-
-def partner_kernel(plan, mine, other, edge, lap_own, dinv, diag, faces, moments,
-                   first, second, third, sums,
-                   wide, lap, prod, v0, v1, v2):
-    blocks = lap_own.shape[0]
-    scratch = (prod, v0, v1, v2)
-    clear_fields(scratch)
-    fill_window(wide, mine, other, edge, blocks + 1)
-    laps(wide, lap, lap.shape[0])
     per = blocks // GROUP
-
-    def step(h, total):
-        s = 1 + h // per
-        b = (h - (s - 1) * per) * GROUP
-        group = [(b + t, (s - 1) * blocks + b + t, (b + t) * PARTNERS + s) for t in range(GROUP)]
-        j_of = [(s - 1) * blocks + plan[g[0], s] for g in group]
-        return krylov(group, lap_own, lap, j_of, (dinv, diag, faces), (first, second, third), scratch, total)
-
-    total = lax.fori_loop(0, (PARTNERS - 1) * per, step, moments[...])
+    shared = (dinv, diag, faces)
+
+    def step(lap_of, s, h, total):
+        group = [(h * GROUP + t, s * blocks + h * GROUP + t, (h * GROUP + t) * PARTNERS + s) for t in range(GROUP)]
+        j_of = [plan[g[0], s] if isinstance(s, int) else (s - 1) * blocks + plan[g[0], s] for g in group]
+        return krylov(group, lap_own, lap_of, j_of, shared, (first, second, third), scratch, total)
+
+    total = lax.fori_loop(0, per, lambda h, t: step(lap, 0, h, t), jnp.zeros((8, nz), f32))
+
+    def rest(n, t):
+        s = 1 + n // per
+        return step(lap_rest, s, n - (s - 1) * per, t)
+
+    total = lax.fori_loop(0, (PARTNERS - 1) * per, rest, total)
     for d in range(sums.shape[0]):
         sums[d] = total
 
 
-def combine_kernel(sums, a0, a1, a2, b0, b1, b2, out):
+def combine_kernel(sums, v0, v1, v2, out):
     m = jnp.sum(sums[...], axis=0)
     mu = [m[k : k + 1] for k in range(MOMENTS)]
     ka = [mu[k] - mu[k + 1] for k in range(MOMENTS - 1)]
@@ -262,13 +270,12 @@
     def pick(c, f):
         return jnp.sum(jnp.where(lane == f, c, 0.0), axis=1, keepdims=True)
 
-    blocks = a0.shape[0]
+    blocks = out.shape[0] // PARTNERS
     for f in range(out.shape[0]):
-        a, s = f // PARTNERS, f % PARTNERS
-        basis, at = ((a0, a1, a2), a) if s == 0 else ((b0, b1, b2), (s - 1) * blocks + a)
+        at = f % PARTNERS * blocks + f // PARTNERS
         c0, c1, c2 = (pick(c, f) for c in x)
         for i in range(out.shape[1]):
-            out[f, i] = c0 * basis[0][at, i] + c1 * basis[1][at, i] + c2 * basis[2][at, i]
+            out[f, i] = c0 * v0[at, i] + c1 * v1[at, i] + c2 * v2[at, i]
 
 
 def shards(modes, regions, stiffness, nonlinear, plan):
@@ -292,23 +299,23 @@
     def partner_core(m, y, h, c):
         return m, y, h, 1 - c
 
+    core = lax.axis_index("space") % 2
     labels = (regions + 1).astype(jnp.bfloat16)[None]
     raw = jnp.concatenate([modes, labels], 0)
+    raw_other = send(raw, partner_core)
     far0 = send(raw, lambda m, y, h, c: (m, y, 1 - h, c))
-    far1 = send(modes, lambda m, y, h, c: (m + 1, y, 1 - h, c))
-    far2 = send(modes, lambda m, y, h, c: (m + 2, y, 1 - h, c))
-    near1 = send(modes, lambda m, y, h, c: (m + 1, y, h, c))
-    near2 = send(modes, lambda m, y, h, c: (m + 2, y, h, c))
-    far12 = jnp.concatenate([far1, far2], 0)
-    near12 = jnp.concatenate([near1, near2], 0)
-    along0 = send(far0, along)
-    near = jnp.concatenate([raw, near12], 0)[:, 1:]
-    edge = send(near, lambda m, y, h, c: (m, y + 1, h, 0) if c == 1 else None)
-    along12 = send(far12, along)
-    mine0 = jnp.concatenate([raw, far0, along0], 1)
-    mine12 = jnp.concatenate([near12, far12, along12], 1)
-    other0 = send(mine0, partner_core)
-    other12 = send(mine12, partner_core)
+    chip = jnp.concatenate([raw, raw_other], 1)
+    four = chip[:per_block]
+    far = send(four, lambda m, y, h, c: (m + 1 + c, y, 1 - h, c))
+    near = send(four, lambda m, y, h, c: (m + 1 + c, y, h, c))
+    far_along = send(far, along)
+    far0_along = send(far0, along)
+    last = lax.dynamic_slice_in_dim(jnp.concatenate([chip, near], 0), 3 - 2 * core, 1, 1)
+    edge = send(last, lambda m, y, h, c: (m, y + 1, h, c))
+    mine = jnp.concatenate([near, far, far_along, edge[per_block + 1 :]], 1)
+    other = send(mine, partner_core)
+    more = jnp.concatenate([far0, far0_along], 1)
+    more_other = send(more, partner_core)
 
     vm = pl.BlockSpec(memory_space=pltpu.VMEM)
     sm = pl.BlockSpec(memory_space=pltpu.SMEM)
@@ -317,57 +324,48 @@
     def array(*shape):
         return jax.ShapeDtypeStruct(shape, f32)
 
-    field_scratch = [pltpu.VMEM((GROUP, WINDOW) + padded, f32) for _ in range(4)]
-    vectors = [array(per_block, *(slabs,), *slab)] * 3
-    a0, a1, a2, lap_own, dinv, diag, faces, moments = pl.pallas_call(
-        own_kernel,
-        out_shape=(
-            *vectors,
-            array(per_block, 9, *slab),
-            array(7, *slab),
-            array(slabs, *slab),
-            array(6, 5, *slab),
-            array(8, nz),
-        ),
-        in_specs=[sm, sm, sm, vm, vm, vm],
-        out_specs=(vm,) * 8,
+    rest = per_block * (PARTNERS - 1)
+    lap_rest = pl.pallas_call(
+        partner_kernel,
+        out_shape=array(rest, 9, *slab),
+        in_specs=[vm] * 2,
+        out_specs=vm,
+        scratch_shapes=[pltpu.VMEM((rest, WINDOW) + padded, f32)],
+        compiler_params=pltpu.CompilerParams(vmem_limit_bytes=20 << 20),
+        cost_estimate=pl.CostEstimate(flops=10_000_000, bytes_accessed=8 << 20, transcendentals=0),
+        name="partner",
+    )(mine, other)
+
+    v0, v1, v2, sums = pl.pallas_call(
+        field_kernel,
+        out_shape=(*([array(fields, slabs, *slab)] * 3), array(n_space, 8, nz)),
+        in_specs=[sm] * 3 + [vm] * 6,
+        out_specs=(vm,) * 4,
         scratch_shapes=[
             pltpu.VMEM((per_block + 1, WINDOW) + padded, f32),
             pltpu.VMEM((9,) + slab, f32),
+            pltpu.VMEM((7,) + slab, f32),
+            pltpu.VMEM((slabs,) + slab, f32),
+            pltpu.VMEM((6, 5) + slab, f32),
             pltpu.VMEM((per_block, 9) + slab, f32),
-            *field_scratch,
-        ],
-        compiler_params=pltpu.CompilerParams(vmem_limit_bytes=24 << 20),
-        cost_estimate=pl.CostEstimate(flops=20_000_000, bytes_accessed=8 << 20, transcendentals=0),
-        name="own",
-    )(plan, stiffness, nonlinear, mine0, other0, edge)
-
-    rest = per_block * (PARTNERS - 1)
-    b0, b1, b2, sums = pl.pallas_call(
-        partner_kernel,
-        out_shape=(*([array(rest, slabs, *slab)] * 3), array(n_space, 8, nz)),
-        in_specs=[sm] + [vm] * 8,
-        out_specs=(vm,) * 4,
-        scratch_shapes=[
-            pltpu.VMEM((rest, WINDOW) + padded, f32),
-            pltpu.VMEM((rest, 9) + slab, f32),
-            *field_scratch,
+            pltpu.VMEM((per_block, 9) + slab, f32),
+            *[pltpu.VMEM((GROUP, WINDOW) + padded, f32) for _ in range(4)],
         ],
         compiler_params=pltpu.CompilerParams(vmem_limit_bytes=24 << 20),
         cost_estimate=pl.CostEstimate(flops=40_000_000, bytes_accessed=16 << 20, transcendentals=0),
-        name="partner",
-    )(plan, mine12, other12, edge, lap_own, dinv, diag, faces, moments)
+        name="fields",
+    )(plan, stiffness, nonlinear, raw, raw_other, more, more_other, edge[: per_block + 1], lap_rest)
 
     gathered = lax.all_to_all(sums, "space", 0, 0)
 
     out = pl.pallas_call(
         combine_kernel,
         out_shape=array(fields, slabs, *slab),
-        in_specs=[vm] * 7,
+        in_specs=[vm] * 4,
         out_specs=vm,
         compiler_params=pltpu.CompilerParams(vmem_limit_bytes=16 << 20),
         name="combine",
-    )(gathered, a0, a1, a2, b0, b1, b2)
+    )(gathered, v0, v1, v2)
     return out.reshape((per_block, PARTNERS, slabs, ny, nz))
 
 

time: 96.4 us -> 107 us (1.11)
  waiting for transfers between devices: 14.4 us -> 26.5 us
  starting transfers between devices: 45.2 us -> 41.7 us
  other arithmetic: 1.95 us -> 3.71 us
  blocking collectives: 22.3 us -> 23.6 us
    ppermute x10 -> x9, waiting for transfers between devices: 14.4 us -> 26.5 us  [send(): return lax.ppermute(x, ('mode', 'space'), pairs)]
    ppermute x10 -> x9, starting transfers between devices: 45.2 us -> 41.7 us  [send(): return lax.ppermute(x, ('mode', 'space'), pairs)]
    concatenate x3, other arithmetic: 0.17 us -> 1.94 us  [the longest x1 0.93 us: shards(): chip = jnp.concatenate([raw, raw_other], 1)]
    all_to_all x1, blocking collectives: 22.3 us -> 23.6 us  [shards(): gathered = lax.all_to_all(sums, 'space', 0, 0)]
  transfers between devices with their start and end apart: 10 -> 9, of which waited for: 6 -> 6; matrix products, arithmetic and copies ran while one was open for 2% -> 1% of each run, Pallas kernels for 4% -> 2%
where the time goes in v1:
time: 107 us
  starting transfers between devices  41.7 us (39%)
  waiting for transfers between devices  26.5 us (25%)
  blocking collectives  23.6 us (22%)
  Pallas kernels  10.9 us (10%)
  other arithmetic  3.71 us (3%)
    ppermute x9, starting transfers between devices, send(): return lax.ppermute(x, ('mode', 'space'), pairs)  41.7 us
    ppermute x9, waiting for transfers between devices, send(): return lax.ppermute(x, ('mode', 'space'), pairs)  26.5 us
    all_to_all x1, blocking collectives, shards(): gathered = lax.all_to_all(sums, 'space', 0, 0)  23.6 us
    pallas_call x1, Pallas kernels, shards(): pl.pallas_call(field_kernel, out_shape=(*[array(fields, slabs, *slab)] *...  7.45 us
    pallas_call x1, Pallas kernels, shards(): pl.pallas_call(partner_kernel, out_shape=array(rest, 9, *slab), in_specs=...  2.18 us
  transfers between devices with their start and end apart: 9, of which 6 were waited for; matrix products, arithmetic and copies ran while one was open for 1% of the time, Pallas kernels for 2%

profile of v1, /device:TPU:1, one launch (start us, length us, event | category | flops | bytes accessed | tf_op | source)
XLA Modules:
  0.0 106.6 jit_solution(10475532852838592184)
XLA Ops:
  0.0 0.8 fusion.3
  0.9 0.9 pad_maximum_fusion.3.mine
  1.8 8.7 %collective-permute-start = (bf16[5,2,64,128]{3,2,1,0:T(8,128)(2,1)S(1)}, bf16[5,2,64,128]{3,2,1,0:T(8,128)(2,1)S(1)}, u32[]{:S(2)}, u32[]{:S(2)}) collective-permute-start(bf16[5,2,64,128]{3,2,1,0:T(8,128)(2,1)S(1)} %pad_maximum_fusion.3.mine), channel_id=1, source_target_pairs={{0,1},{1,0},{2,3},{3,2},{4,5},{5,4},{6,7},{7,6},{8,9},{9,8},{10,11... | collective-permute-start | bytes 491528 | tf_op jit(solution)/shard_map/ppermute | solution.py:294
  10.5 1.0 collective-permute-done.other
  11.5 0.9 pad_maximum_fusion.1
  12.5 5.3 %collective-permute-start.6 = (bf16[4,4,64,128]{3,2,1,0:T(8,128)(2,1)S(1)}, bf16[4,4,64,128]{3,2,1,0:T(8,128)(2,1)S(1)}, u32[]{:S(2)}, u32[]{:S(2)}) collective-permute-start(bf16[4,4,64,128]{3,2,1,0:T(8,128)(2,1)S(1)} %pad_maximum_fusion.1), channel_id=1, source_target_pairs={{0,34},{1,67},{2,32},{3,65},{4,38},{5,71},{6,36},{7,69},{8,42},{9,... | collective-permute-start | bytes 786440 | tf_op jit(solution)/shard_map/ppermute | solution.py:294
  17.8 3.1 %collective-permute-start.4 = (bf16[4,4,64,128]{3,2,1,0:T(8,128)(2,1)S(1)}, bf16[4,4,64,128]{3,2,1,0:T(8,128)(2,1)S(1)}, u32[]{:S(2)}, u32[]{:S(2)}) collective-permute-start(bf16[4,4,64,128]{3,2,1,0:T(8,128)(2,1)S(1)} %pad_maximum_fusion.1), channel_id=1, source_target_pairs={{0,32},{1,65},{2,34},{3,67},{4,36},{5,69},{6,38},{7,71},{8,40},{9,... | collective-permute-start | bytes 786440 | tf_op jit(solution)/shard_map/ppermute | solution.py:294
  20.9 10.0 %collective-permute-done.6 = bf16[4,4,64,128]{3,2,1,0:T(8,128)(2,1)S(1)} collective-permute-done((bf16[4,4,64,128]{3,2,1,0:T(8,128)(2,1)S(1)}, bf16[4,4,64,128]{3,2,1,0:T(8,128)(2,1)S(1)}, u32[]{:S(2)}, u32[]{:S(2)}) %collective-permute-start.6) | collective-permute-done | bytes 262176 | tf_op jit(solution)/shard_map/ppermute | solution.py:294
  30.9 3.2 %collective-permute-start.7 = (bf16[4,4,64,128]{3,2,1,0:T(8,128)(2,1)S(1)}, bf16[4,4,64,128]{3,2,1,0:T(8,128)(2,1)S(1)}, u32[]{:S(2)}, u32[]{:S(2)}) collective-permute-start(bf16[4,4,64,128]{3,2,1,0:T(8,128)(2,1)S(1)} %collective-permute-done.6), channel_id=1, source_target_pairs={{0,4},{1,5},{4,8},{5,9},{6,2},{7,3},{8,12},{9,13},{10,6},{11,7},{1... | collective-permute-start | bytes 786440 | tf_op jit(solution)/shard_map/ppermute | solution.py:294
  34.2 1.2 %collective-permute-done.4 = bf16[4,4,64,128]{3,2,1,0:T(8,128)(2,1)S(1)} collective-permute-done((bf16[4,4,64,128]{3,2,1,0:T(8,128)(2,1)S(1)}, bf16[4,4,64,128]{3,2,1,0:T(8,128)(2,1)S(1)}, u32[]{:S(2)}, u32[]{:S(2)}) %collective-permute-start.4) | collective-permute-done | bytes 262176 | tf_op jit(solution)/shard_map/ppermute | solution.py:294
  35.4 0.9 fusion.2
  36.3 3.2 %collective-permute-start.5 = (bf16[9,1,64,128]{3,2,1,0:T(8,128)(2,1)S(1)}, bf16[9,1,64,128]{3,2,1,0:T(8,128)(2,1)S(1)}, u32[]{:S(2)}, u32[]{:S(2)}) collective-permute-start(bf16[9,1,64,128]{3,2,1,0:T(8,128)(2,1)S(1)} %fusion.2), channel_id=1, source_target_pairs={{0,4},{1,5},{2,6},{3,7},{4,8},{5,9},{6,10},{7,11},{8,12},{9,13},{1... | collective-permute-start | bytes 442376 | tf_op jit(solution)/shard_map/ppermute | solution.py:294
  39.5 2.3 %collective-permute-done.5 = bf16[9,1,64,128]{3,2,1,0:T(8,128)(2,1)S(1)} collective-permute-done((bf16[9,1,64,128]{3,2,1,0:T(8,128)(2,1)S(1)}, bf16[9,1,64,128]{3,2,1,0:T(8,128)(2,1)S(1)}, u32[]{:S(2)}, u32[]{:S(2)}) %collective-permute-start.5) | collective-permute-done | bytes 147488 | tf_op jit(solution)/shard_map/ppermute | solution.py:294
  41.8 0.1 pad_maximum_fusion.mine
  42.0 5.0 %collective-permute-start.8 = (bf16[4,13,64,128]{3,2,1,0:T(8,128)(2,1)S(1)}, bf16[4,13,64,128]{3,2,1,0:T(8,128)(2,1)S(1)}, u32[]{:S(2)}, u32[]{:S(2)}) collective-permute-start(bf16[4,13,64,128]{3,2,1,0:T(8,128)(2,1)S(1)} %pad_maximum_fusion.mine), channel_id=1, source_target_pairs={{0,1},{1,0},{2,3},{3,2},{4,5},{5,4},{6,7},{7,6},{8,9},{9,8},{10,11... | collective-permute-start | bytes 2555912 | tf_op jit(solution)/shard_map/ppermute | solution.py:294
  47.0 1.9 %collective-permute-start.1 = (bf16[5,2,64,128]{3,2,1,0:T(8,128)(2,1)S(1)}, bf16[5,2,64,128]{3,2,1,0:T(8,128)(2,1)S(1)}, u32[]{:S(2)}, u32[]{:S(2)}) collective-permute-start(bf16[5,2,64,128]{3,2,1,0:T(8,128)(2,1)S(1)} %pad_maximum_fusion.3.mine), channel_id=1, source_target_pairs={{0,2},{1,3},{2,0},{3,1},{4,6},{5,7},{6,4},{7,5},{8,10},{9,11},{10,... | collective-permute-start | bytes 491528 | tf_op jit(solution)/shard_map/ppermute | solution.py:294
  48.9 9.7 %collective-permute-done.1 = bf16[5,2,64,128]{3,2,1,0:T(8,128)(2,1)S(1)} collective-permute-done((bf16[5,2,64,128]{3,2,1,0:T(8,128)(2,1)S(1)}, bf16[5,2,64,128]{3,2,1,0:T(8,128)(2,1)S(1)}, u32[]{:S(2)}, u32[]{:S(2)}) %collective-permute-start.1) | collective-permute-done | bytes 163872 | tf_op jit(solution)/shard_map/ppermute | solution.py:294
  58.6 4.1 %collective-permute-start.2 = (bf16[5,2,64,128]{3,2,1,0:T(8,128)(2,1)S(1)}, bf16[5,2,64,128]{3,2,1,0:T(8,128)(2,1)S(1)}, u32[]{:S(2)}, u32[]{:S(2)}) collective-permute-start(bf16[5,2,64,128]{3,2,1,0:T(8,128)(2,1)S(1)} %collective-permute-done.1), channel_id=1, source_target_pairs={{0,4},{1,5},{4,8},{5,9},{6,2},{7,3},{8,12},{9,13},{10,6},{11,7},{1... | collective-permute-start | bytes 491528 | tf_op jit(solution)/shard_map/ppermute | solution.py:294
  62.8 2.2 %collective-permute-done.2 = bf16[5,2,64,128]{3,2,1,0:T(8,128)(2,1)S(1)} collective-permute-done((bf16[5,2,64,128]{3,2,1,0:T(8,128)(2,1)S(1)}, bf16[5,2,64,128]{3,2,1,0:T(8,128)(2,1)S(1)}, u32[]{:S(2)}, u32[]{:S(2)}) %collective-permute-start.2) | collective-permute-done | bytes 163872 | tf_op jit(solution)/shard_map/ppermute | solution.py:294
  65.0 7.1 %collective-permute-start.3 = (bf16[5,4,64,128]{3,2,1,0:T(8,128)(2,1)S(1)}, bf16[5,4,64,128]{3,2,1,0:T(8,128)(2,1)S(1)}, u32[]{:S(2)}, u32[]{:S(2)}) collective-permute-start(bf16[5,4,64,128]{3,2,1,0:T(8,128)(2,1)S(1)} %constant_dynamic-update-slice_fusion.far), channel_id=1, source_target_pairs={{0,1},{1,0},{2,3},{3,2},{4,5},{5,4},{6,7},{7,6},{8,9},{9,8},{10,11... | collective-permute-start | bytes 983048 | tf_op jit(solution)/shard_map/ppermute | solution.py:294
  72.1 2.2 %partner.1.lap_rest = f32[8,9,64,128]{3,2,1,0:T(8,128)S(1)} custom-call(bf16[4,13,64,128]{3,2,1,0:T(8,128)(2,1)S(1)} %pad_maximum_fusion.mine, bf16[4,13,64,128]{3,2,1,0:T(8,128)(2,1)S(1)} %collective-permute-done.8.other), custom_call_target="tpu_custom_call" | custom-call | flops 10000000 | bytes 8388608 | tf_op jit(solution)/shard_map/partner/pallas_call | solution.py:328
  74.3 7.4 %fields.1 = (f32[12,2,64,128]{3,2,1,0:T(8,128)S(1)}, f32[12,2,64,128]{3,2,1,0:T(8,128)S(1)}, f32[12,2,64,128]{3,2,1,0:T(8,128)S(1)}, f32[32,8,128]{2,1,0:T(8,128)S(1)}) custom-call(s32[4,3]{1,0:T(4,128)S(1)} %copy-done, f32[8]{0:T(128)S(1)} %copy-done.1, f32[8]{0:T(128)S(1)} %copy-done.2, bf16[5,2,64,128]{3,2,1,0:T(8,128)(2,1)S(1)} %pad_maximum_fusion.3.mine, ...), custom_call_target="tpu_custom_call" | custom-call | flops 40000000 | bytes 16777216 | tf_op jit(solution)/shard_map/fields/pallas_call | solution.py:339
  81.8 23.6 %all_to_all.5.sums = f32[32,8,128]{2,1,0:T(8,128)S(1)} all-to-all(f32[32,8,128]{2,1,0:T(8,128)S(1)} %get-tuple-element.9), channel_id=1, replica_groups=mesh['mode'=16,'space'=32] {'space'}, dimensions={0} | all-to-all | bytes 262144 | tf_op jit(solution)/shard_map/all_to_all | solution.py:359
  105.4 1.2 %combine.1 = f32[12,2,64,128]{3,2,1,0:T(8,128)} custom-call(f32[32,8,128]{2,1,0:T(8,128)S(1)} %all_to_all.5.sums, f32[12,2,64,128]{3,2,1,0:T(8,128)S(1)} %get-tuple-element.10.v0, f32[12,2,64,128]{3,2,1,0:T(8,128)S(1)} %get-tuple-element.11.v1, f32[12,2,64,128]{3,2,1,0:T(8,128)S(1)} %get-tuple-element.12.v2), custom_call_target="tpu_custom_call" | custom-call | tf_op jit(solution)/shard_map/combine/pallas_call | solution.py:361
  (13 shorter events, 0.1 us)
Async XLA Ops:
  1.8 9.8 %collective-permute-start = (bf16[5,2,64,128]{3,2,1,0:T(8,128)(2,1)S(1)}, bf16[5,2,64,128]{3,2,1,0:T(8,128)(2,1)S(1)}, u32[]{:S(2)}, u32[]{:S(2)}) collective-permute-start(bf16[5,2,64,128]{3,2,1,0:T(8,128)(2,1)S(1)} %pad_maximum_fusion.3.mine), channel_id=1, source_target_pairs={{0,1},{1,0},{2,3},{3,2},{4,5},{5,4},{6,7},{7,6},{8,9},{9,8},{10,11... | collective-permute-start | bytes 491528 | tf_op jit(solution)/shard_map/ppermute | solution.py:294
  12.5 18.5 %collective-permute-start.6 = (bf16[4,4,64,128]{3,2,1,0:T(8,128)(2,1)S(1)}, bf16[4,4,64,128]{3,2,1,0:T(8,128)(2,1)S(1)}, u32[]{:S(2)}, u32[]{:S(2)}) collective-permute-start(bf16[4,4,64,128]{3,2,1,0:T(8,128)(2,1)S(1)} %pad_maximum_fusion.1), channel_id=1, source_target_pairs={{0,34},{1,67},{2,32},{3,65},{4,38},{5,71},{6,36},{7,69},{8,42},{9,... | collective-permute-start | bytes 786440 | tf_op jit(solution)/shard_map/ppermute | solution.py:294
  17.8 17.6 %collective-permute-start.4 = (bf16[4,4,64,128]{3,2,1,0:T(8,128)(2,1)S(1)}, bf16[4,4,64,128]{3,2,1,0:T(8,128)(2,1)S(1)}, u32[]{:S(2)}, u32[]{:S(2)}) collective-permute-start(bf16[4,4,64,128]{3,2,1,0:T(8,128)(2,1)S(1)} %pad_maximum_fusion.1), channel_id=1, source_target_pairs={{0,32},{1,65},{2,34},{3,67},{4,36},{5,69},{6,38},{7,71},{8,40},{9,... | collective-permute-start | bytes 786440 | tf_op jit(solution)/shard_map/ppermute | solution.py:294
  30.9 10.9 %collective-permute-start.7 = (bf16[4,4,64,128]{3,2,1,0:T(8,128)(2,1)S(1)}, bf16[4,4,64,128]{3,2,1,0:T(8,128)(2,1)S(1)}, u32[]{:S(2)}, u32[]{:S(2)}) collective-permute-start(bf16[4,4,64,128]{3,2,1,0:T(8,128)(2,1)S(1)} %collective-permute-done.6), channel_id=1, source_target_pairs={{0,4},{1,5},{4,8},{5,9},{6,2},{7,3},{8,12},{9,13},{10,6},{11,7},{1... | collective-permute-start | bytes 786440 | tf_op jit(solution)/shard_map/ppermute | solution.py:294
  36.3 5.5 %collective-permute-start.5 = (bf16[9,1,64,128]{3,2,1,0:T(8,128)(2,1)S(1)}, bf16[9,1,64,128]{3,2,1,0:T(8,128)(2,1)S(1)}, u32[]{:S(2)}, u32[]{:S(2)}) collective-permute-start(bf16[9,1,64,128]{3,2,1,0:T(8,128)(2,1)S(1)} %fusion.2), channel_id=1, source_target_pairs={{0,4},{1,5},{2,6},{3,7},{4,8},{5,9},{6,10},{7,11},{8,12},{9,13},{1... | collective-permute-start | bytes 442376 | tf_op jit(solution)/shard_map/ppermute | solution.py:294
  42.0 30.1 %collective-permute-start.8 = (bf16[4,13,64,128]{3,2,1,0:T(8,128)(2,1)S(1)}, bf16[4,13,64,128]{3,2,1,0:T(8,128)(2,1)S(1)}, u32[]{:S(2)}, u32[]{:S(2)}) collective-permute-start(bf16[4,13,64,128]{3,2,1,0:T(8,128)(2,1)S(1)} %pad_maximum_fusion.mine), channel_id=1, source_target_pairs={{0,1},{1,0},{2,3},{3,2},{4,5},{5,4},{6,7},{7,6},{8,9},{9,8},{10,11... | collective-permute-start | bytes 2555912 | tf_op jit(solution)/shard_map/ppermute | solution.py:294
  47.0 11.6 %collective-permute-start.1 = (bf16[5,2,64,128]{3,2,1,0:T(8,128)(2,1)S(1)}, bf16[5,2,64,128]{3,2,1,0:T(8,128)(2,1)S(1)}, u32[]{:S(2)}, u32[]{:S(2)}) collective-permute-start(bf16[5,2,64,128]{3,2,1,0:T(8,128)(2,1)S(1)} %pad_maximum_fusion.3.mine), channel_id=1, source_target_pairs={{0,2},{1,3},{2,0},{3,1},{4,6},{5,7},{6,4},{7,5},{8,10},{9,11},{10,... | collective-permute-start | bytes 491528 | tf_op jit(solution)/shard_map/ppermute | solution.py:294
  58.6 6.3 %collective-permute-start.2 = (bf16[5,2,64,128]{3,2,1,0:T(8,128)(2,1)S(1)}, bf16[5,2,64,128]{3,2,1,0:T(8,128)(2,1)S(1)}, u32[]{:S(2)}, u32[]{:S(2)}) collective-permute-start(bf16[5,2,64,128]{3,2,1,0:T(8,128)(2,1)S(1)} %collective-permute-done.1), channel_id=1, source_target_pairs={{0,4},{1,5},{4,8},{5,9},{6,2},{7,3},{8,12},{9,13},{10,6},{11,7},{1... | collective-permute-start | bytes 491528 | tf_op jit(solution)/shard_map/ppermute | solution.py:294
  62.8 11.5 %copy-start = (s32[4,3]{1,0:T(4,128)S(1)}, s32[4,3]{1,0:T(4,128)}, u32[]{:S(2)}) copy-start(s32[4,3]{1,0:T(4,128)} %plan.1) | copy-start | bytes 148
  62.8 11.5 %copy-start.1 = (f32[8]{0:T(128)S(1)}, f32[8]{0:T(128)}, u32[]{:S(2)}) copy-start(f32[8]{0:T(128)} %stiff.1) | copy-start | bytes 100
  62.8 11.5 %copy-start.2 = (f32[8]{0:T(128)S(1)}, f32[8]{0:T(128)}, u32[]{:S(2)}) copy-start(f32[8]{0:T(128)} %cubic.1) | copy-start | bytes 100
  65.0 9.3 %collective-permute-start.3 = (bf16[5,4,64,128]{3,2,1,0:T(8,128)(2,1)S(1)}, bf16[5,4,64,128]{3,2,1,0:T(8,128)(2,1)S(1)}, u32[]{:S(2)}, u32[]{:S(2)}) collective-permute-start(bf16[5,4,64,128]{3,2,1,0:T(8,128)(2,1)S(1)} %constant_dynamic-update-slice_fusion.far), channel_id=1, source_target_pairs={{0,1},{1,0},{2,3},{3,2},{4,5},{5,4},{6,7},{7,6},{8,9},{9,8},{10,11... | collective-permute-start | bytes 983048 | tf_op jit(solution)/shard_map/ppermute | solution.py:294

commit v2 on v0

--- a/solution.py
+++ b/solution.py
@@ -24,33 +24,29 @@
         ref[lead + (i, pl.ds(PAD + ny, PAD))] = zero
 
 
-def fill_window(wide, mine, other, edge, edge_at):
-    stacks, ny = mine.shape[0], mine.shape[2]
+def position():
     space = lax.axis_index("space")
     core = space % 2
     high = (space // 2) % 2
-    origin = 4 * high + 2 * core
-
+    return core, high, 4 * high + 2 * core
+
+
+def clear_window(wide):
     def clear(m, carry):
         clear_rims(wide, (m,))
         return carry
 
-    lax.fori_loop(0, stacks, clear, 0)
-
-    def place(ref, slot, at, first):
-        spot = at - origin
-
-        @pl.when(jnp.logical_and(spot >= 0, spot < WINDOW))
-        def _():
-            for m in range(stacks):
-                wide[m, spot, pl.ds(PAD, ny)] = ref[first + m, slot].astype(f32)
-
-    for ref, q in ((mine, core), (other, 1 - core)):
-        for i in range(2):
-            place(ref, i, 5 + 4 * high + 2 * q + i, 0)
-            place(ref, 2 + i, 5 + 4 * (1 - high) + 2 * q + i, 0)
-            place(ref, 4 + i, 1 + 12 * high + 2 * q + i, 0)
-    place(edge, 0, 4 * high, edge_at)
+    lax.fori_loop(0, wide.shape[0], clear, 0)
+
+
+def place(wide, origin, to, ref, slot, at, first, count):
+    ny = ref.shape[2]
+    spot = at - origin
+
+    @pl.when(jnp.logical_and(spot >= 0, spot < WINDOW))
+    def _():
+        for m in range(count):
+            wide[to + m, spot, pl.ds(PAD, ny)] = ref[first + m, slot].astype(f32)
 
 
 def laplace_at(ref, lead, i, r, lane):
@@ -180,13 +176,27 @@
             clear_rims(ref, (t,))
 
 
-def own_kernel(plan, stiff, cubic, mine, other, edge,
+def pack_kernel(modes, regions, raw):
+    blocks = modes.shape[0]
+    raw[pl.ds(0, blocks)] = modes[...]
+    raw[blocks] = (regions[...] + 1).astype(raw.dtype)
+
+
+def own_kernel(plan, stiff, cubic, mine, other, far, far_other, edge,
                first, second, third, lap_own, dinv, diag, faces, moments,
                wide, gain, lap, prod, v0, v1, v2):
     blocks, nz = lap.shape[0], lap.shape[-1]
+    core, high, origin = position()
     scratch = (prod, v0, v1, v2)
     clear_fields(scratch)
-    fill_window(wide, mine, other, edge, 0)
+    clear_window(wide)
+    stacks = blocks + 1
+    for ref, more, q in ((mine, far, core), (other, far_other, 1 - core)):
+        for i in range(2):
+            place(wide, origin, 0, ref, i, 5 + 4 * high + 2 * q + i, 0, stacks)
+            place(wide, origin, 0, more, i, 5 + 4 * (1 - high) + 2 * q + i, 0, stacks)
+            place(wide, origin, 0, more, 2 + i, 1 + 12 * high + 2 * q + i, 0, stacks)
+    place(wide, origin, 0, edge, 0, 4 * high, 0, stacks)
     material(wide, blocks, stiff, cubic, gain, dinv, diag, faces)
     laps(wide, lap, blocks)
 
@@ -205,13 +215,22 @@
     moments[...] = lax.fori_loop(0, blocks // GROUP, step, jnp.zeros((8, nz), f32))
 
 
-def partner_kernel(plan, mine, other, edge, lap_own, dinv, diag, faces, moments,
+def partner_kernel(plan, mine, other, lap_own, dinv, diag, faces, moments,
                    first, second, third, sums,
                    wide, lap, prod, v0, v1, v2):
-    blocks = lap_own.shape[0]
+    blocks = mine.shape[0]
+    core, high, origin = position()
     scratch = (prod, v0, v1, v2)
     clear_fields(scratch)
-    fill_window(wide, mine, other, edge, blocks + 1)
+    clear_window(wide)
+    for ref, q in ((mine, core), (other, 1 - core)):
+        to = q * blocks
+        for k in range(4):
+            slab = 2 * q + k if k < 2 else 2 * (1 - q) + k - 2
+            place(wide, origin, to, ref, k, 5 + 4 * high + slab, 0, blocks)
+            place(wide, origin, to, ref, 4 + k, 5 + 4 * (1 - high) + slab, 0, blocks)
+            place(wide, origin, to, ref, 8 + k, 1 + 12 * high + slab, 0, blocks)
+        place(wide, origin, to, ref, 12, 4 * high, 0, blocks)
     laps(wide, lap, lap.shape[0])
     per = blocks // GROUP
 
@@ -292,24 +311,6 @@
     def partner_core(m, y, h, c):
         return m, y, h, 1 - c
 
-    labels = (regions + 1).astype(jnp.bfloat16)[None]
-    raw = jnp.concatenate([modes, labels], 0)
-    far0 = send(raw, lambda m, y, h, c: (m, y, 1 - h, c))
-    far1 = send(modes, lambda m, y, h, c: (m + 1, y, 1 - h, c))
-    far2 = send(modes, lambda m, y, h, c: (m + 2, y, 1 - h, c))
-    near1 = send(modes, lambda m, y, h, c: (m + 1, y, h, c))
-    near2 = send(modes, lambda m, y, h, c: (m + 2, y, h, c))
-    far12 = jnp.concatenate([far1, far2], 0)
-    near12 = jnp.concatenate([near1, near2], 0)
-    along0 = send(far0, along)
-    near = jnp.concatenate([raw, near12], 0)[:, 1:]
-    edge = send(near, lambda m, y, h, c: (m, y + 1, h, 0) if c == 1 else None)
-    along12 = send(far12, along)
-    mine0 = jnp.concatenate([raw, far0, along0], 1)
-    mine12 = jnp.concatenate([near12, far12, along12], 1)
-    other0 = send(mine0, partner_core)
-    other12 = send(mine12, partner_core)
-
     vm = pl.BlockSpec(memory_space=pltpu.VMEM)
     sm = pl.BlockSpec(memory_space=pltpu.SMEM)
     slab, padded = (ny, nz), (ny + 2 * PAD, nz)
@@ -317,8 +318,28 @@
     def array(*shape):
         return jax.ShapeDtypeStruct(shape, f32)
 
+    raw = pl.pallas_call(
+        pack_kernel,
+        out_shape=jax.ShapeDtypeStruct((per_block + 1, slabs, *slab), modes.dtype),
+        in_specs=[vm, vm],
+        out_specs=vm,
+        compiler_params=pltpu.CompilerParams(vmem_limit_bytes=4 << 20),
+        name="pack",
+    )(modes, regions)
+
+    odd = lax.axis_index("space") & 1
+    raw_other = send(raw, partner_core)
+    far0 = send(raw, lambda m, y, h, c: (m, y, 1 - h, c))
+    four = jnp.concatenate([raw[:per_block], raw_other[:per_block]], 1)
+    far = send(four, lambda m, y, h, c: (m + 1 + c, y, 1 - h, c))
+    near = send(four, lambda m, y, h, c: (m + 1 + c, y, h, c))
+    edge0 = send(raw[:, 1:], lambda m, y, h, c: (m, y + 1, h, 0) if c == 1 else None)
+    far0_along = send(far0, along)
+    more = jnp.concatenate([far0, far0_along], 1)
+    more_other = send(more, partner_core)
+
     field_scratch = [pltpu.VMEM((GROUP, WINDOW) + padded, f32) for _ in range(4)]
-    vectors = [array(per_block, *(slabs,), *slab)] * 3
+    vectors = [array(per_block, slabs, *slab)] * 3
     a0, a1, a2, lap_own, dinv, diag, faces, moments = pl.pallas_call(
         own_kernel,
         out_shape=(
@@ -329,7 +350,7 @@
             array(6, 5, *slab),
             array(8, nz),
         ),
-        in_specs=[sm, sm, sm, vm, vm, vm],
+        in_specs=[sm] * 3 + [vm] * 5,
         out_specs=(vm,) * 8,
         scratch_shapes=[
             pltpu.VMEM((per_block + 1, WINDOW) + padded, f32),
@@ -340,13 +361,19 @@
         compiler_params=pltpu.CompilerParams(vmem_limit_bytes=24 << 20),
         cost_estimate=pl.CostEstimate(flops=20_000_000, bytes_accessed=8 << 20, transcendentals=0),
         name="own",
-    )(plan, stiffness, nonlinear, mine0, other0, edge)
+    )(plan, stiffness, nonlinear, raw, raw_other, more, more_other, edge0)
+
+    far_along = send(far, along)
+    last = lax.dynamic_slice_in_dim(near, 3 - 2 * odd, 1, 1, allow_negative_indices=False)
+    edge = send(last, lambda m, y, h, c: (m, y + 1, h, c))
+    mine = jnp.concatenate([near, far, far_along, edge], 1)
+    other = send(mine, partner_core)
 
     rest = per_block * (PARTNERS - 1)
     b0, b1, b2, sums = pl.pallas_call(
         partner_kernel,
         out_shape=(*([array(rest, slabs, *slab)] * 3), array(n_space, 8, nz)),
-        in_specs=[sm] + [vm] * 8,
+        in_specs=[sm] + [vm] * 7,
         out_specs=(vm,) * 4,
         scratch_shapes=[
             pltpu.VMEM((rest, WINDOW) + padded, f32),
@@ -356,7 +383,7 @@
         compiler_params=pltpu.CompilerParams(vmem_limit_bytes=24 << 20),
         cost_estimate=pl.CostEstimate(flops=40_000_000, bytes_accessed=16 << 20, transcendentals=0),
         name="partner",
-    )(plan, mine12, other12, edge, lap_own, dinv, diag, faces, moments)
+    )(plan, mine, other, lap_own, dinv, diag, faces, moments)
 
     gathered = lax.all_to_all(sums, "space", 0, 0)
 

time: 96.4 us -> 113 us (1.17)
  waiting for transfers between devices: 14.4 us -> 30.4 us
  blocking collectives: 22.3 us -> 24.8 us
  other arithmetic: 1.95 us -> 0.03 us
  starting transfers between devices: 45.2 us -> 43.3 us
  local copies, waits for them, and re-layouts: 0.05 us -> 1.93 us
    ppermute x10, waiting for transfers between devices: 14.4 us -> 30.4 us  [send(): return lax.ppermute(x, ('mode', 'space'), pairs)]
    all_to_all x1, blocking collectives: 22.3 us -> 24.8 us  [shards(): gathered = lax.all_to_all(sums, 'space', 0, 0)]
    ppermute x10, starting transfers between devices: 45.2 us -> 43.3 us  [send(): return lax.ppermute(x, ('mode', 'space'), pairs)]
    unnamed x9 -> x14, local copies, waits for them, and re-layouts: 0.03 us -> 1.86 us
  transfers between devices with their start and end apart: 10 -> 10, of which waited for: 6 -> 7; matrix products, arithmetic and copies ran while one was open for 2% -> 0% of each run, Pallas kernels for 4% -> 4%
where the time goes in v2:
time: 113 us
  starting transfers between devices  43.3 us (38%)
  waiting for transfers between devices  30.4 us (27%)
  blocking collectives  24.8 us (22%)
  Pallas kernels  12 us (11%)
  local copies, waits for them, and re-layouts  1.93 us (2%)
    ppermute x10, starting transfers between devices, send(): return lax.ppermute(x, ('mode', 'space'), pairs)  43.3 us
    ppermute x10, waiting for transfers between devices, send(): return lax.ppermute(x, ('mode', 'space'), pairs)  30.4 us
    all_to_all x1, blocking collectives, shards(): gathered = lax.all_to_all(sums, 'space', 0, 0)  24.8 us
    pallas_call x1, Pallas kernels, shards(): pl.pallas_call(partner_kernel, out_shape=(*[array(rest, slabs, *slab)] *...  6.44 us
    pallas_call x1, Pallas kernels, shards(): pl.pallas_call(own_kernel, out_shape=(*vectors, array(per_block, 9, *slab...  4.31 us
  transfers between devices with their start and end apart: 10, of which 7 were waited for; matrix products, arithmetic and copies ran while one was open for 0% of the time, Pallas kernels for 4%

profile of v2, /device:TPU:1, one launch (start us, length us, event | category | flops | bytes accessed | tf_op | source)
XLA Modules:
  0.0 112.6 jit_solution(4492349551401136546)
XLA Ops:
  0.0 0.9 copy-done
  0.9 0.8 copy-done.1
  1.8 8.7 %collective-permute-start = (bf16[5,2,64,128]{3,2,1,0:T(8,128)(2,1)S(1)}, bf16[5,2,64,128]{3,2,1,0:T(8,128)(2,1)S(1)}, u32[]{:S(2)}, u32[]{:S(2)}) collective-permute-start(bf16[5,2,64,128]{3,2,1,0:T(8,128)(2,1)S(1)} %pack.1.mine), channel_id=1, source_target_pairs={{0,1},{1,0},{2,3},{3,2},{4,5},{5,4},{6,7},{7,6},{8,9},{9,8},{10,11... | collective-permute-start | bytes 491528 | tf_op jit(solution)/shard_map/ppermute | solution.py:306
  10.5 1.0 collective-permute-done.other
  11.6 5.3 %collective-permute-start.2 = (bf16[4,4,64,128]{3,2,1,0:T(8,128)(2,1)S(1)}, bf16[4,4,64,128]{3,2,1,0:T(8,128)(2,1)S(1)}, u32[]{:S(2)}, u32[]{:S(2)}) collective-permute-start(bf16[4,4,64,128]{3,2,1,0:T(8,128)(2,1)S(1)} %pad_maximum_fusion), channel_id=1, source_target_pairs={{0,34},{1,67},{2,32},{3,65},{4,38},{5,71},{6,36},{7,69},{8,42},{9,... | collective-permute-start | bytes 786440 | tf_op jit(solution)/shard_map/ppermute | solution.py:306
  16.9 3.1 %collective-permute-start.1 = (bf16[4,4,64,128]{3,2,1,0:T(8,128)(2,1)S(1)}, bf16[4,4,64,128]{3,2,1,0:T(8,128)(2,1)S(1)}, u32[]{:S(2)}, u32[]{:S(2)}) collective-permute-start(bf16[4,4,64,128]{3,2,1,0:T(8,128)(2,1)S(1)} %pad_maximum_fusion), channel_id=1, source_target_pairs={{0,32},{1,65},{2,34},{3,67},{4,36},{5,69},{6,38},{7,71},{8,40},{9,... | collective-permute-start | bytes 786440 | tf_op jit(solution)/shard_map/ppermute | solution.py:306
  20.0 10.0 %collective-permute-done.2 = bf16[4,4,64,128]{3,2,1,0:T(8,128)(2,1)S(1)} collective-permute-done((bf16[4,4,64,128]{3,2,1,0:T(8,128)(2,1)S(1)}, bf16[4,4,64,128]{3,2,1,0:T(8,128)(2,1)S(1)}, u32[]{:S(2)}, u32[]{:S(2)}) %collective-permute-start.2) | collective-permute-done | bytes 262176 | tf_op jit(solution)/shard_map/ppermute | solution.py:306
  30.0 3.2 %collective-permute-start.3 = (bf16[4,4,64,128]{3,2,1,0:T(8,128)(2,1)S(1)}, bf16[4,4,64,128]{3,2,1,0:T(8,128)(2,1)S(1)}, u32[]{:S(2)}, u32[]{:S(2)}) collective-permute-start(bf16[4,4,64,128]{3,2,1,0:T(8,128)(2,1)S(1)} %collective-permute-done.2), channel_id=1, source_target_pairs={{0,4},{1,5},{4,8},{5,9},{6,2},{7,3},{8,12},{9,13},{10,6},{11,7},{1... | collective-permute-start | bytes 786440 | tf_op jit(solution)/shard_map/ppermute | solution.py:306
  33.3 1.2 %collective-permute-done.1 = bf16[4,4,64,128]{3,2,1,0:T(8,128)(2,1)S(1)} collective-permute-done((bf16[4,4,64,128]{3,2,1,0:T(8,128)(2,1)S(1)}, bf16[4,4,64,128]{3,2,1,0:T(8,128)(2,1)S(1)}, u32[]{:S(2)}, u32[]{:S(2)}) %collective-permute-start.1) | collective-permute-done | bytes 262176 | tf_op jit(solution)/shard_map/ppermute | solution.py:306
  34.5 0.0 copy-start.3
  34.5 3.3 %collective-permute-start.4 = (bf16[4,1,64,128]{3,2,1,0:T(8,128)(2,1)S(1)}, bf16[4,1,64,128]{3,2,1,0:T(8,128)(2,1)S(1)}, u32[]{:S(2)}, u32[]{:S(2)}) collective-permute-start(bf16[4,1,64,128]{3,2,1,0:T(8,128)(2,1)S(1)} %constant_dynamic-slice_fusion), channel_id=1, source_target_pairs={{0,4},{1,5},{2,6},{3,7},{4,8},{5,9},{6,10},{7,11},{8,12},{9,13},{1... | collective-permute-start | bytes 196616 | tf_op jit(solution)/shard_map/ppermute | solution.py:306
  38.0 1.8 %collective-permute-done.4 = bf16[4,1,64,128]{3,2,1,0:T(8,128)(2,1)S(1)} collective-permute-done((bf16[4,1,64,128]{3,2,1,0:T(8,128)(2,1)S(1)}, bf16[4,1,64,128]{3,2,1,0:T(8,128)(2,1)S(1)}, u32[]{:S(2)}, u32[]{:S(2)}) %collective-permute-start.4) | collective-permute-done | bytes 65568 | tf_op jit(solution)/shard_map/ppermute | solution.py:306
  39.8 5.5 %collective-permute-start.5 = (bf16[4,13,64,128]{3,2,1,0:T(8,128)(2,1)S(1)}, bf16[4,13,64,128]{3,2,1,0:T(8,128)(2,1)S(1)}, u32[]{:S(2)}, u32[]{:S(2)}) collective-permute-start(bf16[4,13,64,128]{3,2,1,0:T(8,128)(2,1)S(1)} %constant_dynamic-update-slice_fusion.mine), channel_id=1, source_target_pairs={{0,1},{1,0},{2,3},{3,2},{4,5},{5,4},{6,7},{7,6},{8,9},{9,8},{10,11... | collective-permute-start | bytes 2555912 | tf_op jit(solution)/shard_map/ppermute | solution.py:306
  45.3 1.9 %collective-permute-start.6 = (bf16[5,2,64,128]{3,2,1,0:T(8,128)(2,1)S(1)}, bf16[5,2,64,128]{3,2,1,0:T(8,128)(2,1)S(1)}, u32[]{:S(2)}, u32[]{:S(2)}) collective-permute-start(bf16[5,2,64,128]{3,2,1,0:T(8,128)(2,1)S(1)} %pack.1.mine), channel_id=1, source_target_pairs={{0,2},{1,3},{2,0},{3,1},{4,6},{5,7},{6,4},{7,5},{8,10},{9,11},{10,... | collective-permute-start | bytes 491528 | tf_op jit(solution)/shard_map/ppermute | solution.py:306
  47.2 12.7 %collective-permute-done.6 = bf16[5,2,64,128]{3,2,1,0:T(8,128)(2,1)S(1)} collective-permute-done((bf16[5,2,64,128]{3,2,1,0:T(8,128)(2,1)S(1)}, bf16[5,2,64,128]{3,2,1,0:T(8,128)(2,1)S(1)}, u32[]{:S(2)}, u32[]{:S(2)}) %collective-permute-start.6) | collective-permute-done | bytes 163872 | tf_op jit(solution)/shard_map/ppermute | solution.py:306
  59.9 3.9 %collective-permute-start.7 = (bf16[5,2,64,128]{3,2,1,0:T(8,128)(2,1)S(1)}, bf16[5,2,64,128]{3,2,1,0:T(8,128)(2,1)S(1)}, u32[]{:S(2)}, u32[]{:S(2)}) collective-permute-start(bf16[5,2,64,128]{3,2,1,0:T(8,128)(2,1)S(1)} %collective-permute-done.6), channel_id=1, source_target_pairs={{0,4},{1,5},{4,8},{5,9},{6,2},{7,3},{8,12},{9,13},{10,6},{11,7},{1... | collective-permute-start | bytes 491528 | tf_op jit(solution)/shard_map/ppermute | solution.py:306
  63.8 2.2 %collective-permute-done.7 = bf16[5,2,64,128]{3,2,1,0:T(8,128)(2,1)S(1)} collective-permute-done((bf16[5,2,64,128]{3,2,1,0:T(8,128)(2,1)S(1)}, bf16[5,2,64,128]{3,2,1,0:T(8,128)(2,1)S(1)}, u32[]{:S(2)}, u32[]{:S(2)}) %collective-permute-start.7) | collective-permute-done | bytes 163872 | tf_op jit(solution)/shard_map/ppermute | solution.py:306
  66.0 4.2 %collective-permute-start.8 = (bf16[5,4,64,128]{3,2,1,0:T(8,128)(2,1)S(1)}, bf16[5,4,64,128]{3,2,1,0:T(8,128)(2,1)S(1)}, u32[]{:S(2)}, u32[]{:S(2)}) collective-permute-start(bf16[5,4,64,128]{3,2,1,0:T(8,128)(2,1)S(1)} %constant_dynamic-update-slice_fusion.4.far), channel_id=1, source_target_pairs={{0,1},{1,0},{2,3},{3,2},{4,5},{5,4},{6,7},{7,6},{8,9},{9,8},{10,11... | collective-permute-start | bytes 983048 | tf_op jit(solution)/shard_map/ppermute | solution.py:306
  70.3 4.0 %collective-permute-start.9 = (bf16[5,1,64,128]{3,2,1,0:T(8,128)(2,1)S(1)}, bf16[5,1,64,128]{3,2,1,0:T(8,128)(2,1)S(1)}, u32[]{:S(2)}, u32[]{:S(2)}) collective-permute-start(bf16[5,1,64,128]{3,2,1,0:T(8,128)(2,1)S(1)} %slice.14), channel_id=1, source_target_pairs={{1,4},{3,6},{5,8},{7,10},{9,12},{11,14},{13,16},{15,18},{17,20},{1... | collective-permute-start | bytes 245768 | tf_op jit(solution)/shard_map/ppermute | solution.py:306
  74.3 1.5 %collective-permute-done.9.edge = bf16[5,1,64,128]{3,2,1,0:T(8,128)(2,1)S(1)} collective-permute-done((bf16[5,1,64,128]{3,2,1,0:T(8,128)(2,1)S(1)}, bf16[5,1,64,128]{3,2,1,0:T(8,128)(2,1)S(1)}, u32[]{:S(2)}, u32[]{:S(2)}) %collective-permute-start.9) | collective-permute-done | bytes 81952 | tf_op jit(solution)/shard_map/ppermute | solution.py:306
  75.8 4.3 %own.1 = (f32[4,2,64,128]{3,2,1,0:T(8,128)S(1)}, f32[4,2,64,128]{3,2,1,0:T(8,128)S(1)}, f32[4,2,64,128]{3,2,1,0:T(8,128)S(1)}, f32[4,9,64,128]{3,2,1,0:T(8,128)S...) custom-call(s32[4,3]{1,0:T(4,128)S(1)} %copy-done.2, ...), custom_call_target="tpu_custom_call" | custom-call | flops 20000000 | bytes 8388608 | tf_op jit(solution)/shard_map/own/pallas_call | solution.py:343
  80.1 6.4 %partner.1 = (f32[8,2,64,128]{3,2,1,0:T(8,128)S(1)}, f32[8,2,64,128]{3,2,1,0:T(8,128)S(1)}, f32[8,2,64,128]{3,2,1,0:T(8,128)S(1)}, f32[32,8,128]{2,1,0:T(8,128)S(1)}) custom-call(s32[4,3]{1,0:T(4,128)S(1)} %copy-done.2, bf16[4,13,64,128]{3,2,1,0:T(8,128)(2,1)S(1)} %constant_dynamic-update-slice_fusion.mine, ...), custom_call_target="tpu_custom_call" | custom-call | flops 40000000 | bytes 16777216 | tf_op jit(solution)/shard_map/partner/pallas_call | solution.py:373
  86.6 24.8 %all_to_all.5.sums = f32[32,8,128]{2,1,0:T(8,128)S(1)} all-to-all(f32[32,8,128]{2,1,0:T(8,128)S(1)} %get-tuple-element.22), channel_id=1, replica_groups=mesh['mode'=16,'space'=32] {'space'}, dimensions={0} | all-to-all | bytes 262144 | tf_op jit(solution)/shard_map/all_to_all | solution.py:388
  111.4 1.2 %combine.1 = f32[12,2,64,128]{3,2,1,0:T(8,128)} custom-call(f32[32,8,128]{2,1,0:T(8,128)S(1)} %all_to_all.5.sums, f32[4,2,64,128]{3,2,1,0:T(8,128)S(1)} %get-tuple-element.23.a0, f32[4,2,64,128]{3,2,1,0:T(8,128)S(1)} %get-tuple-element.24.a1, f32[4,2,64,128]{3,2,1,0:T(8,128)S(1)} %get-tuple-element.25.a2, f32[8,2,64,128]{3,2,1,0:T(8,128)S(1)} %get-tuple-element.26.b0, ...), custom_call_target="tpu_custom_call" | custom-call | tf_op jit(solution)/shard_map/combine/pallas_call | solution.py:390
  (22 shorter events, 0.2 us)
Async XLA Ops:
  0.0 0.9 copy-start
  0.9 0.8 copy-start.1
  1.8 9.8 %collective-permute-start = (bf16[5,2,64,128]{3,2,1,0:T(8,128)(2,1)S(1)}, bf16[5,2,64,128]{3,2,1,0:T(8,128)(2,1)S(1)}, u32[]{:S(2)}, u32[]{:S(2)}) collective-permute-start(bf16[5,2,64,128]{3,2,1,0:T(8,128)(2,1)S(1)} %pack.1.mine), channel_id=1, source_target_pairs={{0,1},{1,0},{2,3},{3,2},{4,5},{5,4},{6,7},{7,6},{8,9},{9,8},{10,11... | collective-permute-start | bytes 491528 | tf_op jit(solution)/shard_map/ppermute | solution.py:306
  11.6 18.5 %collective-permute-start.2 = (bf16[4,4,64,128]{3,2,1,0:T(8,128)(2,1)S(1)}, bf16[4,4,64,128]{3,2,1,0:T(8,128)(2,1)S(1)}, u32[]{:S(2)}, u32[]{:S(2)}) collective-permute-start(bf16[4,4,64,128]{3,2,1,0:T(8,128)(2,1)S(1)} %pad_maximum_fusion), channel_id=1, source_target_pairs={{0,34},{1,67},{2,32},{3,65},{4,38},{5,71},{6,36},{7,69},{8,42},{9,... | collective-permute-start | bytes 786440 | tf_op jit(solution)/shard_map/ppermute | solution.py:306
  16.9 17.6 %collective-permute-start.1 = (bf16[4,4,64,128]{3,2,1,0:T(8,128)(2,1)S(1)}, bf16[4,4,64,128]{3,2,1,0:T(8,128)(2,1)S(1)}, u32[]{:S(2)}, u32[]{:S(2)}) collective-permute-start(bf16[4,4,64,128]{3,2,1,0:T(8,128)(2,1)S(1)} %pad_maximum_fusion), channel_id=1, source_target_pairs={{0,32},{1,65},{2,34},{3,67},{4,36},{5,69},{6,38},{7,71},{8,40},{9,... | collective-permute-start | bytes 786440 | tf_op jit(solution)/shard_map/ppermute | solution.py:306
  30.0 7.9 %collective-permute-start.3 = (bf16[4,4,64,128]{3,2,1,0:T(8,128)(2,1)S(1)}, bf16[4,4,64,128]{3,2,1,0:T(8,128)(2,1)S(1)}, u32[]{:S(2)}, u32[]{:S(2)}) collective-permute-start(bf16[4,4,64,128]{3,2,1,0:T(8,128)(2,1)S(1)} %collective-permute-done.2), channel_id=1, source_target_pairs={{0,4},{1,5},{4,8},{5,9},{6,2},{7,3},{8,12},{9,13},{10,6},{11,7},{1... | collective-permute-start | bytes 786440 | tf_op jit(solution)/shard_map/ppermute | solution.py:306
  34.5 41.3 %copy-start.2 = (s32[4,3]{1,0:T(4,128)S(1)}, s32[4,3]{1,0:T(4,128)}, u32[]{:S(2)}) copy-start(s32[4,3]{1,0:T(4,128)} %plan.3) | copy-start | bytes 148
  34.5 41.3 %copy-start.3 = (f32[8]{0:T(128)S(1)}, f32[8]{0:T(128)}, u32[]{:S(2)}) copy-start(f32[8]{0:T(128)} %stiff.1) | copy-start | bytes 100
  34.5 41.3 %copy-start.4 = (f32[8]{0:T(128)S(1)}, f32[8]{0:T(128)}, u32[]{:S(2)}) copy-start(f32[8]{0:T(128)} %cubic.1) | copy-start | bytes 100
  34.5 5.2 %collective-permute-start.4 = (bf16[4,1,64,128]{3,2,1,0:T(8,128)(2,1)S(1)}, bf16[4,1,64,128]{3,2,1,0:T(8,128)(2,1)S(1)}, u32[]{:S(2)}, u32[]{:S(2)}) collective-permute-start(bf16[4,1,64,128]{3,2,1,0:T(8,128)(2,1)S(1)} %constant_dynamic-slice_fusion), channel_id=1, source_target_pairs={{0,4},{1,5},{2,6},{3,7},{4,8},{5,9},{6,10},{7,11},{8,12},{9,13},{1... | collective-permute-start | bytes 196616 | tf_op jit(solution)/shard_map/ppermute | solution.py:306
  39.8 40.3 %collective-permute-start.5 = (bf16[4,13,64,128]{3,2,1,0:T(8,128)(2,1)S(1)}, bf16[4,13,64,128]{3,2,1,0:T(8,128)(2,1)S(1)}, u32[]{:S(2)}, u32[]{:S(2)}) collective-permute-start(bf16[4,13,64,128]{3,2,1,0:T(8,128)(2,1)S(1)} %constant_dynamic-update-slice_fusion.mine), channel_id=1, source_target_pairs={{0,1},{1,0},{2,3},{3,2},{4,5},{5,4},{6,7},{7,6},{8,9},{9,8},{10,11... | collective-permute-start | bytes 2555912 | tf_op jit(solution)/shard_map/ppermute | solution.py:306
  45.3 14.6 %collective-permute-start.6 = (bf16[5,2,64,128]{3,2,1,0:T(8,128)(2,1)S(1)}, bf16[5,2,64,128]{3,2,1,0:T(8,128)(2,1)S(1)}, u32[]{:S(2)}, u32[]{:S(2)}) collective-permute-start(bf16[5,2,64,128]{3,2,1,0:T(8,128)(2,1)S(1)} %pack.1.mine), channel_id=1, source_target_pairs={{0,2},{1,3},{2,0},{3,1},{4,6},{5,7},{6,4},{7,5},{8,10},{9,11},{10,... | collective-permute-start | bytes 491528 | tf_op jit(solution)/shard_map/ppermute | solution.py:306
  59.9 6.1 %collective-permute-start.7 = (bf16[5,2,64,128]{3,2,1,0:T(8,128)(2,1)S(1)}, bf16[5,2,64,128]{3,2,1,0:T(8,128)(2,1)S(1)}, u32[]{:S(2)}, u32[]{:S(2)}) collective-permute-start(bf16[5,2,64,128]{3,2,1,0:T(8,128)(2,1)S(1)} %collective-permute-done.6), channel_id=1, source_target_pairs={{0,4},{1,5},{4,8},{5,9},{6,2},{7,3},{8,12},{9,13},{10,6},{11,7},{1... | collective-permute-start | bytes 491528 | tf_op jit(solution)/shard_map/ppermute | solution.py:306
  66.0 9.7 %collective-permute-start.8 = (bf16[5,4,64,128]{3,2,1,0:T(8,128)(2,1)S(1)}, bf16[5,4,64,128]{3,2,1,0:T(8,128)(2,1)S(1)}, u32[]{:S(2)}, u32[]{:S(2)}) collective-permute-start(bf16[5,4,64,128]{3,2,1,0:T(8,128)(2,1)S(1)} %constant_dynamic-update-slice_fusion.4.far), channel_id=1, source_target_pairs={{0,1},{1,0},{2,3},{3,2},{4,5},{5,4},{6,7},{7,6},{8,9},{9,8},{10,11... | collective-permute-start | bytes 983048 | tf_op jit(solution)/shard_map/ppermute | solution.py:306
  70.3 5.5 %collective-permute-start.9 = (bf16[5,1,64,128]{3,2,1,0:T(8,128)(2,1)S(1)}, bf16[5,1,64,128]{3,2,1,0:T(8,128)(2,1)S(1)}, u32[]{:S(2)}, u32[]{:S(2)}) collective-permute-start(bf16[5,1,64,128]{3,2,1,0:T(8,128)(2,1)S(1)} %slice.14), channel_id=1, source_target_pairs={{1,4},{3,6},{5,8},{7,10},{9,12},{11,14},{13,16},{15,18},{17,20},{1... | collective-permute-start | bytes 245768 | tf_op jit(solution)/shard_map/ppermute | solution.py:306

commit v3 on v2

--- a/solution.py
+++ b/solution.py
@@ -7,7 +7,8 @@
 
 PARTNERS = 3
 MASS = 0.5
-WINDOW = 11
+WINDOW = 13
+OWN = 4
 MOMENTS = 6
 GROUP = 2
 PAD = 8
@@ -26,9 +27,7 @@
 
 def position():
     space = lax.axis_index("space")
-    core = space % 2
-    high = (space // 2) % 2
-    return core, high, 4 * high + 2 * core
+    return space % 2, (space // 2) % 2
 
 
 def clear_window(wide):
@@ -39,14 +38,14 @@
     lax.fori_loop(0, wide.shape[0], clear, 0)
 
 
-def place(wide, origin, to, ref, slot, at, first, count):
+def place(wide, ref, slot, at):
     ny = ref.shape[2]
-    spot = at - origin
-
-    @pl.when(jnp.logical_and(spot >= 0, spot < WINDOW))
-    def _():
-        for m in range(count):
-            wide[to + m, spot, pl.ds(PAD, ny)] = ref[first + m, slot].astype(f32)
+    for m in range(ref.shape[0]):
+        wide[m, at, pl.ds(PAD, ny)] = ref[m, slot].astype(f32)
+
+
+def spots(high):
+    return 5, 9 - 8 * high, 1 + 8 * high, 0
 
 
 def laplace_at(ref, lead, i, r, lane):
@@ -65,7 +64,7 @@
     row = lax.broadcasted_iota(jnp.int32, (ny, nz), 0)
     lane = lax.broadcasted_iota(jnp.int32, (ny, nz), 1)
     body = pl.ds(PAD, ny)
-    for i in range(1, 10):
+    for i in range(1, 12):
         label = wide[label_at, i, body]
         c = jnp.zeros((ny, nz), f32)
         g = jnp.zeros((ny, nz), f32)
@@ -75,7 +74,7 @@
             g = jnp.where(hit, cubic[r], g)
         wide[label_at, i, body] = c
         gain[i - 1] = g
-    for i in range(2, 9):
+    for i in range(2, 11):
         c = wide[label_at, i, body]
         beside = (
             wide[label_at, i - 1, body],
@@ -89,9 +88,9 @@
         d = MASS + ws[0] + ws[1] + ws[2] + ws[3] + ws[4] + ws[5]
         inv = jnp.where(gain[i - 1] > 0.0, 1.0 / d, 0.0)
         dinv[i - 2] = inv
-        if 5 <= i <= 6:
+        if 5 <= i < 5 + OWN:
             diag[i - 5] = d
-        if 3 <= i <= 7:
+        if 3 <= i <= 9:
             for k in range(4):
                 faces[k, i - 3] = ws[k] * inv
             faces[4, i - 3] = jnp.where(lane > 0, ws[4] * inv, 0.0)
@@ -100,7 +99,7 @@
 
 def krylov(group, lap_own, lap_of, j_of, shared, outs, scratch, total):
     dinv, diag, faces = shared
-    first, second, third = outs
+    keep, give = outs
     prod, v0, v1, v2 = scratch
     ny, nz = diag.shape[-2:]
     lane = lax.broadcasted_iota(jnp.int32, (8, nz), 1)
@@ -108,11 +107,11 @@
     rows = range(0, ny, 8)
 
     for t, (a, _, _) in enumerate(group):
-        for i in range(1, 10):
+        for i in range(1, 12):
             for r in rows:
                 at = pl.ds(r, 8)
                 prod[t, i, pl.ds(PAD + r, 8)] = lap_own[a, i - 1, at] * lap_of[j_of[t], i - 1, at]
-    for i in range(2, 9):
+    for i in range(2, 11):
         for r in rows:
             scale = -dinv[i - 2, pl.ds(r, 8)]
             for t in range(len(group)):
@@ -128,7 +127,7 @@
             return out + 2.0 * lower, x
         return out + (lower + w[1] * ref[t, i + 1, pl.ds(at, 8)]), x
 
-    for src, dst, low, top in ((v0, v1, 3, 8), (v1, v2, 4, 7)):
+    for src, dst, low, top in ((v0, v1, 3, 10), (v1, v2, 4, 9)):
         for i in range(low, top):
             for r in rows:
                 w = [faces[k, i - 3, pl.ds(r, 8)] for k in range(6)]
@@ -136,16 +135,20 @@
                     dst[t, i, pl.ds(PAD + r, 8)] = image(src, t, i, r, w, False)[0]
 
     parts = [[jnp.zeros((8, nz), f32)] * MOMENTS for _ in group]
-    for i in (5, 6):
+    core, _ = position()
+    for n in range(OWN):
+        half, slab = n // 2, n % 2
+        out = keep if half == 0 else give
+        i = 5 + 2 * (core if half == 0 else 1 - core) + slab
         for r in rows:
             w = [faces[k, i - 3, pl.ds(r, 8)] for k in range(6)]
             d = diag[i - 5, pl.ds(r, 8)]
             for t, (_, f, _) in enumerate(group):
                 ring, x2 = image(v2, t, i, r, w, True)
                 x0, x1 = v0[t, i, pl.ds(PAD + r, 8)], v1[t, i, pl.ds(PAD + r, 8)]
-                first[f, i - 5, pl.ds(r, 8)] = x0
-                second[f, i - 5, pl.ds(r, 8)] = x1
-                third[f, i - 5, pl.ds(r, 8)] = x2
+                out[0, f, slab, pl.ds(r, 8)] = x0
+                out[1, f, slab, pl.ds(r, 8)] = x1
+                out[2, f, slab, pl.ds(r, 8)] = x2
                 d0, d1, d2 = d * x0, d * x1, d * x2
                 pairs = (d0 * x0, d1 * x0, d1 * x1, d2 * x1, d2 * x2, d2 * ring)
                 parts[t] = [p + q for p, q in zip(parts[t], pairs)]
@@ -162,7 +165,7 @@
     lane = lax.broadcasted_iota(jnp.int32, (8, nz), 1)
 
     def one(m, carry):
-        for i in range(1, 10):
+        for i in range(1, 12):
             for r in range(0, ny, 8):
                 lap[m, i - 1, pl.ds(r, 8)] = laplace_at(wide, (m,), i, r, lane)
         return carry
@@ -182,71 +185,71 @@
     raw[blocks] = (regions[...] + 1).astype(raw.dtype)
 
 
-def own_kernel(plan, stiff, cubic, mine, other, far, far_other, edge,
-               first, second, third, lap_own, dinv, diag, faces, moments,
+def own_kernel(plan, stiff, cubic, mine, other, more, more_other,
+               keep, give, lap_own, dinv, diag, faces, moments,
                wide, gain, lap, prod, v0, v1, v2):
     blocks, nz = lap.shape[0], lap.shape[-1]
-    core, high, origin = position()
+    core, high = position()
     scratch = (prod, v0, v1, v2)
     clear_fields(scratch)
     clear_window(wide)
-    stacks = blocks + 1
-    for ref, more, q in ((mine, far, core), (other, far_other, 1 - core)):
+    here, there, beyond, edge = spots(high)
+    for ref, rest, q in ((mine, more, core), (other, more_other, 1 - core)):
         for i in range(2):
-            place(wide, origin, 0, ref, i, 5 + 4 * high + 2 * q + i, 0, stacks)
-            place(wide, origin, 0, more, i, 5 + 4 * (1 - high) + 2 * q + i, 0, stacks)
-            place(wide, origin, 0, more, 2 + i, 1 + 12 * high + 2 * q + i, 0, stacks)
-    place(wide, origin, 0, edge, 0, 4 * high, 0, stacks)
+            place(wide, ref, i, here + 2 * q + i)
+            place(wide, rest, i, there + 2 * q + i)
+            place(wide, rest, 2 + i, beyond + 2 * q + i)
+
+        @pl.when(q == 0)
+        def _():
+            place(wide, rest, 4, edge)
+
     material(wide, blocks, stiff, cubic, gain, dinv, diag, faces)
     laps(wide, lap, blocks)
 
     def scaled(m, carry):
-        for i in range(9):
+        for i in range(gain.shape[0]):
             lap_own[m, i] = gain[i] * lap[m, i]
         return carry
 
     lax.fori_loop(0, blocks, scaled, 0)
-
-    def step(h, total):
-        group = [(h * GROUP + t, h * GROUP + t, (h * GROUP + t) * PARTNERS) for t in range(GROUP)]
-        j_of = [plan[g[0], 0] for g in group]
-        return krylov(group, lap_own, lap, j_of, (dinv, diag, faces), (first, second, third), scratch, total)
-
-    moments[...] = lax.fori_loop(0, blocks // GROUP, step, jnp.zeros((8, nz), f32))
-
-
-def partner_kernel(plan, mine, other, lap_own, dinv, diag, faces, moments,
-                   first, second, third, sums,
+    group = [(GROUP * core + t, t, (GROUP * core + t) * PARTNERS) for t in range(GROUP)]
+    j_of = [plan[g[0], 0] for g in group]
+    moments[...] = krylov(
+        group, lap_own, lap, j_of, (dinv, diag, faces), (keep, give), scratch, jnp.zeros((8, nz), f32)
+    )
+
+
+def partner_kernel(plan, near, far, along, edge, lap_own, dinv, diag, faces, moments, keep_own, give_own,
+                   keep, give, sums,
                    wide, lap, prod, v0, v1, v2):
-    blocks = mine.shape[0]
-    core, high, origin = position()
+    blocks = near.shape[0]
+    core, high = position()
     scratch = (prod, v0, v1, v2)
     clear_fields(scratch)
     clear_window(wide)
-    for ref, q in ((mine, core), (other, 1 - core)):
-        to = q * blocks
-        for k in range(4):
-            slab = 2 * q + k if k < 2 else 2 * (1 - q) + k - 2
-            place(wide, origin, to, ref, k, 5 + 4 * high + slab, 0, blocks)
-            place(wide, origin, to, ref, 4 + k, 5 + 4 * (1 - high) + slab, 0, blocks)
-            place(wide, origin, to, ref, 8 + k, 1 + 12 * high + slab, 0, blocks)
-        place(wide, origin, to, ref, 12, 4 * high, 0, blocks)
-    laps(wide, lap, lap.shape[0])
-    per = blocks // GROUP
+    for ref, first in zip((near, far, along), spots(high)):
+        for k in range(OWN):
+            place(wide, ref, k, first + (2 * core + k if k < 2 else 2 * (1 - core) + k - 2))
+    place(wide, edge, 0, 0)
+    for k in range(3):
+        keep[k, pl.ds(0, GROUP)] = keep_own[k]
+        give[k, pl.ds(0, GROUP)] = give_own[k]
+    laps(wide, lap, blocks)
+    s = 1 + core
 
     def step(h, total):
-        s = 1 + h // per
-        b = (h - (s - 1) * per) * GROUP
-        group = [(b + t, (s - 1) * blocks + b + t, (b + t) * PARTNERS + s) for t in range(GROUP)]
-        j_of = [(s - 1) * blocks + plan[g[0], s] for g in group]
-        return krylov(group, lap_own, lap, j_of, (dinv, diag, faces), (first, second, third), scratch, total)
-
-    total = lax.fori_loop(0, (PARTNERS - 1) * per, step, moments[...])
+        b = h * GROUP
+        group = [(b + t, GROUP + b + t, (b + t) * PARTNERS + s) for t in range(GROUP)]
+        j_of = [plan[g[0], s] for g in group]
+        return krylov(group, lap_own, lap, j_of, (dinv, diag, faces), (keep, give), scratch, total)
+
+    total = lax.fori_loop(0, blocks // GROUP, step, moments[...])
     for d in range(sums.shape[0]):
         sums[d] = total
 
 
-def combine_kernel(sums, a0, a1, a2, b0, b1, b2, out):
+def combine_kernel(sums, keep, got, out):
     m = jnp.sum(sums[...], axis=0)
     mu = [m[k : k + 1] for k in range(MOMENTS)]
     ka = [mu[k] - mu[k + 1] for k in range(MOMENTS - 1)]
@@ -281,13 +284,13 @@
     def pick(c, f):
         return jnp.sum(jnp.where(lane == f, c, 0.0), axis=1, keepdims=True)
 
-    blocks = a0.shape[0]
-    for f in range(out.shape[0]):
-        a, s = f // PARTNERS, f % PARTNERS
-        basis, at = ((a0, a1, a2), a) if s == 0 else ((b0, b1, b2), (s - 1) * blocks + a)
-        c0, c1, c2 = (pick(c, f) for c in x)
-        for i in range(out.shape[1]):
-            out[f, i] = c0 * basis[0][at, i] + c1 * basis[1][at, i] + c2 * basis[2][at, i]
+    core, _ = position()
+    for basis, q in ((keep, core), (got, 1 - core)):
+        for n in range(basis.shape[1]):
+            f = (GROUP * q + n) * PARTNERS if n < GROUP else (n - GROUP) * PARTNERS + 1 + q
+            c0, c1, c2 = (pick(c, f) for c in x)
+            for i in range(out.shape[1]):
+                out[f, i] = c0 * basis[0, n, i] + c1 * basis[1, n, i] + c2 * basis[2, n, i]
 
 
 def shards(modes, regions, stiffness, nonlinear, plan):
@@ -335,66 +338,66 @@
     near = send(four, lambda m, y, h, c: (m + 1 + c, y, h, c))
     edge0 = send(raw[:, 1:], lambda m, y, h, c: (m, y + 1, h, 0) if c == 1 else None)
     far0_along = send(far0, along)
-    more = jnp.concatenate([far0, far0_along], 1)
+    more = jnp.concatenate([far0, far0_along, edge0], 1)
     more_other = send(more, partner_core)
 
     field_scratch = [pltpu.VMEM((GROUP, WINDOW) + padded, f32) for _ in range(4)]
-    vectors = [array(per_block, slabs, *slab)] * 3
-    a0, a1, a2, lap_own, dinv, diag, faces, moments = pl.pallas_call(
+    basis = array(3, GROUP, slabs, *slab)
+    keep_own, give_own, lap_own, dinv, diag, faces, moments = pl.pallas_call(
         own_kernel,
         out_shape=(
-            *vectors,
-            array(per_block, 9, *slab),
-            array(7, *slab),
-            array(slabs, *slab),
-            array(6, 5, *slab),
+            basis,
+            basis,
+            array(per_block, WINDOW - 2, *slab),
+            array(WINDOW - 4, *slab),
+            array(OWN, *slab),
+            array(6, WINDOW - 6, *slab),
             array(8, nz),
         ),
-        in_specs=[sm] * 3 + [vm] * 5,
-        out_specs=(vm,) * 8,
+        in_specs=[sm] * 3 + [vm] * 4,
+        out_specs=(vm,) * 7,
         scratch_shapes=[
             pltpu.VMEM((per_block + 1, WINDOW) + padded, f32),
-            pltpu.VMEM((9,) + slab, f32),
-            pltpu.VMEM((per_block, 9) + slab, f32),
+            pltpu.VMEM((WINDOW - 2,) + slab, f32),
+            pltpu.VMEM((per_block, WINDOW - 2) + slab, f32),
             *field_scratch,
         ],
         compiler_params=pltpu.CompilerParams(vmem_limit_bytes=24 << 20),
         cost_estimate=pl.CostEstimate(flops=20_000_000, bytes_accessed=8 << 20, transcendentals=0),
         name="own",
-    )(plan, stiffness, nonlinear, raw, raw_other, more, more_other, edge0)
+    )(plan, stiffness, nonlinear, raw, raw_other, more, more_other)
 
     far_along = send(far, along)
     last = lax.dynamic_slice_in_dim(near, 3 - 2 * odd, 1, 1, allow_negative_indices=False)
     edge = send(last, lambda m, y, h, c: (m, y + 1, h, c))
-    mine = jnp.concatenate([near, far, far_along, edge], 1)
-    other = send(mine, partner_core)
-
-    rest = per_block * (PARTNERS - 1)
-    b0, b1, b2, sums = pl.pallas_call(
+
+    basis = array(3, GROUP + per_block, slabs, *slab)
+    keep, give, sums = pl.pallas_call(
         partner_kernel,
-        out_shape=(*([array(rest, slabs, *slab)] * 3), array(n_space, 8, nz)),
-        in_specs=[sm] + [vm] * 7,
-        out_specs=(vm,) * 4,
+        out_shape=(basis, basis, array(n_space, 8, nz)),
+        in_specs=[sm] + [vm] * 11,
+        out_specs=(vm,) * 3,
         scratch_shapes=[
-            pltpu.VMEM((rest, WINDOW) + padded, f32),
-            pltpu.VMEM((rest, 9) + slab, f32),
+            pltpu.VMEM((per_block, WINDOW) + padded, f32),
+            pltpu.VMEM((per_block, WINDOW - 2) + slab, f32),
             *field_scratch,
         ],
         compiler_params=pltpu.CompilerParams(vmem_limit_bytes=24 << 20),
         cost_estimate=pl.CostEstimate(flops=40_000_000, bytes_accessed=16 << 20, transcendentals=0),
         name="partner",
-    )(plan, mine, other, lap_own, dinv, diag, faces, moments)
-
+    )(plan, near, far, far_along, edge, lap_own, dinv, diag, faces, moments, keep_own, give_own)
+
+    got = send(give, partner_core)
     gathered = lax.all_to_all(sums, "space", 0, 0)
 
     out = pl.pallas_call(
         combine_kernel,
         out_shape=array(fields, slabs, *slab),
-        in_specs=[vm] * 7,
+        in_specs=[vm] * 3,
         out_specs=vm,
         compiler_params=pltpu.CompilerParams(vmem_limit_bytes=16 << 20),
         name="combine",
-    )(gathered, a0, a1, a2, b0, b1, b2)
+    )(gathered, keep, got)
     return out.reshape((per_block, PARTNERS, slabs, ny, nz))
 
 

time: 113 us -> 89 us (0.79)
  waiting for transfers between devices: 30.4 us -> 5.94 us
  starting transfers between devices: 43.3 us -> 48 us
  blocking collectives: 24.8 us -> 22.1 us
  Pallas kernels: 12 us -> 10.3 us
    ppermute x10, waiting for transfers between devices: 30.4 us -> 5.94 us  [send(): return lax.ppermute(x, ('mode', 'space'), pairs)]
    ppermute x10, starting transfers between devices: 43.3 us -> 48 us  [send(): return lax.ppermute(x, ('mode', 'space'), pairs)]
    all_to_all x1, blocking collectives: 24.8 us -> 22.1 us  [shards(): gathered = lax.all_to_all(sums, 'space', 0, 0)]
    pallas_call x2, Pallas kernels: 10.7 us -> 9.11 us  [the longest x1 4.8 us: shards(): pl.pallas_call(partner_kernel, out_shape=(basis, basis, array(n_space, 8,...]
  transfers between devices with their start and end apart: 10 -> 10, of which waited for: 7 -> 2; matrix products, arithmetic and copies ran while one was open for 0% -> 0% of each run, Pallas kernels for 4% -> 5%
where the time goes in v3:
time: 89 us; the launch traced here: 88.5 us
  starting transfers between devices  48 us (54%)
  blocking collectives  22.1 us (25%)
  Pallas kernels  10.3 us (12%)
  waiting for transfers between devices  5.94 us (7%)
  local copies, waits for them, and re-layouts  1.84 us (2%)
    ppermute x10, starting transfers between devices, send(): return lax.ppermute(x, ('mode', 'space'), pairs)  48 us
    all_to_all x1, blocking collectives, shards(): gathered = lax.all_to_all(sums, 'space', 0, 0)  22.1 us
    ppermute x10, waiting for transfers between devices, send(): return lax.ppermute(x, ('mode', 'space'), pairs)  5.94 us
    pallas_call x1, Pallas kernels, shards(): pl.pallas_call(partner_kernel, out_shape=(basis, basis, array(n_space, 8,...  4.8 us
    pallas_call x1, Pallas kernels, shards(): pl.pallas_call(own_kernel, out_shape=(basis, basis, array(per_block, WIND...  4.31 us
    unnamed x12, local copies, waits for them, and re-layouts  1.79 us
  transfers between devices with their start and end apart: 10, of which 2 were waited for; matrix products, arithmetic and copies ran while one was open for 0% of the time, Pallas kernels for 5%

profile of v3, /device:TPU:1, one launch (start us, length us, event | category | flops | bytes accessed | tf_op | source)
XLA Modules:
  0.0 88.5 jit_solution(3524998480184839796)
XLA Ops:
  0.0 0.9 %copy-done = bf16[4,2,64,128]{3,2,1,0:T(8,128)(2,1)S(1)} copy-done((bf16[4,2,64,128]{3,2,1,0:T(8,128)(2,1)S(1)}, bf16[4,2,64,128]{3,2,1,0:T(8,128)(2,1)}, u32[]{:S(2)}) %copy-start) | copy-done | bytes 131096
  0.9 0.8 copy-done.1
  1.8 11.6 %collective-permute-start.5 = (bf16[5,2,64,128]{3,2,1,0:T(8,128)(2,1)S(1)}, bf16[5,2,64,128]{3,2,1,0:T(8,128)(2,1)S(1)}, u32[]{:S(2)}, u32[]{:S(2)}) collective-permute-start(bf16[5,2,64,128]{3,2,1,0:T(8,128)(2,1)S(1)} %pack.1.mine), channel_id=1, source_target_pairs={{0,2},{1,3},{2,0},{3,1},{4,6},{5,7},{6,4},{7,5},{8,10},{9,11},{10,... | collective-permute-start | bytes 491528 | tf_op jit(solution)/shard_map/ppermute | solution.py:309
  13.4 2.9 %collective-permute-start = (bf16[5,2,64,128]{3,2,1,0:T(8,128)(2,1)S(1)}, bf16[5,2,64,128]{3,2,1,0:T(8,128)(2,1)S(1)}, u32[]{:S(2)}, u32[]{:S(2)}) collective-permute-start(bf16[5,2,64,128]{3,2,1,0:T(8,128)(2,1)S(1)} %pack.1.mine), channel_id=1, source_target_pairs={{0,1},{1,0},{2,3},{3,2},{4,5},{5,4},{6,7},{7,6},{8,9},{9,8},{10,11... | collective-permute-start | bytes 491528 | tf_op jit(solution)/shard_map/ppermute | solution.py:309
  16.3 3.1 %collective-permute-start.7 = (bf16[5,1,64,128]{3,2,1,0:T(8,128)(2,1)S(1)}, bf16[5,1,64,128]{3,2,1,0:T(8,128)(2,1)S(1)}, u32[]{:S(2)}, u32[]{:S(2)}) collective-permute-start(bf16[5,1,64,128]{3,2,1,0:T(8,128)(2,1)S(1)} %slice.14), channel_id=1, source_target_pairs={{1,4},{3,6},{5,8},{7,10},{9,12},{11,14},{13,16},{15,18},{17,20},{1... | collective-permute-start | bytes 245768 | tf_op jit(solution)/shard_map/ppermute | solution.py:309
  19.4 0.0 collective-permute-done.5
  19.4 3.2 %collective-permute-start.6 = (bf16[5,2,64,128]{3,2,1,0:T(8,128)(2,1)S(1)}, bf16[5,2,64,128]{3,2,1,0:T(8,128)(2,1)S(1)}, u32[]{:S(2)}, u32[]{:S(2)}) collective-permute-start(bf16[5,2,64,128]{3,2,1,0:T(8,128)(2,1)S(1)} %collective-permute-done.5), channel_id=1, source_target_pairs={{0,4},{1,5},{4,8},{5,9},{6,2},{7,3},{8,12},{9,13},{10,6},{11,7},{1... | collective-permute-start | bytes 491528 | tf_op jit(solution)/shard_map/ppermute | solution.py:309
  22.6 0.0 collective-permute-done.other
  22.7 7.3 %collective-permute-start.2 = (bf16[4,4,64,128]{3,2,1,0:T(8,128)(2,1)S(1)}, bf16[4,4,64,128]{3,2,1,0:T(8,128)(2,1)S(1)}, u32[]{:S(2)}, u32[]{:S(2)}) collective-permute-start(bf16[4,4,64,128]{3,2,1,0:T(8,128)(2,1)S(1)} %pad_maximum_fusion), channel_id=1, source_target_pairs={{0,34},{1,67},{2,32},{3,65},{4,38},{5,71},{6,36},{7,69},{8,42},{9,... | collective-permute-start | bytes 786440 | tf_op jit(solution)/shard_map/ppermute | solution.py:309
  30.0 1.9 %collective-permute-start.1 = (bf16[4,4,64,128]{3,2,1,0:T(8,128)(2,1)S(1)}, bf16[4,4,64,128]{3,2,1,0:T(8,128)(2,1)S(1)}, u32[]{:S(2)}, u32[]{:S(2)}) collective-permute-start(bf16[4,4,64,128]{3,2,1,0:T(8,128)(2,1)S(1)} %pad_maximum_fusion), channel_id=1, source_target_pairs={{0,32},{1,65},{2,34},{3,67},{4,36},{5,69},{6,38},{7,71},{8,40},{9,... | collective-permute-start | bytes 786440 | tf_op jit(solution)/shard_map/ppermute | solution.py:309
  31.9 0.0 collective-permute-done.6
  32.0 0.0 collective-permute-done.7
  32.0 4.1 %collective-permute-start.8 = (bf16[5,5,64,128]{3,2,1,0:T(8,128)(2,1)S(1)}, bf16[5,5,64,128]{3,2,1,0:T(8,128)(2,1)S(1)}, u32[]{:S(2)}, u32[]{:S(2)}) collective-permute-start(bf16[5,5,64,128]{3,2,1,0:T(8,128)(2,1)S(1)} %constant_dynamic-update-slice_fusion.more), channel_id=1, source_target_pairs={{0,1},{1,0},{2,3},{3,2},{4,5},{5,4},{6,7},{7,6},{8,9},{9,8},{10,11... | collective-permute-start | bytes 1228808 | tf_op jit(solution)/shard_map/ppermute | solution.py:309
  36.2 4.6 %collective-permute-done.2.far = bf16[4,4,64,128]{3,2,1,0:T(8,128)(2,1)S(1)} collective-permute-done((bf16[4,4,64,128]{3,2,1,0:T(8,128)(2,1)S(1)}, bf16[4,4,64,128]{3,2,1,0:T(8,128)(2,1)S(1)}, u32[]{:S(2)}, u32[]{:S(2)}) %collective-permute-start.2) | collective-permute-done | bytes 262176 | tf_op jit(solution)/shard_map/ppermute | solution.py:309
  40.8 3.6 %collective-permute-start.3 = (bf16[4,4,64,128]{3,2,1,0:T(8,128)(2,1)S(1)}, bf16[4,4,64,128]{3,2,1,0:T(8,128)(2,1)S(1)}, u32[]{:S(2)}, u32[]{:S(2)}) collective-permute-start(bf16[4,4,64,128]{3,2,1,0:T(8,128)(2,1)S(1)} %collective-permute-done.2.far), channel_id=1, source_target_pairs={{0,4},{1,5},{4,8},{5,9},{6,2},{7,3},{8,12},{9,13},{10,6},{11,7},{1... | collective-permute-start | bytes 786440 | tf_op jit(solution)/shard_map/ppermute | solution.py:309
  44.4 1.3 %collective-permute-done.1.near = bf16[4,4,64,128]{3,2,1,0:T(8,128)(2,1)S(1)} collective-permute-done((bf16[4,4,64,128]{3,2,1,0:T(8,128)(2,1)S(1)}, bf16[4,4,64,128]{3,2,1,0:T(8,128)(2,1)S(1)}, u32[]{:S(2)}, u32[]{:S(2)}) %collective-permute-start.1) | collective-permute-done | bytes 262176 | tf_op jit(solution)/shard_map/ppermute | solution.py:309
  45.7 5.3 %collective-permute-start.4 = (bf16[4,1,64,128]{3,2,1,0:T(8,128)(2,1)S(1)}, bf16[4,1,64,128]{3,2,1,0:T(8,128)(2,1)S(1)}, u32[]{:S(2)}, u32[]{:S(2)}) collective-permute-start(bf16[4,1,64,128]{3,2,1,0:T(8,128)(2,1)S(1)} %constant_dynamic-slice_fusion), channel_id=1, source_target_pairs={{0,4},{1,5},{2,6},{3,7},{4,8},{5,9},{6,10},{7,11},{8,12},{9,13},{1... | collective-permute-start | bytes 196616 | tf_op jit(solution)/shard_map/ppermute | solution.py:309
  51.0 0.0 collective-permute-done.8.more_other
  51.0 4.3 %own.1 = (f32[3,2,2,64,128]{4,3,2,1,0:T(8,128)S(1)}, f32[3,2,2,64,128]{4,3,2,1,0:T(8,128)S(1)}, f32[4,11,64,128]{3,2,1,0:T(8,128)S(1)}, f32[9,64,128]{2,1,0:T(8,...) custom-call(s32[4,3]{1,0:T(4,128)S(1)} %copy-done.2, f32[8]{0:T(128)S(1)} %copy-done.3, ...), custom_call_target="tpu_custom_call" | custom-call | flops 20000000 | bytes 8388608 | tf_op jit(solution)/shard_map/own/pallas_call | solution.py:346
  55.4 0.0 collective-permute-done.4.edge
  55.4 4.8 %partner.1 = (f32[3,6,2,64,128]{4,3,2,1,0:T(8,128)S(1)}, f32[3,6,2,64,128]{4,3,2,1,0:T(8,128)S(1)}, f32[32,8,128]{2,1,0:T(8,128)S(1)}) custom-call(s32[4,3]{1,0:T(4,128)S(1)} %copy-done.2, bf16[4,4,64,128]{3,2,1,0:T(8,128)(2,1)S(1)} %collective-permute-done.1.near, bf16[4,4,64,128]{3,2,1,0:T(8,128)(2,1)S(1)} %collective-permute-done.2.far, ...), custom_call_target="tpu_custom_call" | custom-call | flops 40000000 | bytes 16777216 | tf_op jit(solution)/shard_map/partner/pallas_call | solution.py:375
  60.2 5.0 %collective-permute-start.9 = (f32[3,6,2,64,128]{4,3,2,1,0:T(8,128)S(1)}, f32[3,6,2,64,128]{4,3,2,1,0:T(8,128)S(1)}, u32[]{:S(2)}, u32[]{:S(2)}) collective-permute-start(f32[3,6,2,64,128]{4,3,2,1,0:T(8,128)S(1)} %get-tuple-element.24), channel_id=1, source_target_pairs={{0,1},{1,0},{2,3},{3,2},{4,5},{5,4},{6,7},{7,6},{8,9},{9,8},{10,11... | collective-permute-start | bytes 3538952 | tf_op jit(solution)/shard_map/ppermute | solution.py:309
  65.2 22.1 %all_to_all.5.sums = f32[32,8,128]{2,1,0:T(8,128)S(1)} all-to-all(f32[32,8,128]{2,1,0:T(8,128)S(1)} %get-tuple-element.22), channel_id=1, replica_groups=mesh['mode'=16,'space'=32] {'space'}, dimensions={0} | all-to-all | bytes 262144 | tf_op jit(solution)/shard_map/all_to_all | solution.py:391
  87.3 1.2 %combine.1 = f32[12,2,64,128]{3,2,1,0:T(8,128)} custom-call(f32[32,8,128]{2,1,0:T(8,128)S(1)} %all_to_all.5.sums, f32[3,6,2,64,128]{4,3,2,1,0:T(8,128)S(1)} %get-tuple-element.23.keep, f32[3,6,2,64,128]{4,3,2,1,0:T(8,128)S(1)} %collective-permute-done.9.got), custom_call_target="tpu_custom_call" | custom-call | tf_op jit(solution)/shard_map/combine/pallas_call | solution.py:393
  (19 shorter events, 0.1 us)
Async XLA Ops:
  0.0 0.9 %copy-start = (bf16[4,2,64,128]{3,2,1,0:T(8,128)(2,1)S(1)}, bf16[4,2,64,128]{3,2,1,0:T(8,128)(2,1)}, u32[]{:S(2)}) copy-start(bf16[4,2,64,128]{3,2,1,0:T(8,128)(2,1)} %modes.1) | copy-start | bytes 393220
  0.9 0.8 copy-start.1
  1.7 49.3 %copy-start.2 = (s32[4,3]{1,0:T(4,128)S(1)}, s32[4,3]{1,0:T(4,128)}, u32[]{:S(2)}) copy-start(s32[4,3]{1,0:T(4,128)} %plan.3) | copy-start | bytes 148
  1.7 49.3 %copy-start.3 = (f32[8]{0:T(128)S(1)}, f32[8]{0:T(128)}, u32[]{:S(2)}) copy-start(f32[8]{0:T(128)} %stiff.1) | copy-start | bytes 100
  1.7 49.3 %copy-start.4 = (f32[8]{0:T(128)S(1)}, f32[8]{0:T(128)}, u32[]{:S(2)}) copy-start(f32[8]{0:T(128)} %cubic.1) | copy-start | bytes 100
  1.8 17.6 %collective-permute-start.5 = (bf16[5,2,64,128]{3,2,1,0:T(8,128)(2,1)S(1)}, bf16[5,2,64,128]{3,2,1,0:T(8,128)(2,1)S(1)}, u32[]{:S(2)}, u32[]{:S(2)}) collective-permute-start(bf16[5,2,64,128]{3,2,1,0:T(8,128)(2,1)S(1)} %pack.1.mine), channel_id=1, source_target_pairs={{0,2},{1,3},{2,0},{3,1},{4,6},{5,7},{6,4},{7,5},{8,10},{9,11},{10,... | collective-permute-start | bytes 491528 | tf_op jit(solution)/shard_map/ppermute | solution.py:309
  13.4 9.2 %collective-permute-start = (bf16[5,2,64,128]{3,2,1,0:T(8,128)(2,1)S(1)}, bf16[5,2,64,128]{3,2,1,0:T(8,128)(2,1)S(1)}, u32[]{:S(2)}, u32[]{:S(2)}) collective-permute-start(bf16[5,2,64,128]{3,2,1,0:T(8,128)(2,1)S(1)} %pack.1.mine), channel_id=1, source_target_pairs={{0,1},{1,0},{2,3},{3,2},{4,5},{5,4},{6,7},{7,6},{8,9},{9,8},{10,11... | collective-permute-start | bytes 491528 | tf_op jit(solution)/shard_map/ppermute | solution.py:309
  16.3 15.7 %collective-permute-start.7 = (bf16[5,1,64,128]{3,2,1,0:T(8,128)(2,1)S(1)}, bf16[5,1,64,128]{3,2,1,0:T(8,128)(2,1)S(1)}, u32[]{:S(2)}, u32[]{:S(2)}) collective-permute-start(bf16[5,1,64,128]{3,2,1,0:T(8,128)(2,1)S(1)} %slice.14), channel_id=1, source_target_pairs={{1,4},{3,6},{5,8},{7,10},{9,12},{11,14},{13,16},{15,18},{17,20},{1... | collective-permute-start | bytes 245768 | tf_op jit(solution)/shard_map/ppermute | solution.py:309
  19.4 12.6 %collective-permute-start.6 = (bf16[5,2,64,128]{3,2,1,0:T(8,128)(2,1)S(1)}, bf16[5,2,64,128]{3,2,1,0:T(8,128)(2,1)S(1)}, u32[]{:S(2)}, u32[]{:S(2)}) collective-permute-start(bf16[5,2,64,128]{3,2,1,0:T(8,128)(2,1)S(1)} %collective-permute-done.5), channel_id=1, source_target_pairs={{0,4},{1,5},{4,8},{5,9},{6,2},{7,3},{8,12},{9,13},{10,6},{11,7},{1... | collective-permute-start | bytes 491528 | tf_op jit(solution)/shard_map/ppermute | solution.py:309
  22.7 18.1 %collective-permute-start.2 = (bf16[4,4,64,128]{3,2,1,0:T(8,128)(2,1)S(1)}, bf16[4,4,64,128]{3,2,1,0:T(8,128)(2,1)S(1)}, u32[]{:S(2)}, u32[]{:S(2)}) collective-permute-start(bf16[4,4,64,128]{3,2,1,0:T(8,128)(2,1)S(1)} %pad_maximum_fusion), channel_id=1, source_target_pairs={{0,34},{1,67},{2,32},{3,65},{4,38},{5,71},{6,36},{7,69},{8,42},{9,... | collective-permute-start | bytes 786440 | tf_op jit(solution)/shard_map/ppermute | solution.py:309
  30.0 15.7 %collective-permute-start.1 = (bf16[4,4,64,128]{3,2,1,0:T(8,128)(2,1)S(1)}, bf16[4,4,64,128]{3,2,1,0:T(8,128)(2,1)S(1)}, u32[]{:S(2)}, u32[]{:S(2)}) collective-permute-start(bf16[4,4,64,128]{3,2,1,0:T(8,128)(2,1)S(1)} %pad_maximum_fusion), channel_id=1, source_target_pairs={{0,32},{1,65},{2,34},{3,67},{4,36},{5,69},{6,38},{7,71},{8,40},{9,... | collective-permute-start | bytes 786440 | tf_op jit(solution)/shard_map/ppermute | solution.py:309
  32.0 19.0 %collective-permute-start.8 = (bf16[5,5,64,128]{3,2,1,0:T(8,128)(2,1)S(1)}, bf16[5,5,64,128]{3,2,1,0:T(8,128)(2,1)S(1)}, u32[]{:S(2)}, u32[]{:S(2)}) collective-permute-start(bf16[5,5,64,128]{3,2,1,0:T(8,128)(2,1)S(1)} %constant_dynamic-update-slice_fusion.more), channel_id=1, source_target_pairs={{0,1},{1,0},{2,3},{3,2},{4,5},{5,4},{6,7},{7,6},{8,9},{9,8},{10,11... | collective-permute-start | bytes 1228808 | tf_op jit(solution)/shard_map/ppermute | solution.py:309
  40.8 14.6 %collective-permute-start.3 = (bf16[4,4,64,128]{3,2,1,0:T(8,128)(2,1)S(1)}, bf16[4,4,64,128]{3,2,1,0:T(8,128)(2,1)S(1)}, u32[]{:S(2)}, u32[]{:S(2)}) collective-permute-start(bf16[4,4,64,128]{3,2,1,0:T(8,128)(2,1)S(1)} %collective-permute-done.2.far), channel_id=1, source_target_pairs={{0,4},{1,5},{4,8},{5,9},{6,2},{7,3},{8,12},{9,13},{10,6},{11,7},{1... | collective-permute-start | bytes 786440 | tf_op jit(solution)/shard_map/ppermute | solution.py:309
  45.7 9.7 %collective-permute-start.4 = (bf16[4,1,64,128]{3,2,1,0:T(8,128)(2,1)S(1)}, bf16[4,1,64,128]{3,2,1,0:T(8,128)(2,1)S(1)}, u32[]{:S(2)}, u32[]{:S(2)}) collective-permute-start(bf16[4,1,64,128]{3,2,1,0:T(8,128)(2,1)S(1)} %constant_dynamic-slice_fusion), channel_id=1, source_target_pairs={{0,4},{1,5},{2,6},{3,7},{4,8},{5,9},{6,10},{7,11},{8,12},{9,13},{1... | collective-permute-start | bytes 196616 | tf_op jit(solution)/shard_map/ppermute | solution.py:309
  60.2 27.1 %collective-permute-start.9 = (f32[3,6,2,64,128]{4,3,2,1,0:T(8,128)S(1)}, f32[3,6,2,64,128]{4,3,2,1,0:T(8,128)S(1)}, u32[]{:S(2)}, u32[]{:S(2)}) collective-permute-start(f32[3,6,2,64,128]{4,3,2,1,0:T(8,128)S(1)} %get-tuple-element.24), channel_id=1, source_target_pairs={{0,1},{1,0},{2,3},{3,2},{4,5},{5,4},{6,7},{7,6},{8,9},{9,8},{10,11... | collective-permute-start | bytes 3538952 | tf_op jit(solution)/shard_map/ppermute | solution.py:309

commit v4 on v3

--- a/solution.py
+++ b/solution.py
@@ -38,10 +38,12 @@
     lax.fori_loop(0, wide.shape[0], clear, 0)
 
 
-def place(wide, ref, slot, at):
+def place(wide, exact, ref, slot, at):
     ny = ref.shape[2]
     for m in range(ref.shape[0]):
         wide[m, at, pl.ds(PAD, ny)] = ref[m, slot].astype(f32)
+    for m in range(exact.shape[0]):
+        exact[m, at] = ref[m, slot]
 
 
 def spots(high):
@@ -117,22 +119,25 @@
             for t in range(len(group)):
                 v0[t, i, pl.ds(PAD + r, 8)] = laplace_at(prod, (t,), i, r, lane) * scale
 
-    def image(ref, t, i, r, w, twice):
+    def image(ref, t, i, r, w):
         at = PAD + r
         x = ref[t, i, pl.ds(at, 8)]
         out = w[2] * ref[t, i, pl.ds(at - 1, 8)] + w[3] * ref[t, i, pl.ds(at + 1, 8)]
         out = out + (w[4] * pltpu.roll(x, 1, 1) + w[5] * pltpu.roll(x, nz - 1, 1))
-        lower = w[0] * ref[t, i - 1, pl.ds(at, 8)]
-        if twice:
-            return out + 2.0 * lower, x
-        return out + (lower + w[1] * ref[t, i + 1, pl.ds(at, 8)]), x
+        return out + (w[0] * ref[t, i - 1, pl.ds(at, 8)] + w[1] * ref[t, i + 1, pl.ds(at, 8)])
+
+    def lower(ref, t, i, r, w):
+        at = PAD + r
+        x = ref[t, i, pl.ds(at, 8)]
+        out = w[0] * ref[t, i - 1, pl.ds(at, 8)] + w[1] * ref[t, i, pl.ds(at - 1, 8)]
+        return 2.0 * (out + w[2] * pltpu.roll(x, 1, 1)), x
 
     for src, dst, low, top in ((v0, v1, 3, 10), (v1, v2, 4, 9)):
         for i in range(low, top):
             for r in rows:
                 w = [faces[k, i - 3, pl.ds(r, 8)] for k in range(6)]
                 for t in range(len(group)):
-                    dst[t, i, pl.ds(PAD + r, 8)] = image(src, t, i, r, w, False)[0]
+                    dst[t, i, pl.ds(PAD + r, 8)] = image(src, t, i, r, w)
 
     parts = [[jnp.zeros((8, nz), f32)] * MOMENTS for _ in group]
     core, _ = position()
@@ -141,10 +146,10 @@
         out = keep if half == 0 else give
         i = 5 + 2 * (core if half == 0 else 1 - core) + slab
         for r in rows:
-            w = [faces[k, i - 3, pl.ds(r, 8)] for k in range(6)]
+            w = [faces[k, i - 3, pl.ds(r, 8)] for k in (0, 2, 4)]
             d = diag[i - 5, pl.ds(r, 8)]
             for t, (_, f, _) in enumerate(group):
-                ring, x2 = image(v2, t, i, r, w, True)
+                ring, x2 = lower(v2, t, i, r, w)
                 x0, x1 = v0[t, i, pl.ds(PAD + r, 8)], v1[t, i, pl.ds(PAD + r, 8)]
                 out[0, f, slab, pl.ds(r, 8)] = x0
                 out[1, f, slab, pl.ds(r, 8)] = x1
@@ -160,14 +165,22 @@
     return total
 
 
-def laps(wide, lap, count):
-    ny, nz = lap.shape[-2:]
-    lane = lax.broadcasted_iota(jnp.int32, (8, nz), 1)
+def laps(wide, exact, lap):
+    count, places, ny, nz = lap.shape
+    r = lax.broadcasted_iota(jnp.int32, (nz, nz), 0)
+    c = lax.broadcasted_iota(jnp.int32, (nz, nz), 1)
+    beside = jnp.where(jnp.abs(r - c) == 1, -1.0, 0.0)
+    line = jnp.where(r == c, 6.0, beside).astype(exact.dtype)
 
     def one(m, carry):
-        for i in range(1, 12):
+        rows = exact[m, pl.ds(1, places)].reshape(places * ny, nz)
+        lap[m] = jnp.dot(rows, line, preferred_element_type=f32).reshape(places, ny, nz)
+        for i in range(1, places + 1):
             for r in range(0, ny, 8):
-                lap[m, i - 1, pl.ds(r, 8)] = laplace_at(wide, (m,), i, r, lane)
+                at = PAD + r
+                beside = wide[m, i, pl.ds(at - 1, 8)] + wide[m, i, pl.ds(at + 1, 8)]
+                slabs = wide[m, i - 1, pl.ds(at, 8)] + wide[m, i + 1, pl.ds(at, 8)]
+                lap[m, i - 1, pl.ds(r, 8)] = lap[m, i - 1, pl.ds(r, 8)] - (beside + slabs)
         return carry
 
     lax.fori_loop(0, count, one, 0)
@@ -179,15 +192,15 @@
             clear_rims(ref, (t,))
 
 
-def pack_kernel(modes, regions, raw):
+def pack_kernel(modes, labels, raw):
     blocks = modes.shape[0]
     raw[pl.ds(0, blocks)] = modes[...]
-    raw[blocks] = (regions[...] + 1).astype(raw.dtype)
+    raw[blocks] = labels[...]
 
 
 def own_kernel(plan, stiff, cubic, mine, other, more, more_other,
                keep, give, lap_own, dinv, diag, faces, moments,
-               wide, gain, lap, prod, v0, v1, v2):
+               wide, exact, gain, lap, prod, v0, v1, v2):
     blocks, nz = lap.shape[0], lap.shape[-1]
     core, high = position()
     scratch = (prod, v0, v1, v2)
@@ -196,16 +209,16 @@
     here, there, beyond, edge = spots(high)
     for ref, rest, q in ((mine, more, core), (other, more_other, 1 - core)):
         for i in range(2):
-            place(wide, ref, i, here + 2 * q + i)
-            place(wide, rest, i, there + 2 * q + i)
-            place(wide, rest, 2 + i, beyond + 2 * q + i)
+            place(wide, exact, ref, i, here + 2 * q + i)
+            place(wide, exact, rest, i, there + 2 * q + i)
+            place(wide, exact, rest, 2 + i, beyond + 2 * q + i)
 
         @pl.when(q == 0)
         def _():
-            place(wide, rest, 4, edge)
+            place(wide, exact, rest, 4, edge)
 
     material(wide, blocks, stiff, cubic, gain, dinv, diag, faces)
-    laps(wide, lap, blocks)
+    laps(wide, exact, lap)
 
     def scaled(m, carry):
         for i in range(gain.shape[0]):
@@ -222,7 +235,7 @@
 
 def partner_kernel(plan, near, far, along, edge, lap_own, dinv, diag, faces, moments, keep_own, give_own,
                    keep, give, sums,
-                   wide, lap, prod, v0, v1, v2):
+                   wide, exact, lap, prod, v0, v1, v2):
     blocks = near.shape[0]
     core, high = position()
     scratch = (prod, v0, v1, v2)
@@ -230,12 +243,12 @@
     clear_window(wide)
     for ref, first in zip((near, far, along), spots(high)):
         for k in range(OWN):
-            place(wide, ref, k, first + (2 * core + k if k < 2 else 2 * (1 - core) + k - 2))
-    place(wide, edge, 0, 0)
+            place(wide, exact, ref, k, first + (2 * core + k if k < 2 else 2 * (1 - core) + k - 2))
+    place(wide, exact, edge, 0, 0)
     for k in range(3):
         keep[k, pl.ds(0, GROUP)] = keep_own[k]
         give[k, pl.ds(0, GROUP)] = give_own[k]
-    laps(wide, lap, blocks)
+    laps(wide, exact, lap)
     s = 1 + core
 
     def step(h, total):
@@ -328,7 +341,7 @@
         out_specs=vm,
         compiler_params=pltpu.CompilerParams(vmem_limit_bytes=4 << 20),
         name="pack",
-    )(modes, regions)
+    )(modes, (regions + 1).astype(modes.dtype))
 
     odd = lax.axis_index("space") & 1
     raw_other = send(raw, partner_core)
@@ -358,6 +371,7 @@
         out_specs=(vm,) * 7,
         scratch_shapes=[
             pltpu.VMEM((per_block + 1, WINDOW) + padded, f32),
+            pltpu.VMEM((per_block, WINDOW) + slab, modes.dtype),
             pltpu.VMEM((WINDOW - 2,) + slab, f32),
             pltpu.VMEM((per_block, WINDOW - 2) + slab, f32),
             *field_scratch,
@@ -379,6 +393,7 @@
         out_specs=(vm,) * 3,
         scratch_shapes=[
             pltpu.VMEM((per_block, WINDOW) + padded, f32),
+            pltpu.VMEM((per_block, WINDOW) + slab, modes.dtype),
             pltpu.VMEM((per_block, WINDOW - 2) + slab, f32),
             *field_scratch,
         ],

time: 89 us -> 88.5 us (level)
    unnamed x12 -> x10, local copies, waits for them, and re-layouts: 1.79 us -> 0.95 us
where the time goes in v4:
time: 88.5 us; the launch traced here: 88.1 us
  starting transfers between devices  48 us (54%)
  blocking collectives  22.1 us (25%)
  Pallas kernels  9.87 us (11%)
  waiting for transfers between devices  5.94 us (7%)
  local copies, waits for them, and re-layouts  1 us (1%)
    ppermute x10, starting transfers between devices, send(): return lax.ppermute(x, ('mode', 'space'), pairs)  48 us
    all_to_all x1, blocking collectives, shards(): gathered = lax.all_to_all(sums, 'space', 0, 0)  22.1 us
    ppermute x10, waiting for transfers between devices, send(): return lax.ppermute(x, ('mode', 'space'), pairs)  5.94 us
    pallas_call x1, Pallas kernels, shards(): pl.pallas_call(partner_kernel, out_shape=(basis, basis, array(n_space, 8,...  4.56 us
    pallas_call x1, Pallas kernels, shards(): pl.pallas_call(own_kernel, out_shape=(basis, basis, array(per_block, WIND...  4.08 us
  transfers between devices with their start and end apart: 10, of which 2 were waited for; matrix products, arithmetic and copies ran while one was open for 0% of the time, Pallas kernels for 5%

profile of v4, /device:TPU:1, one launch (start us, length us, event | category | flops | bytes accessed | tf_op | source)
XLA Modules:
  0.0 88.1 jit_solution(3053182216807856244)
XLA Ops:
  0.0 0.8 add_convert_fusion.labels
  0.9 0.0 copy-start
  0.9 0.9 %copy-done = bf16[4,2,64,128]{3,2,1,0:T(8,128)(2,1)S(1)} copy-done((bf16[4,2,64,128]{3,2,1,0:T(8,128)(2,1)S(1)}, bf16[4,2,64,128]{3,2,1,0:T(8,128)(2,1)}, u32[]{:S(2)}) %copy-start) | copy-done | bytes 131096
  1.8 11.6 %collective-permute-start.5 = (bf16[5,2,64,128]{3,2,1,0:T(8,128)(2,1)S(1)}, bf16[5,2,64,128]{3,2,1,0:T(8,128)(2,1)S(1)}, u32[]{:S(2)}, u32[]{:S(2)}) collective-permute-start(bf16[5,2,64,128]{3,2,1,0:T(8,128)(2,1)S(1)} %pack.1.mine), channel_id=1, source_target_pairs={{0,2},{1,3},{2,0},{3,1},{4,6},{5,7},{6,4},{7,5},{8,10},{9,11},{10,... | collective-permute-start | bytes 491528 | tf_op jit(solution)/shard_map/ppermute | solution.py:322
  13.4 2.9 %collective-permute-start = (bf16[5,2,64,128]{3,2,1,0:T(8,128)(2,1)S(1)}, bf16[5,2,64,128]{3,2,1,0:T(8,128)(2,1)S(1)}, u32[]{:S(2)}, u32[]{:S(2)}) collective-permute-start(bf16[5,2,64,128]{3,2,1,0:T(8,128)(2,1)S(1)} %pack.1.mine), channel_id=1, source_target_pairs={{0,1},{1,0},{2,3},{3,2},{4,5},{5,4},{6,7},{7,6},{8,9},{9,8},{10,11... | collective-permute-start | bytes 491528 | tf_op jit(solution)/shard_map/ppermute | solution.py:322
  16.3 3.1 %collective-permute-start.7 = (bf16[5,1,64,128]{3,2,1,0:T(8,128)(2,1)S(1)}, bf16[5,1,64,128]{3,2,1,0:T(8,128)(2,1)S(1)}, u32[]{:S(2)}, u32[]{:S(2)}) collective-permute-start(bf16[5,1,64,128]{3,2,1,0:T(8,128)(2,1)S(1)} %slice.14), channel_id=1, source_target_pairs={{1,4},{3,6},{5,8},{7,10},{9,12},{11,14},{13,16},{15,18},{17,20},{1... | collective-permute-start | bytes 245768 | tf_op jit(solution)/shard_map/ppermute | solution.py:322
  19.4 0.0 collective-permute-done.5
  19.4 3.2 %collective-permute-start.6 = (bf16[5,2,64,128]{3,2,1,0:T(8,128)(2,1)S(1)}, bf16[5,2,64,128]{3,2,1,0:T(8,128)(2,1)S(1)}, u32[]{:S(2)}, u32[]{:S(2)}) collective-permute-start(bf16[5,2,64,128]{3,2,1,0:T(8,128)(2,1)S(1)} %collective-permute-done.5), channel_id=1, source_target_pairs={{0,4},{1,5},{4,8},{5,9},{6,2},{7,3},{8,12},{9,13},{10,6},{11,7},{1... | collective-permute-start | bytes 491528 | tf_op jit(solution)/shard_map/ppermute | solution.py:322
  22.6 0.0 collective-permute-done.other
  22.7 7.3 %collective-permute-start.2 = (bf16[4,4,64,128]{3,2,1,0:T(8,128)(2,1)S(1)}, bf16[4,4,64,128]{3,2,1,0:T(8,128)(2,1)S(1)}, u32[]{:S(2)}, u32[]{:S(2)}) collective-permute-start(bf16[4,4,64,128]{3,2,1,0:T(8,128)(2,1)S(1)} %pad_maximum_fusion), channel_id=1, source_target_pairs={{0,34},{1,67},{2,32},{3,65},{4,38},{5,71},{6,36},{7,69},{8,42},{9,... | collective-permute-start | bytes 786440 | tf_op jit(solution)/shard_map/ppermute | solution.py:322
  30.0 1.9 %collective-permute-start.1 = (bf16[4,4,64,128]{3,2,1,0:T(8,128)(2,1)S(1)}, bf16[4,4,64,128]{3,2,1,0:T(8,128)(2,1)S(1)}, u32[]{:S(2)}, u32[]{:S(2)}) collective-permute-start(bf16[4,4,64,128]{3,2,1,0:T(8,128)(2,1)S(1)} %pad_maximum_fusion), channel_id=1, source_target_pairs={{0,32},{1,65},{2,34},{3,67},{4,36},{5,69},{6,38},{7,71},{8,40},{9,... | collective-permute-start | bytes 786440 | tf_op jit(solution)/shard_map/ppermute | solution.py:322
  32.0 0.0 collective-permute-done.6
  32.0 0.0 collective-permute-done.7
  32.0 4.1 %collective-permute-start.8 = (bf16[5,5,64,128]{3,2,1,0:T(8,128)(2,1)S(1)}, bf16[5,5,64,128]{3,2,1,0:T(8,128)(2,1)S(1)}, u32[]{:S(2)}, u32[]{:S(2)}) collective-permute-start(bf16[5,5,64,128]{3,2,1,0:T(8,128)(2,1)S(1)} %constant_dynamic-update-slice_fusion.more), channel_id=1, source_target_pairs={{0,1},{1,0},{2,3},{3,2},{4,5},{5,4},{6,7},{7,6},{8,9},{9,8},{10,11... | collective-permute-start | bytes 1228808 | tf_op jit(solution)/shard_map/ppermute | solution.py:322
  36.2 4.6 %collective-permute-done.2.far = bf16[4,4,64,128]{3,2,1,0:T(8,128)(2,1)S(1)} collective-permute-done((bf16[4,4,64,128]{3,2,1,0:T(8,128)(2,1)S(1)}, bf16[4,4,64,128]{3,2,1,0:T(8,128)(2,1)S(1)}, u32[]{:S(2)}, u32[]{:S(2)}) %collective-permute-start.2) | collective-permute-done | bytes 262176 | tf_op jit(solution)/shard_map/ppermute | solution.py:322
  40.8 3.6 %collective-permute-start.3 = (bf16[4,4,64,128]{3,2,1,0:T(8,128)(2,1)S(1)}, bf16[4,4,64,128]{3,2,1,0:T(8,128)(2,1)S(1)}, u32[]{:S(2)}, u32[]{:S(2)}) collective-permute-start(bf16[4,4,64,128]{3,2,1,0:T(8,128)(2,1)S(1)} %collective-permute-done.2.far), channel_id=1, source_target_pairs={{0,4},{1,5},{4,8},{5,9},{6,2},{7,3},{8,12},{9,13},{10,6},{11,7},{1... | collective-permute-start | bytes 786440 | tf_op jit(solution)/shard_map/ppermute | solution.py:322
  44.4 1.3 %collective-permute-done.1.near = bf16[4,4,64,128]{3,2,1,0:T(8,128)(2,1)S(1)} collective-permute-done((bf16[4,4,64,128]{3,2,1,0:T(8,128)(2,1)S(1)}, bf16[4,4,64,128]{3,2,1,0:T(8,128)(2,1)S(1)}, u32[]{:S(2)}, u32[]{:S(2)}) %collective-permute-start.1) | collective-permute-done | bytes 262176 | tf_op jit(solution)/shard_map/ppermute | solution.py:322
  45.7 5.3 %collective-permute-start.4 = (bf16[4,1,64,128]{3,2,1,0:T(8,128)(2,1)S(1)}, bf16[4,1,64,128]{3,2,1,0:T(8,128)(2,1)S(1)}, u32[]{:S(2)}, u32[]{:S(2)}) collective-permute-start(bf16[4,1,64,128]{3,2,1,0:T(8,128)(2,1)S(1)} %constant_dynamic-slice_fusion), channel_id=1, source_target_pairs={{0,4},{1,5},{2,6},{3,7},{4,8},{5,9},{6,10},{7,11},{8,12},{9,13},{1... | collective-permute-start | bytes 196616 | tf_op jit(solution)/shard_map/ppermute | solution.py:322
  51.1 4.1 %own.1 = (f32[3,2,2,64,128]{4,3,2,1,0:T(8,128)S(1)}, f32[3,2,2,64,128]{4,3,2,1,0:T(8,128)S(1)}, f32[4,11,64,128]{3,2,1,0:T(8,128)S(1)}, f32[9,64,128]{2,1,0:T(8,...) custom-call(s32[4,3]{1,0:T(4,128)S(1)} %copy-done.1, f32[8]{0:T(128)S(1)} %copy-done.2, ...), custom_call_target="tpu_custom_call" | custom-call | flops 20000000 | bytes 8388608 | tf_op jit(solution)/shard_map/own/pallas_call | solution.py:359
  55.1 4.6 %partner.1 = (f32[3,6,2,64,128]{4,3,2,1,0:T(8,128)S(1)}, f32[3,6,2,64,128]{4,3,2,1,0:T(8,128)S(1)}, f32[32,8,128]{2,1,0:T(8,128)S(1)}) custom-call(s32[4,3]{1,0:T(4,128)S(1)} %copy-done.1, bf16[4,4,64,128]{3,2,1,0:T(8,128)(2,1)S(1)} %collective-permute-done.1.near, bf16[4,4,64,128]{3,2,1,0:T(8,128)(2,1)S(1)} %collective-permute-done.2.far, ...), custom_call_target="tpu_custom_call" | custom-call | flops 40000000 | bytes 16777216 | tf_op jit(solution)/shard_map/partner/pallas_call | solution.py:389
  59.7 5.0 %collective-permute-start.9 = (f32[3,6,2,64,128]{4,3,2,1,0:T(8,128)S(1)}, f32[3,6,2,64,128]{4,3,2,1,0:T(8,128)S(1)}, u32[]{:S(2)}, u32[]{:S(2)}) collective-permute-start(f32[3,6,2,64,128]{4,3,2,1,0:T(8,128)S(1)} %get-tuple-element.24), channel_id=1, source_target_pairs={{0,1},{1,0},{2,3},{3,2},{4,5},{5,4},{6,7},{7,6},{8,9},{9,8},{10,11... | collective-permute-start | bytes 3538952 | tf_op jit(solution)/shard_map/ppermute | solution.py:322
  64.7 22.1 %all_to_all.5.sums = f32[32,8,128]{2,1,0:T(8,128)S(1)} all-to-all(f32[32,8,128]{2,1,0:T(8,128)S(1)} %get-tuple-element.22), channel_id=1, replica_groups=mesh['mode'=16,'space'=32] {'space'}, dimensions={0} | all-to-all | bytes 262144 | tf_op jit(solution)/shard_map/all_to_all | solution.py:406
  86.8 0.0 collective-permute-done.9.got
  86.8 1.2 %combine.1 = f32[12,2,64,128]{3,2,1,0:T(8,128)} custom-call(f32[32,8,128]{2,1,0:T(8,128)S(1)} %all_to_all.5.sums, f32[3,6,2,64,128]{4,3,2,1,0:T(8,128)S(1)} %get-tuple-element.23.keep, f32[3,6,2,64,128]{4,3,2,1,0:T(8,128)S(1)} %collective-permute-done.9.got), custom_call_target="tpu_custom_call" | custom-call | tf_op jit(solution)/shard_map/combine/pallas_call | solution.py:408
  (18 shorter events, 0.1 us)
Async XLA Ops:
  0.9 0.9 %copy-start = (bf16[4,2,64,128]{3,2,1,0:T(8,128)(2,1)S(1)}, bf16[4,2,64,128]{3,2,1,0:T(8,128)(2,1)}, u32[]{:S(2)}) copy-start(bf16[4,2,64,128]{3,2,1,0:T(8,128)(2,1)} %modes.1) | copy-start | bytes 393220
  1.8 49.3 %copy-start.1 = (s32[4,3]{1,0:T(4,128)S(1)}, s32[4,3]{1,0:T(4,128)}, u32[]{:S(2)}) copy-start(s32[4,3]{1,0:T(4,128)} %plan.3) | copy-start | bytes 148
  1.8 49.3 %copy-start.2 = (f32[8]{0:T(128)S(1)}, f32[8]{0:T(128)}, u32[]{:S(2)}) copy-start(f32[8]{0:T(128)} %stiff.1) | copy-start | bytes 100
  1.8 49.3 %copy-start.3 = (f32[8]{0:T(128)S(1)}, f32[8]{0:T(128)}, u32[]{:S(2)}) copy-start(f32[8]{0:T(128)} %cubic.1) | copy-start | bytes 100
  1.8 17.6 %collective-permute-start.5 = (bf16[5,2,64,128]{3,2,1,0:T(8,128)(2,1)S(1)}, bf16[5,2,64,128]{3,2,1,0:T(8,128)(2,1)S(1)}, u32[]{:S(2)}, u32[]{:S(2)}) collective-permute-start(bf16[5,2,64,128]{3,2,1,0:T(8,128)(2,1)S(1)} %pack.1.mine), channel_id=1, source_target_pairs={{0,2},{1,3},{2,0},{3,1},{4,6},{5,7},{6,4},{7,5},{8,10},{9,11},{10,... | collective-permute-start | bytes 491528 | tf_op jit(solution)/shard_map/ppermute | solution.py:322
  13.4 9.2 %collective-permute-start = (bf16[5,2,64,128]{3,2,1,0:T(8,128)(2,1)S(1)}, bf16[5,2,64,128]{3,2,1,0:T(8,128)(2,1)S(1)}, u32[]{:S(2)}, u32[]{:S(2)}) collective-permute-start(bf16[5,2,64,128]{3,2,1,0:T(8,128)(2,1)S(1)} %pack.1.mine), channel_id=1, source_target_pairs={{0,1},{1,0},{2,3},{3,2},{4,5},{5,4},{6,7},{7,6},{8,9},{9,8},{10,11... | collective-permute-start | bytes 491528 | tf_op jit(solution)/shard_map/ppermute | solution.py:322
  16.3 15.7 %collective-permute-start.7 = (bf16[5,1,64,128]{3,2,1,0:T(8,128)(2,1)S(1)}, bf16[5,1,64,128]{3,2,1,0:T(8,128)(2,1)S(1)}, u32[]{:S(2)}, u32[]{:S(2)}) collective-permute-start(bf16[5,1,64,128]{3,2,1,0:T(8,128)(2,1)S(1)} %slice.14), channel_id=1, source_target_pairs={{1,4},{3,6},{5,8},{7,10},{9,12},{11,14},{13,16},{15,18},{17,20},{1... | collective-permute-start | bytes 245768 | tf_op jit(solution)/shard_map/ppermute | solution.py:322
  19.4 12.6 %collective-permute-start.6 = (bf16[5,2,64,128]{3,2,1,0:T(8,128)(2,1)S(1)}, bf16[5,2,64,128]{3,2,1,0:T(8,128)(2,1)S(1)}, u32[]{:S(2)}, u32[]{:S(2)}) collective-permute-start(bf16[5,2,64,128]{3,2,1,0:T(8,128)(2,1)S(1)} %collective-permute-done.5), channel_id=1, source_target_pairs={{0,4},{1,5},{4,8},{5,9},{6,2},{7,3},{8,12},{9,13},{10,6},{11,7},{1... | collective-permute-start | bytes 491528 | tf_op jit(solution)/shard_map/ppermute | solution.py:322
  22.7 18.1 %collective-permute-start.2 = (bf16[4,4,64,128]{3,2,1,0:T(8,128)(2,1)S(1)}, bf16[4,4,64,128]{3,2,1,0:T(8,128)(2,1)S(1)}, u32[]{:S(2)}, u32[]{:S(2)}) collective-permute-start(bf16[4,4,64,128]{3,2,1,0:T(8,128)(2,1)S(1)} %pad_maximum_fusion), channel_id=1, source_target_pairs={{0,34},{1,67},{2,32},{3,65},{4,38},{5,71},{6,36},{7,69},{8,42},{9,... | collective-permute-start | bytes 786440 | tf_op jit(solution)/shard_map/ppermute | solution.py:322
  30.0 15.7 %collective-permute-start.1 = (bf16[4,4,64,128]{3,2,1,0:T(8,128)(2,1)S(1)}, bf16[4,4,64,128]{3,2,1,0:T(8,128)(2,1)S(1)}, u32[]{:S(2)}, u32[]{:S(2)}) collective-permute-start(bf16[4,4,64,128]{3,2,1,0:T(8,128)(2,1)S(1)} %pad_maximum_fusion), channel_id=1, source_target_pairs={{0,32},{1,65},{2,34},{3,67},{4,36},{5,69},{6,38},{7,71},{8,40},{9,... | collective-permute-start | bytes 786440 | tf_op jit(solution)/shard_map/ppermute | solution.py:322
  32.0 19.0 %collective-permute-start.8 = (bf16[5,5,64,128]{3,2,1,0:T(8,128)(2,1)S(1)}, bf16[5,5,64,128]{3,2,1,0:T(8,128)(2,1)S(1)}, u32[]{:S(2)}, u32[]{:S(2)}) collective-permute-start(bf16[5,5,64,128]{3,2,1,0:T(8,128)(2,1)S(1)} %constant_dynamic-update-slice_fusion.more), channel_id=1, source_target_pairs={{0,1},{1,0},{2,3},{3,2},{4,5},{5,4},{6,7},{7,6},{8,9},{9,8},{10,11... | collective-permute-start | bytes 1228808 | tf_op jit(solution)/shard_map/ppermute | solution.py:322
  40.8 14.3 %collective-permute-start.3 = (bf16[4,4,64,128]{3,2,1,0:T(8,128)(2,1)S(1)}, bf16[4,4,64,128]{3,2,1,0:T(8,128)(2,1)S(1)}, u32[]{:S(2)}, u32[]{:S(2)}) collective-permute-start(bf16[4,4,64,128]{3,2,1,0:T(8,128)(2,1)S(1)} %collective-permute-done.2.far), channel_id=1, source_target_pairs={{0,4},{1,5},{4,8},{5,9},{6,2},{7,3},{8,12},{9,13},{10,6},{11,7},{1... | collective-permute-start | bytes 786440 | tf_op jit(solution)/shard_map/ppermute | solution.py:322
  45.7 9.5 %collective-permute-start.4 = (bf16[4,1,64,128]{3,2,1,0:T(8,128)(2,1)S(1)}, bf16[4,1,64,128]{3,2,1,0:T(8,128)(2,1)S(1)}, u32[]{:S(2)}, u32[]{:S(2)}) collective-permute-start(bf16[4,1,64,128]{3,2,1,0:T(8,128)(2,1)S(1)} %constant_dynamic-slice_fusion), channel_id=1, source_target_pairs={{0,4},{1,5},{2,6},{3,7},{4,8},{5,9},{6,10},{7,11},{8,12},{9,13},{1... | collective-permute-start | bytes 196616 | tf_op jit(solution)/shard_map/ppermute | solution.py:322
  59.7 27.1 %collective-permute-start.9 = (f32[3,6,2,64,128]{4,3,2,1,0:T(8,128)S(1)}, f32[3,6,2,64,128]{4,3,2,1,0:T(8,128)S(1)}, u32[]{:S(2)}, u32[]{:S(2)}) collective-permute-start(f32[3,6,2,64,128]{4,3,2,1,0:T(8,128)S(1)} %get-tuple-element.24), channel_id=1, source_target_pairs={{0,1},{1,0},{2,3},{3,2},{4,5},{5,4},{6,7},{7,6},{8,9},{9,8},{10,11... | collective-permute-start | bytes 3538952 | tf_op jit(solution)/shard_map/ppermute | solution.py:322

commit v5 on v4

--- a/solution.py
+++ b/solution.py
@@ -192,10 +192,17 @@
             clear_rims(ref, (t,))
 
 
-def pack_kernel(modes, labels, raw):
+def pack_kernel(modes, regions, raw, ids, sems):
     blocks = modes.shape[0]
-    raw[pl.ds(0, blocks)] = modes[...]
-    raw[blocks] = labels[...]
+    copies = (
+        pltpu.make_async_copy(regions, ids, sems.at[0]),
+        pltpu.make_async_copy(modes, raw.at[pl.ds(0, blocks)], sems.at[1]),
+    )
+    for copy in copies:
+        copy.start()
+    copies[0].wait()
+    raw[blocks] = (ids[...] + 1).astype(raw.dtype)
+    copies[1].wait()
 
 
 def own_kernel(plan, stiff, cubic, mine, other, more, more_other,
@@ -337,11 +344,12 @@
     raw = pl.pallas_call(
         pack_kernel,
         out_shape=jax.ShapeDtypeStruct((per_block + 1, slabs, *slab), modes.dtype),
-        in_specs=[vm, vm],
+        in_specs=[pl.BlockSpec(memory_space=pltpu.HBM)] * 2,
         out_specs=vm,
+        scratch_shapes=[pltpu.VMEM((slabs,) + slab, jnp.int32), pltpu.SemaphoreType.DMA((2,))],
         compiler_params=pltpu.CompilerParams(vmem_limit_bytes=4 << 20),
         name="pack",
-    )(modes, (regions + 1).astype(modes.dtype))
+    )(*(pltpu.with_memory_space_constraint(v, pltpu.HBM) for v in (modes, regions)))
 
     odd = lax.axis_index("space") & 1
     raw_other = send(raw, partner_core)

time: 88.5 us -> 87.5 us (0.989)
  Pallas kernels: 9.87 us -> 10.9 us
  local copies, waits for them, and re-layouts: 1 us -> 0.1 us
    pallas_call x1, Pallas kernels: 0.01 us -> 0.99 us  [shards(): pl.pallas_call(pack_kernel, out_shape=jax.ShapeDtypeStruct((per_block + 1...]
    unnamed x10 -> x8, local copies, waits for them, and re-layouts: 0.95 us -> 0.05 us
where the time goes in v5:
time: 87.5 us; the launch traced here: 87.1 us
  starting transfers between devices  47.9 us (55%)
  blocking collectives  22.1 us (25%)
  Pallas kernels  10.9 us (12%)
  waiting for transfers between devices  5.94 us (7%)
    ppermute x10, starting transfers between devices, send(): return lax.ppermute(x, ('mode', 'space'), pairs)  47.9 us
    all_to_all x1, blocking collectives, shards(): gathered = lax.all_to_all(sums, 'space', 0, 0)  22.1 us
    ppermute x10, waiting for transfers between devices, send(): return lax.ppermute(x, ('mode', 'space'), pairs)  5.94 us
    pallas_call x1, Pallas kernels, shards(): pl.pallas_call(partner_kernel, out_shape=(basis, basis, array(n_space, 8,...  4.57 us
    pallas_call x1, Pallas kernels, shards(): pl.pallas_call(own_kernel, out_shape=(basis, basis, array(per_block, WIND...  4.07 us
  transfers between devices with their start and end apart: 10, of which 2 were waited for; matrix products, arithmetic and copies ran while one was open for 0% of the time, Pallas kernels for 5%

profile of v5, /device:TPU:1, one launch (start us, length us, event | category | flops | bytes accessed | tf_op | source)
XLA Modules:
  0.0 87.1 jit_solution(8080580031228275463)
XLA Ops:
  0.0 1.0 %pack.1.mine = bf16[5,2,64,128]{3,2,1,0:T(8,128)(2,1)S(1)} custom-call(bf16[4,2,64,128]{3,2,1,0:T(8,128)(2,1)} %modes.1, s32[2,64,128]{2,1,0:T(8,128)} %regions.1), custom_call_target="tpu_custom_call" | custom-call | tf_op jit(solution)/shard_map/pack/pallas_call | solution.py:344
  1.0 11.5 %collective-permute-start.5 = (bf16[5,2,64,128]{3,2,1,0:T(8,128)(2,1)S(1)}, bf16[5,2,64,128]{3,2,1,0:T(8,128)(2,1)S(1)}, u32[]{:S(2)}, u32[]{:S(2)}) collective-permute-start(bf16[5,2,64,128]{3,2,1,0:T(8,128)(2,1)S(1)} %pack.1.mine), channel_id=1, source_target_pairs={{0,2},{1,3},{2,0},{3,1},{4,6},{5,7},{6,4},{7,5},{8,10},{9,11},{10,... | collective-permute-start | bytes 491528 | tf_op jit(solution)/shard_map/ppermute | solution.py:329
  12.5 2.9 %collective-permute-start = (bf16[5,2,64,128]{3,2,1,0:T(8,128)(2,1)S(1)}, bf16[5,2,64,128]{3,2,1,0:T(8,128)(2,1)S(1)}, u32[]{:S(2)}, u32[]{:S(2)}) collective-permute-start(bf16[5,2,64,128]{3,2,1,0:T(8,128)(2,1)S(1)} %pack.1.mine), channel_id=1, source_target_pairs={{0,1},{1,0},{2,3},{3,2},{4,5},{5,4},{6,7},{7,6},{8,9},{9,8},{10,11... | collective-permute-start | bytes 491528 | tf_op jit(solution)/shard_map/ppermute | solution.py:329
  15.4 3.1 %collective-permute-start.7 = (bf16[5,1,64,128]{3,2,1,0:T(8,128)(2,1)S(1)}, bf16[5,1,64,128]{3,2,1,0:T(8,128)(2,1)S(1)}, u32[]{:S(2)}, u32[]{:S(2)}) collective-permute-start(bf16[5,1,64,128]{3,2,1,0:T(8,128)(2,1)S(1)} %slice.14), channel_id=1, source_target_pairs={{1,4},{3,6},{5,8},{7,10},{9,12},{11,14},{13,16},{15,18},{17,20},{1... | collective-permute-start | bytes 245768 | tf_op jit(solution)/shard_map/ppermute | solution.py:329
  18.5 0.0 collective-permute-done.5
  18.5 3.2 %collective-permute-start.6 = (bf16[5,2,64,128]{3,2,1,0:T(8,128)(2,1)S(1)}, bf16[5,2,64,128]{3,2,1,0:T(8,128)(2,1)S(1)}, u32[]{:S(2)}, u32[]{:S(2)}) collective-permute-start(bf16[5,2,64,128]{3,2,1,0:T(8,128)(2,1)S(1)} %collective-permute-done.5), channel_id=1, source_target_pairs={{0,4},{1,5},{4,8},{5,9},{6,2},{7,3},{8,12},{9,13},{10,6},{11,7},{1... | collective-permute-start | bytes 491528 | tf_op jit(solution)/shard_map/ppermute | solution.py:329
  21.7 0.0 collective-permute-done.other
  21.8 7.3 %collective-permute-start.2 = (bf16[4,4,64,128]{3,2,1,0:T(8,128)(2,1)S(1)}, bf16[4,4,64,128]{3,2,1,0:T(8,128)(2,1)S(1)}, u32[]{:S(2)}, u32[]{:S(2)}) collective-permute-start(bf16[4,4,64,128]{3,2,1,0:T(8,128)(2,1)S(1)} %pad_maximum_fusion), channel_id=1, source_target_pairs={{0,34},{1,67},{2,32},{3,65},{4,38},{5,71},{6,36},{7,69},{8,42},{9,... | collective-permute-start | bytes 786440 | tf_op jit(solution)/shard_map/ppermute | solution.py:329
  29.1 1.9 %collective-permute-start.1 = (bf16[4,4,64,128]{3,2,1,0:T(8,128)(2,1)S(1)}, bf16[4,4,64,128]{3,2,1,0:T(8,128)(2,1)S(1)}, u32[]{:S(2)}, u32[]{:S(2)}) collective-permute-start(bf16[4,4,64,128]{3,2,1,0:T(8,128)(2,1)S(1)} %pad_maximum_fusion), channel_id=1, source_target_pairs={{0,32},{1,65},{2,34},{3,67},{4,36},{5,69},{6,38},{7,71},{8,40},{9,... | collective-permute-start | bytes 786440 | tf_op jit(solution)/shard_map/ppermute | solution.py:329
  31.1 0.0 collective-permute-done.6
  31.1 0.0 collective-permute-done.7
  31.1 4.1 %collective-permute-start.8 = (bf16[5,5,64,128]{3,2,1,0:T(8,128)(2,1)S(1)}, bf16[5,5,64,128]{3,2,1,0:T(8,128)(2,1)S(1)}, u32[]{:S(2)}, u32[]{:S(2)}) collective-permute-start(bf16[5,5,64,128]{3,2,1,0:T(8,128)(2,1)S(1)} %constant_dynamic-update-slice_fusion.more), channel_id=1, source_target_pairs={{0,1},{1,0},{2,3},{3,2},{4,5},{5,4},{6,7},{7,6},{8,9},{9,8},{10,11... | collective-permute-start | bytes 1228808 | tf_op jit(solution)/shard_map/ppermute | solution.py:329
  35.3 4.6 %collective-permute-done.2.far = bf16[4,4,64,128]{3,2,1,0:T(8,128)(2,1)S(1)} collective-permute-done((bf16[4,4,64,128]{3,2,1,0:T(8,128)(2,1)S(1)}, bf16[4,4,64,128]{3,2,1,0:T(8,128)(2,1)S(1)}, u32[]{:S(2)}, u32[]{:S(2)}) %collective-permute-start.2) | collective-permute-done | bytes 262176 | tf_op jit(solution)/shard_map/ppermute | solution.py:329
  39.9 3.6 %collective-permute-start.3 = (bf16[4,4,64,128]{3,2,1,0:T(8,128)(2,1)S(1)}, bf16[4,4,64,128]{3,2,1,0:T(8,128)(2,1)S(1)}, u32[]{:S(2)}, u32[]{:S(2)}) collective-permute-start(bf16[4,4,64,128]{3,2,1,0:T(8,128)(2,1)S(1)} %collective-permute-done.2.far), channel_id=1, source_target_pairs={{0,4},{1,5},{4,8},{5,9},{6,2},{7,3},{8,12},{9,13},{10,6},{11,7},{1... | collective-permute-start | bytes 786440 | tf_op jit(solution)/shard_map/ppermute | solution.py:329
  43.5 1.3 %collective-permute-done.1.near = bf16[4,4,64,128]{3,2,1,0:T(8,128)(2,1)S(1)} collective-permute-done((bf16[4,4,64,128]{3,2,1,0:T(8,128)(2,1)S(1)}, bf16[4,4,64,128]{3,2,1,0:T(8,128)(2,1)S(1)}, u32[]{:S(2)}, u32[]{:S(2)}) %collective-permute-start.1) | collective-permute-done | bytes 262176 | tf_op jit(solution)/shard_map/ppermute | solution.py:329
  44.8 5.3 %collective-permute-start.4 = (bf16[4,1,64,128]{3,2,1,0:T(8,128)(2,1)S(1)}, bf16[4,1,64,128]{3,2,1,0:T(8,128)(2,1)S(1)}, u32[]{:S(2)}, u32[]{:S(2)}) collective-permute-start(bf16[4,1,64,128]{3,2,1,0:T(8,128)(2,1)S(1)} %constant_dynamic-slice_fusion), channel_id=1, source_target_pairs={{0,4},{1,5},{2,6},{3,7},{4,8},{5,9},{6,10},{7,11},{8,12},{9,13},{1... | collective-permute-start | bytes 196616 | tf_op jit(solution)/shard_map/ppermute | solution.py:329
  50.1 0.0 collective-permute-done.8.more_other
  50.2 4.1 %own.1 = (f32[3,2,2,64,128]{4,3,2,1,0:T(8,128)S(1)}, f32[3,2,2,64,128]{4,3,2,1,0:T(8,128)S(1)}, f32[4,11,64,128]{3,2,1,0:T(8,128)S(1)}, f32[9,64,128]{2,1,0:T(8,...) custom-call(s32[4,3]{1,0:T(4,128)S(1)} %copy-done, f32[8]{0:T(128)S(1)} %copy-done.1, ...), custom_call_target="tpu_custom_call" | custom-call | flops 20000000 | bytes 8388608 | tf_op jit(solution)/shard_map/own/pallas_call | solution.py:367
  54.2 0.0 collective-permute-done.4.edge
  54.2 0.0 collective-permute-done.3.along
  54.2 4.6 %partner.1 = (f32[3,6,2,64,128]{4,3,2,1,0:T(8,128)S(1)}, f32[3,6,2,64,128]{4,3,2,1,0:T(8,128)S(1)}, f32[32,8,128]{2,1,0:T(8,128)S(1)}) custom-call(s32[4,3]{1,0:T(4,128)S(1)} %copy-done, bf16[4,4,64,128]{3,2,1,0:T(8,128)(2,1)S(1)} %collective-permute-done.1.near, bf16[4,4,64,128]{3,2,1,0:T(8,128)(2,1)S(1)} %collective-permute-done.2.far, ...), custom_call_target="tpu_custom_call" | custom-call | flops 40000000 | bytes 16777216 | tf_op jit(solution)/shard_map/partner/pallas_call | solution.py:397
  58.8 5.0 %collective-permute-start.9 = (f32[3,6,2,64,128]{4,3,2,1,0:T(8,128)S(1)}, f32[3,6,2,64,128]{4,3,2,1,0:T(8,128)S(1)}, u32[]{:S(2)}, u32[]{:S(2)}) collective-permute-start(f32[3,6,2,64,128]{4,3,2,1,0:T(8,128)S(1)} %get-tuple-element.24), channel_id=1, source_target_pairs={{0,1},{1,0},{2,3},{3,2},{4,5},{5,4},{6,7},{7,6},{8,9},{9,8},{10,11... | collective-permute-start | bytes 3538952 | tf_op jit(solution)/shard_map/ppermute | solution.py:329
  63.8 22.1 %all_to_all.5.sums = f32[32,8,128]{2,1,0:T(8,128)S(1)} all-to-all(f32[32,8,128]{2,1,0:T(8,128)S(1)} %get-tuple-element.22), channel_id=1, replica_groups=mesh['mode'=16,'space'=32] {'space'}, dimensions={0} | all-to-all | bytes 262144 | tf_op jit(solution)/shard_map/all_to_all | solution.py:414
  85.9 1.2 %combine.1 = f32[12,2,64,128]{3,2,1,0:T(8,128)} custom-call(f32[32,8,128]{2,1,0:T(8,128)S(1)} %all_to_all.5.sums, f32[3,6,2,64,128]{4,3,2,1,0:T(8,128)S(1)} %get-tuple-element.23.keep, f32[3,6,2,64,128]{4,3,2,1,0:T(8,128)S(1)} %collective-permute-done.9.got), custom_call_target="tpu_custom_call" | custom-call | tf_op jit(solution)/shard_map/combine/pallas_call | solution.py:416
  (15 shorter events, 0.1 us)
Async XLA Ops:
  0.0 50.1 %copy-start = (s32[4,3]{1,0:T(4,128)S(1)}, s32[4,3]{1,0:T(4,128)}, u32[]{:S(2)}) copy-start(s32[4,3]{1,0:T(4,128)} %plan.3) | copy-start | bytes 148
  0.0 50.1 %copy-start.2 = (f32[8]{0:T(128)S(1)}, f32[8]{0:T(128)}, u32[]{:S(2)}) copy-start(f32[8]{0:T(128)} %cubic.1) | copy-start | bytes 100
  0.0 50.1 %copy-start.1 = (f32[8]{0:T(128)S(1)}, f32[8]{0:T(128)}, u32[]{:S(2)}) copy-start(f32[8]{0:T(128)} %stiff.1) | copy-start | bytes 100
  1.0 17.5 %collective-permute-start.5 = (bf16[5,2,64,128]{3,2,1,0:T(8,128)(2,1)S(1)}, bf16[5,2,64,128]{3,2,1,0:T(8,128)(2,1)S(1)}, u32[]{:S(2)}, u32[]{:S(2)}) collective-permute-start(bf16[5,2,64,128]{3,2,1,0:T(8,128)(2,1)S(1)} %pack.1.mine), channel_id=1, source_target_pairs={{0,2},{1,3},{2,0},{3,1},{4,6},{5,7},{6,4},{7,5},{8,10},{9,11},{10,... | collective-permute-start | bytes 491528 | tf_op jit(solution)/shard_map/ppermute | solution.py:329
  12.5 9.2 %collective-permute-start = (bf16[5,2,64,128]{3,2,1,0:T(8,128)(2,1)S(1)}, bf16[5,2,64,128]{3,2,1,0:T(8,128)(2,1)S(1)}, u32[]{:S(2)}, u32[]{:S(2)}) collective-permute-start(bf16[5,2,64,128]{3,2,1,0:T(8,128)(2,1)S(1)} %pack.1.mine), channel_id=1, source_target_pairs={{0,1},{1,0},{2,3},{3,2},{4,5},{5,4},{6,7},{7,6},{8,9},{9,8},{10,11... | collective-permute-start | bytes 491528 | tf_op jit(solution)/shard_map/ppermute | solution.py:329
  15.4 15.7 %collective-permute-start.7 = (bf16[5,1,64,128]{3,2,1,0:T(8,128)(2,1)S(1)}, bf16[5,1,64,128]{3,2,1,0:T(8,128)(2,1)S(1)}, u32[]{:S(2)}, u32[]{:S(2)}) collective-permute-start(bf16[5,1,64,128]{3,2,1,0:T(8,128)(2,1)S(1)} %slice.14), channel_id=1, source_target_pairs={{1,4},{3,6},{5,8},{7,10},{9,12},{11,14},{13,16},{15,18},{17,20},{1... | collective-permute-start | bytes 245768 | tf_op jit(solution)/shard_map/ppermute | solution.py:329
  18.5 12.6 %collective-permute-start.6 = (bf16[5,2,64,128]{3,2,1,0:T(8,128)(2,1)S(1)}, bf16[5,2,64,128]{3,2,1,0:T(8,128)(2,1)S(1)}, u32[]{:S(2)}, u32[]{:S(2)}) collective-permute-start(bf16[5,2,64,128]{3,2,1,0:T(8,128)(2,1)S(1)} %collective-permute-done.5), channel_id=1, source_target_pairs={{0,4},{1,5},{4,8},{5,9},{6,2},{7,3},{8,12},{9,13},{10,6},{11,7},{1... | collective-permute-start | bytes 491528 | tf_op jit(solution)/shard_map/ppermute | solution.py:329
  21.8 18.1 %collective-permute-start.2 = (bf16[4,4,64,128]{3,2,1,0:T(8,128)(2,1)S(1)}, bf16[4,4,64,128]{3,2,1,0:T(8,128)(2,1)S(1)}, u32[]{:S(2)}, u32[]{:S(2)}) collective-permute-start(bf16[4,4,64,128]{3,2,1,0:T(8,128)(2,1)S(1)} %pad_maximum_fusion), channel_id=1, source_target_pairs={{0,34},{1,67},{2,32},{3,65},{4,38},{5,71},{6,36},{7,69},{8,42},{9,... | collective-permute-start | bytes 786440 | tf_op jit(solution)/shard_map/ppermute | solution.py:329
  29.1 15.7 %collective-permute-start.1 = (bf16[4,4,64,128]{3,2,1,0:T(8,128)(2,1)S(1)}, bf16[4,4,64,128]{3,2,1,0:T(8,128)(2,1)S(1)}, u32[]{:S(2)}, u32[]{:S(2)}) collective-permute-start(bf16[4,4,64,128]{3,2,1,0:T(8,128)(2,1)S(1)} %pad_maximum_fusion), channel_id=1, source_target_pairs={{0,32},{1,65},{2,34},{3,67},{4,36},{5,69},{6,38},{7,71},{8,40},{9,... | collective-permute-start | bytes 786440 | tf_op jit(solution)/shard_map/ppermute | solution.py:329
  31.1 19.0 %collective-permute-start.8 = (bf16[5,5,64,128]{3,2,1,0:T(8,128)(2,1)S(1)}, bf16[5,5,64,128]{3,2,1,0:T(8,128)(2,1)S(1)}, u32[]{:S(2)}, u32[]{:S(2)}) collective-permute-start(bf16[5,5,64,128]{3,2,1,0:T(8,128)(2,1)S(1)} %constant_dynamic-update-slice_fusion.more), channel_id=1, source_target_pairs={{0,1},{1,0},{2,3},{3,2},{4,5},{5,4},{6,7},{7,6},{8,9},{9,8},{10,11... | collective-permute-start | bytes 1228808 | tf_op jit(solution)/shard_map/ppermute | solution.py:329
  39.9 14.3 %collective-permute-start.3 = (bf16[4,4,64,128]{3,2,1,0:T(8,128)(2,1)S(1)}, bf16[4,4,64,128]{3,2,1,0:T(8,128)(2,1)S(1)}, u32[]{:S(2)}, u32[]{:S(2)}) collective-permute-start(bf16[4,4,64,128]{3,2,1,0:T(8,128)(2,1)S(1)} %collective-permute-done.2.far), channel_id=1, source_target_pairs={{0,4},{1,5},{4,8},{5,9},{6,2},{7,3},{8,12},{9,13},{10,6},{11,7},{1... | collective-permute-start | bytes 786440 | tf_op jit(solution)/shard_map/ppermute | solution.py:329
  44.8 9.5 %collective-permute-start.4 = (bf16[4,1,64,128]{3,2,1,0:T(8,128)(2,1)S(1)}, bf16[4,1,64,128]{3,2,1,0:T(8,128)(2,1)S(1)}, u32[]{:S(2)}, u32[]{:S(2)}) collective-permute-start(bf16[4,1,64,128]{3,2,1,0:T(8,128)(2,1)S(1)} %constant_dynamic-slice_fusion), channel_id=1, source_target_pairs={{0,4},{1,5},{2,6},{3,7},{4,8},{5,9},{6,10},{7,11},{8,12},{9,13},{1... | collective-permute-start | bytes 196616 | tf_op jit(solution)/shard_map/ppermute | solution.py:329
  58.8 27.1 %collective-permute-start.9 = (f32[3,6,2,64,128]{4,3,2,1,0:T(8,128)S(1)}, f32[3,6,2,64,128]{4,3,2,1,0:T(8,128)S(1)}, u32[]{:S(2)}, u32[]{:S(2)}) collective-permute-start(f32[3,6,2,64,128]{4,3,2,1,0:T(8,128)S(1)} %get-tuple-element.24), channel_id=1, source_target_pairs={{0,1},{1,0},{2,3},{3,2},{4,5},{5,4},{6,7},{7,6},{8,9},{9,8},{10,11... | collective-permute-start | bytes 3538952 | tf_op jit(solution)/shard_map/ppermute | solution.py:329

commit v6 on v5

--- a/solution.py
+++ b/solution.py
@@ -269,7 +269,7 @@
         sums[d] = total
 
 
-def combine_kernel(sums, keep, got, out):
+def combine_kernel(sums, keep, got, out, held, sems):
     m = jnp.sum(sums[...], axis=0)
     mu = [m[k : k + 1] for k in range(MOMENTS)]
     ka = [mu[k] - mu[k + 1] for k in range(MOMENTS - 1)]
@@ -305,12 +305,18 @@
         return jnp.sum(jnp.where(lane == f, c, 0.0), axis=1, keepdims=True)
 
     core, _ = position()
+    copies = []
     for basis, q in ((keep, core), (got, 1 - core)):
         for n in range(basis.shape[1]):
             f = (GROUP * q + n) * PARTNERS if n < GROUP else (n - GROUP) * PARTNERS + 1 + q
             c0, c1, c2 = (pick(c, f) for c in x)
+            at = n if basis is keep else basis.shape[1] + n
             for i in range(out.shape[1]):
-                out[f, i] = c0 * basis[0, n, i] + c1 * basis[1, n, i] + c2 * basis[2, n, i]
+                held[at, i] = c0 * basis[0, n, i] + c1 * basis[1, n, i] + c2 * basis[2, n, i]
+            copies.append(pltpu.make_async_copy(held.at[at], out.at[f], sems.at[at]))
+            copies[-1].start()
+    for copy in copies:
+        copy.wait()
 
 
 def shards(modes, regions, stiffness, nonlinear, plan):
@@ -417,7 +423,8 @@
         combine_kernel,
         out_shape=array(fields, slabs, *slab),
         in_specs=[vm] * 3,
-        out_specs=vm,
+        out_specs=pl.BlockSpec(memory_space=pltpu.HBM),
+        scratch_shapes=[pltpu.VMEM((fields, slabs) + slab, f32), pltpu.SemaphoreType.DMA((fields,))],
         compiler_params=pltpu.CompilerParams(vmem_limit_bytes=16 << 20),
         name="combine",
     )(gathered, keep, got)

time: 87.5 us -> 87.5 us (level)
  no operation moved by 1% of the time
where the time goes in v6:
time: 87.5 us; the launch traced here: 87.1 us
  starting transfers between devices  47.9 us (55%)
  blocking collectives  22.1 us (25%)
  Pallas kernels  10.8 us (12%)
  waiting for transfers between devices  5.94 us (7%)
    ppermute x10, starting transfers between devices, send(): return lax.ppermute(x, ('mode', 'space'), pairs)  47.9 us
    all_to_all x1, blocking collectives, shards(): gathered = lax.all_to_all(sums, 'space', 0, 0)  22.1 us
    ppermute x10, waiting for transfers between devices, send(): return lax.ppermute(x, ('mode', 'space'), pairs)  5.94 us
    pallas_call x1, Pallas kernels, shards(): pl.pallas_call(partner_kernel, out_shape=(basis, basis, array(n_space, 8,...  4.57 us
    pallas_call x1, Pallas kernels, shards(): pl.pallas_call(own_kernel, out_shape=(basis, basis, array(per_block, WIND...  4.07 us
  transfers between devices with their start and end apart: 10, of which 2 were waited for; matrix products, arithmetic and copies ran while one was open for 0% of the time, Pallas kernels for 5%

profile of v6, /device:TPU:1, one launch (start us, length us, event | category | flops | bytes accessed | tf_op | source)
XLA Modules:
  0.0 87.1 jit_solution(1734063173874284469)
XLA Ops:
  0.0 1.0 %pack.1.mine = bf16[5,2,64,128]{3,2,1,0:T(8,128)(2,1)S(1)} custom-call(bf16[4,2,64,128]{3,2,1,0:T(8,128)(2,1)} %modes.1, s32[2,64,128]{2,1,0:T(8,128)} %regions.1), custom_call_target="tpu_custom_call" | custom-call | tf_op jit(solution)/shard_map/pack/pallas_call | solution.py:350
  1.0 11.5 %collective-permute-start.5 = (bf16[5,2,64,128]{3,2,1,0:T(8,128)(2,1)S(1)}, bf16[5,2,64,128]{3,2,1,0:T(8,128)(2,1)S(1)}, u32[]{:S(2)}, u32[]{:S(2)}) collective-permute-start(bf16[5,2,64,128]{3,2,1,0:T(8,128)(2,1)S(1)} %pack.1.mine), channel_id=1, source_target_pairs={{0,2},{1,3},{2,0},{3,1},{4,6},{5,7},{6,4},{7,5},{8,10},{9,11},{10,... | collective-permute-start | bytes 491528 | tf_op jit(solution)/shard_map/ppermute | solution.py:335
  12.5 2.9 %collective-permute-start = (bf16[5,2,64,128]{3,2,1,0:T(8,128)(2,1)S(1)}, bf16[5,2,64,128]{3,2,1,0:T(8,128)(2,1)S(1)}, u32[]{:S(2)}, u32[]{:S(2)}) collective-permute-start(bf16[5,2,64,128]{3,2,1,0:T(8,128)(2,1)S(1)} %pack.1.mine), channel_id=1, source_target_pairs={{0,1},{1,0},{2,3},{3,2},{4,5},{5,4},{6,7},{7,6},{8,9},{9,8},{10,11... | collective-permute-start | bytes 491528 | tf_op jit(solution)/shard_map/ppermute | solution.py:335
  15.4 3.1 %collective-permute-start.7 = (bf16[5,1,64,128]{3,2,1,0:T(8,128)(2,1)S(1)}, bf16[5,1,64,128]{3,2,1,0:T(8,128)(2,1)S(1)}, u32[]{:S(2)}, u32[]{:S(2)}) collective-permute-start(bf16[5,1,64,128]{3,2,1,0:T(8,128)(2,1)S(1)} %slice.14), channel_id=1, source_target_pairs={{1,4},{3,6},{5,8},{7,10},{9,12},{11,14},{13,16},{15,18},{17,20},{1... | collective-permute-start | bytes 245768 | tf_op jit(solution)/shard_map/ppermute | solution.py:335
  18.5 0.0 collective-permute-done.5
  18.5 3.2 %collective-permute-start.6 = (bf16[5,2,64,128]{3,2,1,0:T(8,128)(2,1)S(1)}, bf16[5,2,64,128]{3,2,1,0:T(8,128)(2,1)S(1)}, u32[]{:S(2)}, u32[]{:S(2)}) collective-permute-start(bf16[5,2,64,128]{3,2,1,0:T(8,128)(2,1)S(1)} %collective-permute-done.5), channel_id=1, source_target_pairs={{0,4},{1,5},{4,8},{5,9},{6,2},{7,3},{8,12},{9,13},{10,6},{11,7},{1... | collective-permute-start | bytes 491528 | tf_op jit(solution)/shard_map/ppermute | solution.py:335
  21.7 0.0 collective-permute-done.other
  21.8 7.3 %collective-permute-start.2 = (bf16[4,4,64,128]{3,2,1,0:T(8,128)(2,1)S(1)}, bf16[4,4,64,128]{3,2,1,0:T(8,128)(2,1)S(1)}, u32[]{:S(2)}, u32[]{:S(2)}) collective-permute-start(bf16[4,4,64,128]{3,2,1,0:T(8,128)(2,1)S(1)} %pad_maximum_fusion), channel_id=1, source_target_pairs={{0,34},{1,67},{2,32},{3,65},{4,38},{5,71},{6,36},{7,69},{8,42},{9,... | collective-permute-start | bytes 786440 | tf_op jit(solution)/shard_map/ppermute | solution.py:335
  29.1 1.9 %collective-permute-start.1 = (bf16[4,4,64,128]{3,2,1,0:T(8,128)(2,1)S(1)}, bf16[4,4,64,128]{3,2,1,0:T(8,128)(2,1)S(1)}, u32[]{:S(2)}, u32[]{:S(2)}) collective-permute-start(bf16[4,4,64,128]{3,2,1,0:T(8,128)(2,1)S(1)} %pad_maximum_fusion), channel_id=1, source_target_pairs={{0,32},{1,65},{2,34},{3,67},{4,36},{5,69},{6,38},{7,71},{8,40},{9,... | collective-permute-start | bytes 786440 | tf_op jit(solution)/shard_map/ppermute | solution.py:335
  31.1 0.0 collective-permute-done.6
  31.1 0.0 collective-permute-done.7
  31.1 4.1 %collective-permute-start.8 = (bf16[5,5,64,128]{3,2,1,0:T(8,128)(2,1)S(1)}, bf16[5,5,64,128]{3,2,1,0:T(8,128)(2,1)S(1)}, u32[]{:S(2)}, u32[]{:S(2)}) collective-permute-start(bf16[5,5,64,128]{3,2,1,0:T(8,128)(2,1)S(1)} %constant_dynamic-update-slice_fusion.more), channel_id=1, source_target_pairs={{0,1},{1,0},{2,3},{3,2},{4,5},{5,4},{6,7},{7,6},{8,9},{9,8},{10,11... | collective-permute-start | bytes 1228808 | tf_op jit(solution)/shard_map/ppermute | solution.py:335
  35.3 4.6 %collective-permute-done.2.far = bf16[4,4,64,128]{3,2,1,0:T(8,128)(2,1)S(1)} collective-permute-done((bf16[4,4,64,128]{3,2,1,0:T(8,128)(2,1)S(1)}, bf16[4,4,64,128]{3,2,1,0:T(8,128)(2,1)S(1)}, u32[]{:S(2)}, u32[]{:S(2)}) %collective-permute-start.2) | collective-permute-done | bytes 262176 | tf_op jit(solution)/shard_map/ppermute | solution.py:335
  39.9 3.6 %collective-permute-start.3 = (bf16[4,4,64,128]{3,2,1,0:T(8,128)(2,1)S(1)}, bf16[4,4,64,128]{3,2,1,0:T(8,128)(2,1)S(1)}, u32[]{:S(2)}, u32[]{:S(2)}) collective-permute-start(bf16[4,4,64,128]{3,2,1,0:T(8,128)(2,1)S(1)} %collective-permute-done.2.far), channel_id=1, source_target_pairs={{0,4},{1,5},{4,8},{5,9},{6,2},{7,3},{8,12},{9,13},{10,6},{11,7},{1... | collective-permute-start | bytes 786440 | tf_op jit(solution)/shard_map/ppermute | solution.py:335
  43.5 1.3 %collective-permute-done.1.near = bf16[4,4,64,128]{3,2,1,0:T(8,128)(2,1)S(1)} collective-permute-done((bf16[4,4,64,128]{3,2,1,0:T(8,128)(2,1)S(1)}, bf16[4,4,64,128]{3,2,1,0:T(8,128)(2,1)S(1)}, u32[]{:S(2)}, u32[]{:S(2)}) %collective-permute-start.1) | collective-permute-done | bytes 262176 | tf_op jit(solution)/shard_map/ppermute | solution.py:335
  44.8 5.3 %collective-permute-start.4 = (bf16[4,1,64,128]{3,2,1,0:T(8,128)(2,1)S(1)}, bf16[4,1,64,128]{3,2,1,0:T(8,128)(2,1)S(1)}, u32[]{:S(2)}, u32[]{:S(2)}) collective-permute-start(bf16[4,1,64,128]{3,2,1,0:T(8,128)(2,1)S(1)} %constant_dynamic-slice_fusion), channel_id=1, source_target_pairs={{0,4},{1,5},{2,6},{3,7},{4,8},{5,9},{6,10},{7,11},{8,12},{9,13},{1... | collective-permute-start | bytes 196616 | tf_op jit(solution)/shard_map/ppermute | solution.py:335
  50.1 0.0 collective-permute-done.8.more_other
  50.2 4.1 %own.1 = (f32[3,2,2,64,128]{4,3,2,1,0:T(8,128)S(1)}, f32[3,2,2,64,128]{4,3,2,1,0:T(8,128)S(1)}, f32[4,11,64,128]{3,2,1,0:T(8,128)S(1)}, f32[9,64,128]{2,1,0:T(8,...) custom-call(s32[4,3]{1,0:T(4,128)S(1)} %copy-done, f32[8]{0:T(128)S(1)} %copy-done.1, ...), custom_call_target="tpu_custom_call" | custom-call | flops 20000000 | bytes 8388608 | tf_op jit(solution)/shard_map/own/pallas_call | solution.py:373
  54.2 0.0 collective-permute-done.4.edge
  54.2 0.0 collective-permute-done.3.along
  54.2 4.6 %partner.1 = (f32[3,6,2,64,128]{4,3,2,1,0:T(8,128)S(1)}, f32[3,6,2,64,128]{4,3,2,1,0:T(8,128)S(1)}, f32[32,8,128]{2,1,0:T(8,128)S(1)}) custom-call(s32[4,3]{1,0:T(4,128)S(1)} %copy-done, bf16[4,4,64,128]{3,2,1,0:T(8,128)(2,1)S(1)} %collective-permute-done.1.near, bf16[4,4,64,128]{3,2,1,0:T(8,128)(2,1)S(1)} %collective-permute-done.2.far, ...), custom_call_target="tpu_custom_call" | custom-call | flops 40000000 | bytes 16777216 | tf_op jit(solution)/shard_map/partner/pallas_call | solution.py:403
  58.8 5.0 %collective-permute-start.9 = (f32[3,6,2,64,128]{4,3,2,1,0:T(8,128)S(1)}, f32[3,6,2,64,128]{4,3,2,1,0:T(8,128)S(1)}, u32[]{:S(2)}, u32[]{:S(2)}) collective-permute-start(f32[3,6,2,64,128]{4,3,2,1,0:T(8,128)S(1)} %get-tuple-element.24), channel_id=1, source_target_pairs={{0,1},{1,0},{2,3},{3,2},{4,5},{5,4},{6,7},{7,6},{8,9},{9,8},{10,11... | collective-permute-start | bytes 3538952 | tf_op jit(solution)/shard_map/ppermute | solution.py:335
  63.8 22.1 %all_to_all.5.sums = f32[32,8,128]{2,1,0:T(8,128)S(1)} all-to-all(f32[32,8,128]{2,1,0:T(8,128)S(1)} %get-tuple-element.22), channel_id=1, replica_groups=mesh['mode'=16,'space'=32] {'space'}, dimensions={0} | all-to-all | bytes 262144 | tf_op jit(solution)/shard_map/all_to_all | solution.py:420
  85.9 1.2 %combine.1 = f32[12,2,64,128]{3,2,1,0:T(8,128)} custom-call(f32[32,8,128]{2,1,0:T(8,128)S(1)} %all_to_all.5.sums, f32[3,6,2,64,128]{4,3,2,1,0:T(8,128)S(1)} %get-tuple-element.23.keep, f32[3,6,2,64,128]{4,3,2,1,0:T(8,128)S(1)} %collective-permute-done.9.got), custom_call_target="tpu_custom_call" | custom-call | tf_op jit(solution)/shard_map/combine/pallas_call | solution.py:422
  (15 shorter events, 0.1 us)
Async XLA Ops:
  0.0 50.1 %copy-start = (s32[4,3]{1,0:T(4,128)S(1)}, s32[4,3]{1,0:T(4,128)}, u32[]{:S(2)}) copy-start(s32[4,3]{1,0:T(4,128)} %plan.3) | copy-start | bytes 148
  0.0 50.1 %copy-start.2 = (f32[8]{0:T(128)S(1)}, f32[8]{0:T(128)}, u32[]{:S(2)}) copy-start(f32[8]{0:T(128)} %cubic.1) | copy-start | bytes 100
  0.0 50.1 %copy-start.1 = (f32[8]{0:T(128)S(1)}, f32[8]{0:T(128)}, u32[]{:S(2)}) copy-start(f32[8]{0:T(128)} %stiff.1) | copy-start | bytes 100
  1.0 17.5 %collective-permute-start.5 = (bf16[5,2,64,128]{3,2,1,0:T(8,128)(2,1)S(1)}, bf16[5,2,64,128]{3,2,1,0:T(8,128)(2,1)S(1)}, u32[]{:S(2)}, u32[]{:S(2)}) collective-permute-start(bf16[5,2,64,128]{3,2,1,0:T(8,128)(2,1)S(1)} %pack.1.mine), channel_id=1, source_target_pairs={{0,2},{1,3},{2,0},{3,1},{4,6},{5,7},{6,4},{7,5},{8,10},{9,11},{10,... | collective-permute-start | bytes 491528 | tf_op jit(solution)/shard_map/ppermute | solution.py:335
  12.5 9.2 %collective-permute-start = (bf16[5,2,64,128]{3,2,1,0:T(8,128)(2,1)S(1)}, bf16[5,2,64,128]{3,2,1,0:T(8,128)(2,1)S(1)}, u32[]{:S(2)}, u32[]{:S(2)}) collective-permute-start(bf16[5,2,64,128]{3,2,1,0:T(8,128)(2,1)S(1)} %pack.1.mine), channel_id=1, source_target_pairs={{0,1},{1,0},{2,3},{3,2},{4,5},{5,4},{6,7},{7,6},{8,9},{9,8},{10,11... | collective-permute-start | bytes 491528 | tf_op jit(solution)/shard_map/ppermute | solution.py:335
  15.4 15.7 %collective-permute-start.7 = (bf16[5,1,64,128]{3,2,1,0:T(8,128)(2,1)S(1)}, bf16[5,1,64,128]{3,2,1,0:T(8,128)(2,1)S(1)}, u32[]{:S(2)}, u32[]{:S(2)}) collective-permute-start(bf16[5,1,64,128]{3,2,1,0:T(8,128)(2,1)S(1)} %slice.14), channel_id=1, source_target_pairs={{1,4},{3,6},{5,8},{7,10},{9,12},{11,14},{13,16},{15,18},{17,20},{1... | collective-permute-start | bytes 245768 | tf_op jit(solution)/shard_map/ppermute | solution.py:335
  18.5 12.6 %collective-permute-start.6 = (bf16[5,2,64,128]{3,2,1,0:T(8,128)(2,1)S(1)}, bf16[5,2,64,128]{3,2,1,0:T(8,128)(2,1)S(1)}, u32[]{:S(2)}, u32[]{:S(2)}) collective-permute-start(bf16[5,2,64,128]{3,2,1,0:T(8,128)(2,1)S(1)} %collective-permute-done.5), channel_id=1, source_target_pairs={{0,4},{1,5},{4,8},{5,9},{6,2},{7,3},{8,12},{9,13},{10,6},{11,7},{1... | collective-permute-start | bytes 491528 | tf_op jit(solution)/shard_map/ppermute | solution.py:335
  21.8 18.1 %collective-permute-start.2 = (bf16[4,4,64,128]{3,2,1,0:T(8,128)(2,1)S(1)}, bf16[4,4,64,128]{3,2,1,0:T(8,128)(2,1)S(1)}, u32[]{:S(2)}, u32[]{:S(2)}) collective-permute-start(bf16[4,4,64,128]{3,2,1,0:T(8,128)(2,1)S(1)} %pad_maximum_fusion), channel_id=1, source_target_pairs={{0,34},{1,67},{2,32},{3,65},{4,38},{5,71},{6,36},{7,69},{8,42},{9,... | collective-permute-start | bytes 786440 | tf_op jit(solution)/shard_map/ppermute | solution.py:335
  29.1 15.7 %collective-permute-start.1 = (bf16[4,4,64,128]{3,2,1,0:T(8,128)(2,1)S(1)}, bf16[4,4,64,128]{3,2,1,0:T(8,128)(2,1)S(1)}, u32[]{:S(2)}, u32[]{:S(2)}) collective-permute-start(bf16[4,4,64,128]{3,2,1,0:T(8,128)(2,1)S(1)} %pad_maximum_fusion), channel_id=1, source_target_pairs={{0,32},{1,65},{2,34},{3,67},{4,36},{5,69},{6,38},{7,71},{8,40},{9,... | collective-permute-start | bytes 786440 | tf_op jit(solution)/shard_map/ppermute | solution.py:335
  31.1 19.0 %collective-permute-start.8 = (bf16[5,5,64,128]{3,2,1,0:T(8,128)(2,1)S(1)}, bf16[5,5,64,128]{3,2,1,0:T(8,128)(2,1)S(1)}, u32[]{:S(2)}, u32[]{:S(2)}) collective-permute-start(bf16[5,5,64,128]{3,2,1,0:T(8,128)(2,1)S(1)} %constant_dynamic-update-slice_fusion.more), channel_id=1, source_target_pairs={{0,1},{1,0},{2,3},{3,2},{4,5},{5,4},{6,7},{7,6},{8,9},{9,8},{10,11... | collective-permute-start | bytes 1228808 | tf_op jit(solution)/shard_map/ppermute | solution.py:335
  39.9 14.3 %collective-permute-start.3 = (bf16[4,4,64,128]{3,2,1,0:T(8,128)(2,1)S(1)}, bf16[4,4,64,128]{3,2,1,0:T(8,128)(2,1)S(1)}, u32[]{:S(2)}, u32[]{:S(2)}) collective-permute-start(bf16[4,4,64,128]{3,2,1,0:T(8,128)(2,1)S(1)} %collective-permute-done.2.far), channel_id=1, source_target_pairs={{0,4},{1,5},{4,8},{5,9},{6,2},{7,3},{8,12},{9,13},{10,6},{11,7},{1... | collective-permute-start | bytes 786440 | tf_op jit(solution)/shard_map/ppermute | solution.py:335
  44.8 9.5 %collective-permute-start.4 = (bf16[4,1,64,128]{3,2,1,0:T(8,128)(2,1)S(1)}, bf16[4,1,64,128]{3,2,1,0:T(8,128)(2,1)S(1)}, u32[]{:S(2)}, u32[]{:S(2)}) collective-permute-start(bf16[4,1,64,128]{3,2,1,0:T(8,128)(2,1)S(1)} %constant_dynamic-slice_fusion), channel_id=1, source_target_pairs={{0,4},{1,5},{2,6},{3,7},{4,8},{5,9},{6,10},{7,11},{8,12},{9,13},{1... | collective-permute-start | bytes 196616 | tf_op jit(solution)/shard_map/ppermute | solution.py:335
  58.8 27.1 %collective-permute-start.9 = (f32[3,6,2,64,128]{4,3,2,1,0:T(8,128)S(1)}, f32[3,6,2,64,128]{4,3,2,1,0:T(8,128)S(1)}, u32[]{:S(2)}, u32[]{:S(2)}) collective-permute-start(f32[3,6,2,64,128]{4,3,2,1,0:T(8,128)S(1)} %get-tuple-element.24), channel_id=1, source_target_pairs={{0,1},{1,0},{2,3},{3,2},{4,5},{5,4},{6,7},{7,6},{8,9},{9,8},{10,11... | collective-permute-start | bytes 3538952 | tf_op jit(solution)/shard_map/ppermute | solution.py:335

commit v7 on v6

--- a/solution.py
+++ b/solution.py
@@ -205,7 +205,7 @@
     copies[1].wait()
 
 
-def own_kernel(plan, stiff, cubic, mine, other, more, more_other,
+def own_kernel(plan, stiff, cubic, mine, other, more, more_other, last,
                keep, give, lap_own, dinv, diag, faces, moments,
                wide, exact, gain, lap, prod, v0, v1, v2):
     blocks, nz = lap.shape[0], lap.shape[-1]
@@ -219,10 +219,7 @@
             place(wide, exact, ref, i, here + 2 * q + i)
             place(wide, exact, rest, i, there + 2 * q + i)
             place(wide, exact, rest, 2 + i, beyond + 2 * q + i)
-
-        @pl.when(q == 0)
-        def _():
-            place(wide, exact, rest, 4, edge)
+    place(wide, exact, last, 0, edge)
 
     material(wide, blocks, stiff, cubic, gain, dinv, diag, faces)
     laps(wide, exact, lap)
@@ -240,7 +237,7 @@
     )
 
 
-def partner_kernel(plan, near, far, along, edge, lap_own, dinv, diag, faces, moments, keep_own, give_own,
+def partner_kernel(plan, near, far, along, lap_own, dinv, diag, faces, moments, keep_own, give_own,
                    keep, give, sums,
                    wide, exact, lap, prod, v0, v1, v2):
     blocks = near.shape[0]
@@ -251,7 +248,7 @@
     for ref, first in zip((near, far, along), spots(high)):
         for k in range(OWN):
             place(wide, exact, ref, k, first + (2 * core + k if k < 2 else 2 * (1 - core) + k - 2))
-    place(wide, exact, edge, 0, 0)
+    place(wide, exact, near, OWN, 0)
     for k in range(3):
         keep[k, pl.ds(0, GROUP)] = keep_own[k]
         give[k, pl.ds(0, GROUP)] = give_own[k]
@@ -360,12 +357,15 @@
     odd = lax.axis_index("space") & 1
     raw_other = send(raw, partner_core)
     far0 = send(raw, lambda m, y, h, c: (m, y, 1 - h, c))
-    four = jnp.concatenate([raw[:per_block], raw_other[:per_block]], 1)
+    chip = jnp.concatenate([raw, raw_other], 1)
+    four = chip[:per_block]
+    last = lax.dynamic_slice_in_dim(chip, 3 - 2 * odd, 1, 1, allow_negative_indices=False)
+    edge = send(last, lambda m, y, h, c: (m, y + 1, h, c))
     far = send(four, lambda m, y, h, c: (m + 1 + c, y, 1 - h, c))
-    near = send(four, lambda m, y, h, c: (m + 1 + c, y, h, c))
-    edge0 = send(raw[:, 1:], lambda m, y, h, c: (m, y + 1, h, 0) if c == 1 else None)
+    five = jnp.concatenate([four, edge[:per_block]], 1)
+    near = send(five, lambda m, y, h, c: (m + 1 + c, y, h, c))
     far0_along = send(far0, along)
-    more = jnp.concatenate([far0, far0_along, edge0], 1)
+    more = jnp.concatenate([far0, far0_along], 1)
     more_other = send(more, partner_core)
 
     field_scratch = [pltpu.VMEM((GROUP, WINDOW) + padded, f32) for _ in range(4)]
@@ -381,7 +381,7 @@
             array(6, WINDOW - 6, *slab),
             array(8, nz),
         ),
-        in_specs=[sm] * 3 + [vm] * 4,
+        in_specs=[sm] * 3 + [vm] * 5,
         out_specs=(vm,) * 7,
         scratch_shapes=[
             pltpu.VMEM((per_block + 1, WINDOW) + padded, f32),
@@ -393,17 +393,15 @@
         compiler_params=pltpu.CompilerParams(vmem_limit_bytes=24 << 20),
         cost_estimate=pl.CostEstimate(flops=20_000_000, bytes_accessed=8 << 20, transcendentals=0),
         name="own",
-    )(plan, stiffness, nonlinear, raw, raw_other, more, more_other)
+    )(plan, stiffness, nonlinear, raw, raw_other, more, more_other, edge)
 
     far_along = send(far, along)
-    last = lax.dynamic_slice_in_dim(near, 3 - 2 * odd, 1, 1, allow_negative_indices=False)
-    edge = send(last, lambda m, y, h, c: (m, y + 1, h, c))
 
     basis = array(3, GROUP + per_block, slabs, *slab)
     keep, give, sums = pl.pallas_call(
         partner_kernel,
         out_shape=(basis, basis, array(n_space, 8, nz)),
-        in_specs=[sm] + [vm] * 11,
+        in_specs=[sm] + [vm] * 10,
         out_specs=(vm,) * 3,
         scratch_shapes=[
             pltpu.VMEM((per_block, WINDOW) + padded, f32),
@@ -414,7 +412,7 @@
         compiler_params=pltpu.CompilerParams(vmem_limit_bytes=24 << 20),
         cost_estimate=pl.CostEstimate(flops=40_000_000, bytes_accessed=16 << 20, transcendentals=0),
         name="partner",
-    )(plan, near, far, far_along, edge, lap_own, dinv, diag, faces, moments, keep_own, give_own)
+    )(plan, near, far, far_along, lap_own, dinv, diag, faces, moments, keep_own, give_own)
 
     got = send(give, partner_core)
     gathered = lax.all_to_all(sums, "space", 0, 0)

time: 87.5 us -> 88 us (level)
  starting transfers between devices: 47.9 us -> 44.5 us
  waiting for transfers between devices: 5.94 us -> 8.98 us
  blocking collectives: 22.1 us -> 23 us
    ppermute x10 -> x9, starting transfers between devices: 47.9 us -> 44.5 us  [send(): return lax.ppermute(x, ('mode', 'space'), pairs)]
    ppermute x10 -> x9, waiting for transfers between devices: 5.94 us -> 8.98 us  [send(): return lax.ppermute(x, ('mode', 'space'), pairs)]
  transfers between devices with their start and end apart: 10 -> 9, of which waited for: 2 -> 2; matrix products, arithmetic and copies ran while one was open for 0% -> 0% of each run, Pallas kernels for 5% -> 5%
where the time goes in v7:
time: 88 us; the launch traced here: 87.7 us
  starting transfers between devices  44.5 us (51%)
  blocking collectives  23 us (26%)
  Pallas kernels  10.8 us (12%)
  waiting for transfers between devices  8.98 us (10%)
    ppermute x9, starting transfers between devices, send(): return lax.ppermute(x, ('mode', 'space'), pairs)  44.5 us
    all_to_all x1, blocking collectives, shards(): gathered = lax.all_to_all(sums, 'space', 0, 0)  23 us
    ppermute x9, waiting for transfers between devices, send(): return lax.ppermute(x, ('mode', 'space'), pairs)  8.98 us
    pallas_call x1, Pallas kernels, shards(): pl.pallas_call(partner_kernel, out_shape=(basis, basis, array(n_space, 8,...  4.55 us
    pallas_call x1, Pallas kernels, shards(): pl.pallas_call(own_kernel, out_shape=(basis, basis, array(per_block, WIND...  4.07 us
  transfers between devices with their start and end apart: 9, of which 2 were waited for; matrix products, arithmetic and copies ran while one was open for 0% of the time, Pallas kernels for 5%

profile of v7, /device:TPU:1, one launch (start us, length us, event | category | flops | bytes accessed | tf_op | source)
XLA Modules:
  0.0 87.7 jit_solution(8350907826069545207)
XLA Ops:
  0.0 1.0 %pack.1.mine = bf16[5,2,64,128]{3,2,1,0:T(8,128)(2,1)S(1)} custom-call(bf16[4,2,64,128]{3,2,1,0:T(8,128)(2,1)} %modes.1, s32[2,64,128]{2,1,0:T(8,128)} %regions.1), custom_call_target="tpu_custom_call" | custom-call | tf_op jit(solution)/shard_map/pack/pallas_call | solution.py:347
  1.0 8.7 %collective-permute-start = (bf16[5,2,64,128]{3,2,1,0:T(8,128)(2,1)S(1)}, bf16[5,2,64,128]{3,2,1,0:T(8,128)(2,1)S(1)}, u32[]{:S(2)}, u32[]{:S(2)}) collective-permute-start(bf16[5,2,64,128]{3,2,1,0:T(8,128)(2,1)S(1)} %pack.1.mine), channel_id=1, source_target_pairs={{0,1},{1,0},{2,3},{3,2},{4,5},{5,4},{6,7},{7,6},{8,9},{9,8},{10,11... | collective-permute-start | bytes 491528 | tf_op jit(solution)/shard_map/ppermute | solution.py:332
  9.7 5.3 %collective-permute-start.5 = (bf16[5,2,64,128]{3,2,1,0:T(8,128)(2,1)S(1)}, bf16[5,2,64,128]{3,2,1,0:T(8,128)(2,1)S(1)}, u32[]{:S(2)}, u32[]{:S(2)}) collective-permute-start(bf16[5,2,64,128]{3,2,1,0:T(8,128)(2,1)S(1)} %pack.1.mine), channel_id=1, source_target_pairs={{0,2},{1,3},{2,0},{3,1},{4,6},{5,7},{6,4},{7,5},{8,10},{9,11},{10,... | collective-permute-start | bytes 491528 | tf_op jit(solution)/shard_map/ppermute | solution.py:332
  15.0 0.0 copy-start
  15.0 0.0 copy-start.1
  15.1 0.0 copy-start.2
  15.1 3.2 %collective-permute-start.1 = (bf16[5,1,64,128]{3,2,1,0:T(8,128)(2,1)S(1)}, bf16[5,1,64,128]{3,2,1,0:T(8,128)(2,1)S(1)}, u32[]{:S(2)}, u32[]{:S(2)}) collective-permute-start(bf16[5,1,64,128]{3,2,1,0:T(8,128)(2,1)S(1)} %fusion.1), channel_id=1, source_target_pairs={{0,4},{1,5},{2,6},{3,7},{4,8},{5,9},{6,10},{7,11},{8,12},{9,13},{1... | collective-permute-start | bytes 245768 | tf_op jit(solution)/shard_map/ppermute | solution.py:332
  18.3 2.9 %collective-permute-done.5 = bf16[5,2,64,128]{3,2,1,0:T(8,128)(2,1)S(1)} collective-permute-done((bf16[5,2,64,128]{3,2,1,0:T(8,128)(2,1)S(1)}, bf16[5,2,64,128]{3,2,1,0:T(8,128)(2,1)S(1)}, u32[]{:S(2)}, u32[]{:S(2)}) %collective-permute-start.5) | collective-permute-done | bytes 163872 | tf_op jit(solution)/shard_map/ppermute | solution.py:332
  21.3 1.5 %collective-permute-start.6 = (bf16[5,2,64,128]{3,2,1,0:T(8,128)(2,1)S(1)}, bf16[5,2,64,128]{3,2,1,0:T(8,128)(2,1)S(1)}, u32[]{:S(2)}, u32[]{:S(2)}) collective-permute-start(bf16[5,2,64,128]{3,2,1,0:T(8,128)(2,1)S(1)} %collective-permute-done.5), channel_id=1, source_target_pairs={{0,4},{1,5},{4,8},{5,9},{6,2},{7,3},{8,12},{9,13},{10,6},{11,7},{1... | collective-permute-start | bytes 491528 | tf_op jit(solution)/shard_map/ppermute | solution.py:332
  22.8 8.5 %collective-permute-start.3 = (bf16[4,4,64,128]{3,2,1,0:T(8,128)(2,1)S(1)}, bf16[4,4,64,128]{3,2,1,0:T(8,128)(2,1)S(1)}, u32[]{:S(2)}, u32[]{:S(2)}) collective-permute-start(bf16[4,4,64,128]{3,2,1,0:T(8,128)(2,1)S(1)} %fusion), channel_id=1, source_target_pairs={{0,34},{1,67},{2,32},{3,65},{4,38},{5,71},{6,36},{7,69},{8,42},{9,... | collective-permute-start | bytes 786440 | tf_op jit(solution)/shard_map/ppermute | solution.py:332
  31.3 0.0 collective-permute-done.1.last
  31.3 0.0 collective-permute-done.6
  31.4 3.0 %collective-permute-start.7 = (bf16[5,4,64,128]{3,2,1,0:T(8,128)(2,1)S(1)}, bf16[5,4,64,128]{3,2,1,0:T(8,128)(2,1)S(1)}, u32[]{:S(2)}, u32[]{:S(2)}) collective-permute-start(bf16[5,4,64,128]{3,2,1,0:T(8,128)(2,1)S(1)} %constant_dynamic-update-slice_fusion.more), channel_id=1, source_target_pairs={{0,1},{1,0},{2,3},{3,2},{4,5},{5,4},{6,7},{7,6},{8,9},{9,8},{10,11... | collective-permute-start | bytes 983048 | tf_op jit(solution)/shard_map/ppermute | solution.py:332
  34.4 2.4 %collective-permute-start.2 = (bf16[4,5,64,128]{3,2,1,0:T(8,128)(2,1)S(1)}, bf16[4,5,64,128]{3,2,1,0:T(8,128)(2,1)S(1)}, u32[]{:S(2)}, u32[]{:S(2)}) collective-permute-start(bf16[4,5,64,128]{3,2,1,0:T(8,128)(2,1)S(1)} %pad_maximum_fusion), channel_id=1, source_target_pairs={{0,32},{1,65},{2,34},{3,67},{4,36},{5,69},{6,38},{7,71},{8,40},{9,... | collective-permute-start | bytes 983048 | tf_op jit(solution)/shard_map/ppermute | solution.py:332
  36.8 6.0 %collective-permute-done.3.far = bf16[4,4,64,128]{3,2,1,0:T(8,128)(2,1)S(1)} collective-permute-done((bf16[4,4,64,128]{3,2,1,0:T(8,128)(2,1)S(1)}, bf16[4,4,64,128]{3,2,1,0:T(8,128)(2,1)S(1)}, u32[]{:S(2)}, u32[]{:S(2)}) %collective-permute-start.3) | collective-permute-done | bytes 262176 | tf_op jit(solution)/shard_map/ppermute | solution.py:332
  42.9 3.3 %collective-permute-start.4 = (bf16[4,4,64,128]{3,2,1,0:T(8,128)(2,1)S(1)}, bf16[4,4,64,128]{3,2,1,0:T(8,128)(2,1)S(1)}, u32[]{:S(2)}, u32[]{:S(2)}) collective-permute-start(bf16[4,4,64,128]{3,2,1,0:T(8,128)(2,1)S(1)} %collective-permute-done.3.far), channel_id=1, source_target_pairs={{0,4},{1,5},{4,8},{5,9},{6,2},{7,3},{8,12},{9,13},{10,6},{11,7},{1... | collective-permute-start | bytes 786440 | tf_op jit(solution)/shard_map/ppermute | solution.py:332
  46.2 0.0 collective-permute-done.7.more_other
  46.2 4.1 %own.1 = (f32[3,2,2,64,128]{4,3,2,1,0:T(8,128)S(1)}, f32[3,2,2,64,128]{4,3,2,1,0:T(8,128)S(1)}, f32[4,11,64,128]{3,2,1,0:T(8,128)S(1)}, f32[9,64,128]{2,1,0:T(8,...) custom-call(s32[4,3]{1,0:T(4,128)S(1)} %copy-done, f32[8]{0:T(128)S(1)} %copy-done.1, ...), custom_call_target="tpu_custom_call" | custom-call | flops 20000000 | bytes 8388608 | tf_op jit(solution)/shard_map/own/pallas_call | solution.py:373
  50.3 0.0 collective-permute-done.2.near
  50.3 0.0 collective-permute-done.4.along
  50.3 4.6 %partner.1 = (f32[3,6,2,64,128]{4,3,2,1,0:T(8,128)S(1)}, f32[3,6,2,64,128]{4,3,2,1,0:T(8,128)S(1)}, f32[32,8,128]{2,1,0:T(8,128)S(1)}) custom-call(s32[4,3]{1,0:T(4,128)S(1)} %copy-done, bf16[4,5,64,128]{3,2,1,0:T(8,128)(2,1)S(1)} %collective-permute-done.2.near, bf16[4,4,64,128]{3,2,1,0:T(8,128)(2,1)S(1)} %collective-permute-done.3.far, ...), custom_call_target="tpu_custom_call" | custom-call | flops 40000000 | bytes 16777216 | tf_op jit(solution)/shard_map/partner/pallas_call | solution.py:401
  54.9 8.6 %collective-permute-start.8 = (f32[3,6,2,64,128]{4,3,2,1,0:T(8,128)S(1)}, f32[3,6,2,64,128]{4,3,2,1,0:T(8,128)S(1)}, u32[]{:S(2)}, u32[]{:S(2)}) collective-permute-start(f32[3,6,2,64,128]{4,3,2,1,0:T(8,128)S(1)} %get-tuple-element.24), channel_id=1, source_target_pairs={{0,1},{1,0},{2,3},{3,2},{4,5},{5,4},{6,7},{7,6},{8,9},{9,8},{10,11... | collective-permute-start | bytes 3538952 | tf_op jit(solution)/shard_map/ppermute | solution.py:332
  63.5 23.0 %all_to_all.5.sums = f32[32,8,128]{2,1,0:T(8,128)S(1)} all-to-all(f32[32,8,128]{2,1,0:T(8,128)S(1)} %get-tuple-element.22), channel_id=1, replica_groups=mesh['mode'=16,'space'=32] {'space'}, dimensions={0} | all-to-all | bytes 262144 | tf_op jit(solution)/shard_map/all_to_all | solution.py:418
  86.5 1.2 %combine.1 = f32[12,2,64,128]{3,2,1,0:T(8,128)} custom-call(f32[32,8,128]{2,1,0:T(8,128)S(1)} %all_to_all.5.sums, f32[3,6,2,64,128]{4,3,2,1,0:T(8,128)S(1)} %get-tuple-element.23.keep, f32[3,6,2,64,128]{4,3,2,1,0:T(8,128)S(1)} %collective-permute-done.8.got), custom_call_target="tpu_custom_call" | custom-call | tf_op jit(solution)/shard_map/combine/pallas_call | solution.py:420
  (11 shorter events, 0.2 us)
Async XLA Ops:
  1.0 14.1 %collective-permute-start = (bf16[5,2,64,128]{3,2,1,0:T(8,128)(2,1)S(1)}, bf16[5,2,64,128]{3,2,1,0:T(8,128)(2,1)S(1)}, u32[]{:S(2)}, u32[]{:S(2)}) collective-permute-start(bf16[5,2,64,128]{3,2,1,0:T(8,128)(2,1)S(1)} %pack.1.mine), channel_id=1, source_target_pairs={{0,1},{1,0},{2,3},{3,2},{4,5},{5,4},{6,7},{7,6},{8,9},{9,8},{10,11... | collective-permute-start | bytes 491528 | tf_op jit(solution)/shard_map/ppermute | solution.py:332
  9.7 11.5 %collective-permute-start.5 = (bf16[5,2,64,128]{3,2,1,0:T(8,128)(2,1)S(1)}, bf16[5,2,64,128]{3,2,1,0:T(8,128)(2,1)S(1)}, u32[]{:S(2)}, u32[]{:S(2)}) collective-permute-start(bf16[5,2,64,128]{3,2,1,0:T(8,128)(2,1)S(1)} %pack.1.mine), channel_id=1, source_target_pairs={{0,2},{1,3},{2,0},{3,1},{4,6},{5,7},{6,4},{7,5},{8,10},{9,11},{10,... | collective-permute-start | bytes 491528 | tf_op jit(solution)/shard_map/ppermute | solution.py:332
  15.0 31.2 %copy-start = (s32[4,3]{1,0:T(4,128)S(1)}, s32[4,3]{1,0:T(4,128)}, u32[]{:S(2)}) copy-start(s32[4,3]{1,0:T(4,128)} %plan.3) | copy-start | bytes 148
  15.0 31.2 %copy-start.1 = (f32[8]{0:T(128)S(1)}, f32[8]{0:T(128)}, u32[]{:S(2)}) copy-start(f32[8]{0:T(128)} %stiff.1) | copy-start | bytes 100
  15.1 31.2 %copy-start.2 = (f32[8]{0:T(128)S(1)}, f32[8]{0:T(128)}, u32[]{:S(2)}) copy-start(f32[8]{0:T(128)} %cubic.1) | copy-start | bytes 100
  15.1 16.2 %collective-permute-start.1 = (bf16[5,1,64,128]{3,2,1,0:T(8,128)(2,1)S(1)}, bf16[5,1,64,128]{3,2,1,0:T(8,128)(2,1)S(1)}, u32[]{:S(2)}, u32[]{:S(2)}) collective-permute-start(bf16[5,1,64,128]{3,2,1,0:T(8,128)(2,1)S(1)} %fusion.1), channel_id=1, source_target_pairs={{0,4},{1,5},{2,6},{3,7},{4,8},{5,9},{6,10},{7,11},{8,12},{9,13},{1... | collective-permute-start | bytes 245768 | tf_op jit(solution)/shard_map/ppermute | solution.py:332
  21.3 10.1 %collective-permute-start.6 = (bf16[5,2,64,128]{3,2,1,0:T(8,128)(2,1)S(1)}, bf16[5,2,64,128]{3,2,1,0:T(8,128)(2,1)S(1)}, u32[]{:S(2)}, u32[]{:S(2)}) collective-permute-start(bf16[5,2,64,128]{3,2,1,0:T(8,128)(2,1)S(1)} %collective-permute-done.5), channel_id=1, source_target_pairs={{0,4},{1,5},{4,8},{5,9},{6,2},{7,3},{8,12},{9,13},{10,6},{11,7},{1... | collective-permute-start | bytes 491528 | tf_op jit(solution)/shard_map/ppermute | solution.py:332
  22.8 20.1 %collective-permute-start.3 = (bf16[4,4,64,128]{3,2,1,0:T(8,128)(2,1)S(1)}, bf16[4,4,64,128]{3,2,1,0:T(8,128)(2,1)S(1)}, u32[]{:S(2)}, u32[]{:S(2)}) collective-permute-start(bf16[4,4,64,128]{3,2,1,0:T(8,128)(2,1)S(1)} %fusion), channel_id=1, source_target_pairs={{0,34},{1,67},{2,32},{3,65},{4,38},{5,71},{6,36},{7,69},{8,42},{9,... | collective-permute-start | bytes 786440 | tf_op jit(solution)/shard_map/ppermute | solution.py:332
  31.4 14.8 %collective-permute-start.7 = (bf16[5,4,64,128]{3,2,1,0:T(8,128)(2,1)S(1)}, bf16[5,4,64,128]{3,2,1,0:T(8,128)(2,1)S(1)}, u32[]{:S(2)}, u32[]{:S(2)}) collective-permute-start(bf16[5,4,64,128]{3,2,1,0:T(8,128)(2,1)S(1)} %constant_dynamic-update-slice_fusion.more), channel_id=1, source_target_pairs={{0,1},{1,0},{2,3},{3,2},{4,5},{5,4},{6,7},{7,6},{8,9},{9,8},{10,11... | collective-permute-start | bytes 983048 | tf_op jit(solution)/shard_map/ppermute | solution.py:332
  34.4 15.9 %collective-permute-start.2 = (bf16[4,5,64,128]{3,2,1,0:T(8,128)(2,1)S(1)}, bf16[4,5,64,128]{3,2,1,0:T(8,128)(2,1)S(1)}, u32[]{:S(2)}, u32[]{:S(2)}) collective-permute-start(bf16[4,5,64,128]{3,2,1,0:T(8,128)(2,1)S(1)} %pad_maximum_fusion), channel_id=1, source_target_pairs={{0,32},{1,65},{2,34},{3,67},{4,36},{5,69},{6,38},{7,71},{8,40},{9,... | collective-permute-start | bytes 983048 | tf_op jit(solution)/shard_map/ppermute | solution.py:332
  42.9 7.4 %collective-permute-start.4 = (bf16[4,4,64,128]{3,2,1,0:T(8,128)(2,1)S(1)}, bf16[4,4,64,128]{3,2,1,0:T(8,128)(2,1)S(1)}, u32[]{:S(2)}, u32[]{:S(2)}) collective-permute-start(bf16[4,4,64,128]{3,2,1,0:T(8,128)(2,1)S(1)} %collective-permute-done.3.far), channel_id=1, source_target_pairs={{0,4},{1,5},{4,8},{5,9},{6,2},{7,3},{8,12},{9,13},{10,6},{11,7},{1... | collective-permute-start | bytes 786440 | tf_op jit(solution)/shard_map/ppermute | solution.py:332
  54.9 31.6 %collective-permute-start.8 = (f32[3,6,2,64,128]{4,3,2,1,0:T(8,128)S(1)}, f32[3,6,2,64,128]{4,3,2,1,0:T(8,128)S(1)}, u32[]{:S(2)}, u32[]{:S(2)}) collective-permute-start(f32[3,6,2,64,128]{4,3,2,1,0:T(8,128)S(1)} %get-tuple-element.24), channel_id=1, source_target_pairs={{0,1},{1,0},{2,3},{3,2},{4,5},{5,4},{6,7},{7,6},{8,9},{9,8},{10,11... | collective-permute-start | bytes 3538952 | tf_op jit(solution)/shard_map/ppermute | solution.py:332
